TPU v7x, 32 devices: a whole 2x2x4 slice. The times are simulated.
32 devices in a mesh: cell: 8 (over y, x, core), view: 4 (over z).
Axes of the slice: x: 2, y: 2, z: 4, core: 2. Of those that a mesh axis runs over, the one named last changes fastest.
Arguments:
- attributes: float32 [14, 65536], P(None, ('cell', 'view'))
- tile_anchor: float32 [2, 1536], P(None, ('cell', 'view')), may hold values from -2 to 4
- target: float32 [1536, 4, 256], P(('cell', 'view'))
- preconditioner: float32 [14, 14, 65536], P(None, None, ('cell', 'view')), as said below
- send_index: int32 [32, 32, 96], P(('cell', 'view')), may hold values from 0 to 2047, as said below
- tile_list: int32 [1536, 64], P(('cell', 'view')), may hold values from 0 to 3071, as said below
- pair_index: int32 [1536], P(('cell', 'view')), may hold values from 0 to 47, as said below
Outputs:
- update: float32 [14, 65536], P(None, ('cell', 'view'))
- step_residual: float32 [14, 65536], P(None, ('cell', 'view'))
Inputs may be any that keep to these rules, and one draw needn't show every extreme that they name: `send_index`: for each pair of devices, the 96 local Gaussian numbers that one sends to the other are distinct. `tile_list`: entries number a device's received rows by source device, then slot (96 a source); on each device the entries of its tiles are a permutation of those row numbers. `pair_index`: on each device, a permutation of its tiles' local numbers. `preconditioner`: each 14 x 14 block is symmetric and diagonally dominant with a positive diagonal.
All inputs are finite; a program needn't handle non-finite values.
Results may differ from a plain program's by a relative error of at most 0.0003.
Values sent between devices are 32-bit elements; how exact they have to be, the bound alone decides.
No kernel may reach another device: no remote copies, remote signals or barrier semaphores. Data moves between devices by JAX's collectives and lax.ppermute only.
A program may use at most 128 MiB of HBM per device.

v0:
```python
import math

import jax
import jax.numpy as jnp
from jax import lax
from jax.sharding import PartitionSpec as P

ITERS = 2


DAMPING = 0.5
PRIOR_WEIGHT = 0.3
DILATION = 0.3


def shifted(value, axis, by):
    devices = lax.axis_size(axis)
    return lax.ppermute(value, axis, [(i, (i + by) % devices) for i in range(devices)])


def camera_axes():
    tilt_cos, tilt_sin = (math.cos(0.3), math.sin(0.3))
    turn_cos, turn_sin = (math.cos(0.2), math.sin(0.2))
    return (
        (turn_cos, turn_sin * tilt_sin, turn_sin * tilt_cos),
        (0.0, tilt_cos, -tilt_sin),
        (-turn_sin, turn_cos * tilt_sin, turn_cos * tilt_cos),
    )


def render(listed, anchor):
    camera = camera_axes()
    factor_rows = (
        (jnp.exp(listed[3]), None, None),
        (listed[4], jnp.exp(listed[5]), None),
        (listed[6], listed[7], jnp.exp(listed[8])),
    )
    screen = []
    for axis_row in range(2):
        place_value = (
            camera[axis_row][0] * listed[0]
            + camera[axis_row][1] * listed[1]
            + camera[axis_row][2] * listed[2]
        )
        screen.append(place_value - anchor[axis_row][:, None])
    depth_values = camera[2][0] * listed[0] + camera[2][1] * listed[1] + camera[2][2] * listed[2]
    projected = []
    for axis_row in range(2):
        row_terms = []
        for column_index in range(3):
            total_term = camera[axis_row][column_index] * factor_rows[column_index][column_index]
            for inner_index in range(column_index + 1, 3):
                total_term = (
                    total_term
                    + camera[axis_row][inner_index] * factor_rows[inner_index][column_index]
                )
            row_terms.append(total_term)
        projected.append(row_terms)
    cov_xx = (
        projected[0][0] * projected[0][0]
        + projected[0][1] * projected[0][1]
        + projected[0][2] * projected[0][2]
        + DILATION
    )
    cov_xy = (
        projected[0][0] * projected[1][0]
        + projected[0][1] * projected[1][1]
        + projected[0][2] * projected[1][2]
    )
    cov_yy = (
        projected[1][0] * projected[1][0]
        + projected[1][1] * projected[1][1]
        + projected[1][2] * projected[1][2]
        + DILATION
    )
    determinant = cov_xx * cov_yy - cov_xy * cov_xy
    conic_xx = (cov_yy / determinant)[..., None]
    conic_xy = (-cov_xy / determinant)[..., None]
    conic_yy = (cov_xx / determinant)[..., None]
    opacity = 0.99 * jax.nn.sigmoid(listed[9])
    pixels = jnp.arange(256)
    pixel_x = (pixels % 16).astype(jnp.float32) + 0.5
    pixel_y = (pixels // 16).astype(jnp.float32) + 0.5
    offset_x = pixel_x - screen[0][:, :, None]
    offset_y = pixel_y - screen[1][:, :, None]
    exponent = -0.5 * (
        conic_xx * offset_x * offset_x
        + 2.0 * conic_xy * offset_x * offset_y
        + conic_yy * offset_y * offset_y
    )
    coverage = opacity[..., None] * jnp.exp(exponent)
    log_keep = jnp.log1p(-coverage)
    earlier = (jnp.arange(64)[None, :] < jnp.arange(64)[:, None]).astype(jnp.float32)
    before = jnp.einsum("jk,bkp->bjp", earlier, log_keep, precision=lax.Precision.HIGHEST)
    weight = jnp.exp(before) * coverage
    colours = jnp.einsum("cbk,bkp->bcp", listed[10:14], weight, precision=lax.Precision.HIGHEST)
    depths = jnp.einsum("bk,bkp->bp", depth_values, weight, precision=lax.Precision.HIGHEST)
    return (colours, depths)


def local(attributes, tile_anchor, target, preconditioner, send_index, tile_list, pair_index):
    cell_count = lax.axis_size("cell")
    view_count = lax.axis_size("view")
    devices = cell_count * view_count
    send_ids = send_index[0]
    slot_count = send_ids.shape[1]
    tiles_here = tile_list.shape[0]
    entries = tile_list.reshape(-1)
    entry_inverse = jnp.argsort(entries)
    pair_inverse = jnp.argsort(pair_index)

    def route(outgoing, forward):
        if forward:
            return lax.all_to_all(
                outgoing, ("cell", "view"), split_axis=1, concat_axis=1, tiled=True
            )
        return lax.all_to_all(outgoing, ("cell", "view"), split_axis=1, concat_axis=1, tiled=True)

    def deliver(values):
        received = route(values[:, send_ids], True)
        return received.reshape(14, -1)[:, entries].reshape(14, tiles_here, 64)

    def collect(cotangent):
        flattened = cotangent.reshape(14, -1)[:, entry_inverse].reshape(14, devices, slot_count)
        returned = route(flattened, False)
        summed = jax.ops.segment_sum(
            returned.reshape(14, -1).T, send_ids.reshape(-1), num_segments=attributes.shape[1]
        )
        return summed.T

    def neighbour(depth_map):
        return shifted(depth_map, "view", -1)[pair_index]

    def depth_cotangent(prior_term):
        arrived = shifted(prior_term[pair_inverse], "view", 1)
        return PRIOR_WEIGHT * prior_term - PRIOR_WEIGHT * arrived

    def apply_scaling(vector):
        return jnp.einsum("ijg,jg->ig", preconditioner, vector, precision=lax.Precision.HIGHEST)

    def global_inner(first, second):
        return lax.psum(jnp.sum(first * second), ("cell", "view"))

    def local_render(values):
        return render(values, tile_anchor)

    listed_now = deliver(attributes)
    (colours, depths), pull_fn = jax.vjp(local_render, listed_now)
    _, tangent_fn = jax.vjp(pull_fn, (jnp.zeros_like(colours), jnp.zeros_like(depths)))
    photometric = colours - target
    prior_term = PRIOR_WEIGHT * (depths - neighbour(depths))
    gradient = collect(pull_fn((photometric, depth_cotangent(prior_term)))[0])
    residual = -gradient
    solution = jnp.zeros_like(attributes)
    scaled = apply_scaling(residual)
    direction = scaled
    scaled_norm = global_inner(residual, scaled)
    for iteration in range(ITERS):
        colour_tangent, depth_tangent = tangent_fn((deliver(direction),))[0]
        prior_tangent = PRIOR_WEIGHT * (depth_tangent - neighbour(depth_tangent))
        normal_image = (
            collect(pull_fn((colour_tangent, depth_cotangent(prior_tangent)))[0])
            + DAMPING * direction
        )
        curvature_sum = lax.psum(jnp.sum(direction * normal_image), ("cell", "view"))
        step_size = scaled_norm / curvature_sum
        solution = solution + step_size * direction
        residual = residual - step_size * normal_image
        if iteration + 1 < ITERS:
            scaled = apply_scaling(residual)
            next_norm = global_inner(residual, scaled)
            direction = scaled + next_norm / scaled_norm * direction
            scaled_norm = next_norm
    return (solution, residual)


def solution(mesh):
    in_specs = (
        P(None, ("cell", "view")),
        P(None, ("cell", "view")),
        P(("cell", "view"), None, None),
        P(None, None, ("cell", "view")),
        P(("cell", "view"), None, None),
        P(("cell", "view"), None),
        P(("cell", "view")),
    )
    out_specs = (P(None, ("cell", "view")), P(None, ("cell", "view")))
    return jax.shard_map(local, mesh=mesh, in_specs=in_specs, out_specs=out_specs, check_vma=False)
```

profile of v0, /device:TPU:0, one launch (start us, length us, event | category | flops | bytes accessed | tf_op | source)
XLA Modules:
  0.0 688.7 jit_solution(14497731297453291714)
XLA Ops:
  2.7 8.1 %gather_fusion = f32[3072,14]{1,0:T(8,128)S(1)} fusion(f32[14,2048]{0,1:T(8,128)S(1)} %copy.404, s32[3072]{0:T(1024)S(1)} %broadcast_clamp_fusion.1), kind=kCustom, calls=%fused_computation | custom fusion | bytes 356352 | tf_op jit(solution)/shard_map/gather | solution.py:120
  12.1 7.3 %all-to-all-start = ((f32[14,32,96]{2,0,1:T(8,128)}), f32[14,32,96]{2,0,1:T(8,128)S(1)}, u32[]{:S(2)}, u32[]{:S(2)}) async-start(f32[14,32,96]{2,0,1:T(8,128)} %bitcast.2), calls=%async_computation | async-start | bytes 524288 | tf_op jit(solution)/shard_map/all_to_all | solution.py:114
  22.9 5.8 sort.35
  30.3 8.1 %gather_fusion.1 = f32[3072,14]{1,0:T(8,128)S(1)} fusion(f32[14,3072]{0,1:T(8,128)S(1)} %bitcast.428, s32[3072]{0:T(1024)S(1)} %broadcast_clamp_fusion), kind=kCustom, calls=%fused_computation.1 | custom fusion | bytes 356352 | tf_op jit(solution)/shard_map/gather | solution.py:121
  45.7 10.2 %bitcast_multiply_fusion.8 = (f32[48,64,256]{2,1,0:T(8,128)S(1)}, f32[48,256,64]{1,2,0:T(8,128)}) fusion(f32[48,64]{1,0:T(8,128)S(1)} %get-tuple-element.224, f32[48,64]{1,0:T(8,128)S(1)} %broadcast_subtract_fusion, f32[256]{0:T(256)S(1)} %copy-done.163, f32[48,64]{1,0:T(8,128)S(1)} %get-tuple-element.223, f32[48,64]{1,0:T(8,128)S(1)} %broadcast_subtract_fusion.1, ...), kind=kOutput, calls=%fused_computation.206 | convolution fusion | flops 624431104 | bytes 6367232 | tf_op jit(solution)/shard_map/jvp(jk,bkp->bjp)/dot_general | solution.py:94
  57.6 3.7 collective-permute-start
  62.9 3.4 fusion.336
  70.2 4.3 fusion.234
  86.9 2.7 fusion.226
  89.8 13.4 %fusion.44 = (f32[48,64]{1,0:T(8,128)S(1)}, f32[48,64]{1,0:T(8,128)S(1)}, f32[48,64]{1,0:T(8,128)S(1)}, f32[48,64]{1,0:T(8,128)S(1)}, f32[48,64]{1,0:T(8,128)S(1)}, /*index=5*/f32[48,64]{1,0:T(8,128)S(1)}) fusion(f32[48,64]{1,0:T(8,128)S(1)} %copy-done.81, f32[48,64]{1,0:T(8,128)S(1)} %copy-done.142, f32[256]{0:T(256)S(1)} %copy-done.164, ...), kind=kOutput, calls=%fused_computation.113 | convolution fusion | flops 651937792 | bytes 6502400 | tf_op jit(solution)/shard_map/transpose(jvp(jk,bkp->bjp))/dot_general | solution.py:94
  104.3 2.7 copy.465
  107.0 13.2 %gather_fusion.4 = f32[3072,14]{1,0:T(8,128)} fusion(f32[14,3072]{0,1:T(8,128)} %bitcast.431, s32[3072]{0:T(1024)} %fusion.294), kind=kCustom, calls=%fused_computation.4 | custom fusion | bytes 356352 | tf_op jit(solution)/shard_map/gather | solution.py:124
  120.3 2.6 copy.413
  122.9 6.2 all-to-all-start.1
  129.8 12.3 %copy.448 = f32[14,14,2048]{0,1,2:T(8,128)} copy(f32[14,14,2048]{2,1,0:T(8,128)} %param.10) | data formatting | bytes 3211264 | tf_op args[3]
  144.0 2.6 copy.415
  146.5 18.4 %scatter_custom_fusion = f32[2048,14]{1,0:T(8,128)} fusion(s32[3072]{0:T(1024)} %reshape.2786, f32[3072,14]{1,0:T(8,128)} %copy.415, f32[]{:T(128)} %constant.25.clone.1), kind=kCustom, calls=%fused_computation.298 | custom fusion | flops 43008 | bytes 115200 | tf_op jit(solution)/shard_map/scatter-add | solution.py:126
  166.2 17.7 %fusion.338 = f32[2048,1,14]{2,1,0:T(1,128)} fusion(f32[14,2048,1]{0,2,1:T(1,128)S(1)} %bitcast.433, f32[14,14,2048]{0,1,2:T(8,128)} %copy.448), kind=kOutput, calls=%fused_computation.628 | convolution fusion | flops 4816896 | bytes 1835008 | tf_op jit(solution)/shard_map/ijg,jg->ig/dot_general | solution.py:139
  183.9 12.0 %gather_fusion.5 = f32[3072,14]{1,0:T(8,128)} fusion(f32[14,2048]{0,1:T(8,128)} %bitcast.419, s32[3072]{0:T(1024)S(1)} %broadcast_clamp_fusion.1), kind=kCustom, calls=%fused_computation.5 | custom fusion | bytes 356352 | tf_op jit(solution)/shard_map/gather | solution.py:120
  196.0 2.6 copy.416
  198.6 16.1 %all_to_all.30 = f32[14,32,96]{2,0,1:T(8,128)} all-to-all(f32[14,32,96]{2,0,1:T(8,128)} %bitcast.447), channel_id=1, replica_groups=mesh['cell'=8,'view'=4] {'cell','view'}, dimensions={1} | all-to-all | bytes 344064 | tf_op jit(solution)/shard_map/all_to_all | solution.py:114
  214.7 2.6 copy.417
  217.3 12.2 %gather_fusion.6 = f32[3072,14]{1,0:T(8,128)} fusion(f32[14,3072]{0,1:T(8,128)} %bitcast.429, s32[3072]{0:T(1024)S(1)} %copy-done.90), kind=kCustom, calls=%fused_computation.6 | custom fusion | bytes 356352 | tf_op jit(solution)/shard_map/gather | solution.py:121
  229.6 2.6 copy.418
  232.2 3.2 add_reduce_fusion.5
  256.2 14.3 %fusion.53 = f32[48,64,256]{2,1,0:T(8,128)S(1)} fusion(f32[48,256,64]{1,2,0:T(8,128)S(1)} %copy-done.174, f32[48,64]{1,0:T(8,128)S(1)} %copy-done.158, f32[48,64]{1,0:T(8,128)S(1)} %get-tuple-element.189, f32[48,64]{1,0:T(8,128)S(1)} %neg.806, f32[48,64]{1,0:T(8,128)S(1)} %copy-done.160, f32[48,64]{1,0:T(8,128)S(1)} %get-tuple-element.188, ...), kind=kOutput, calls=%fused_computation.122 | convolution fusion | flops 663752704 | bytes 6477824 | tf_op jit(solution)/shard_map/transpose(jvp(transpose(jvp(jk,bkp->bjp))))/dot_general | solution.py:94
  270.6 2.4 fusion.341
  280.1 3.3 fusion.339
  287.4 2.7 fusion.231
  290.2 3.0 collective-permute-done.3
  293.3 13.3 %fusion.55 = (f32[48,64]{1,0:T(8,128)S(1)}, f32[48,64]{1,0:T(8,128)S(1)}, f32[48,64]{1,0:T(8,128)S(1)}, f32[48,64]{1,0:T(8,128)S(1)}, f32[48,64]{1,0:T(8,128)S(1)}, /*index=5*/f32[48,64]{1,0:T(8,128)S(1)}) fusion(f32[48,64]{1,0:T(8,128)S(1)} %copy-done.83, f32[48,64]{1,0:T(8,128)S(1)} %copy-done.144, f32[256]{0:T(256)S(1)} %copy-done.166, ...), kind=kOutput, calls=%fused_computation.124 | convolution fusion | flops 651937792 | bytes 6502400 | tf_op jit(solution)/shard_map/transpose(jvp(jk,bkp->bjp))/dot_general | solution.py:94
  306.8 2.7 fusion.224
  310.5 2.7 copy.467
  313.2 13.2 %gather_fusion.9 = f32[3072,14]{1,0:T(8,128)} fusion(f32[14,3072]{0,1:T(8,128)} %bitcast.432, s32[3072]{0:T(1024)} %fusion.294), kind=kCustom, calls=%fused_computation.9 | custom fusion | bytes 356352 | tf_op jit(solution)/shard_map/gather | solution.py:124
  326.4 2.6 copy.425
  329.0 12.8 %all_to_all.31 = f32[14,32,96]{2,0,1:T(8,128)S(1)} all-to-all(f32[14,32,96]{2,0,1:T(8,128)} %copy.425), channel_id=1, replica_groups=mesh['cell'=8,'view'=4] {'cell','view'}, dimensions={1} | all-to-all | bytes 344064 | tf_op jit(solution)/shard_map/all_to_all | solution.py:117
  342.8 2.6 copy.427
  345.3 18.3 %scatter_custom_fusion.1 = f32[2048,14]{1,0:T(8,128)} fusion(s32[3072]{0:T(1024)} %reshape.2786, f32[3072,14]{1,0:T(8,128)} %copy.427, f32[]{:T(128)} %constant.25.clone.1), kind=kCustom, calls=%fused_computation.296 | custom fusion | flops 43008 | bytes 115200 | tf_op jit(solution)/shard_map/scatter-add | solution.py:126
  363.6 2.8 multiply_reduce_fusion.5
  366.4 38.6 %all-reduce.51 = (f32[]{:T(128)}, f32[]{:T(128)}) all-reduce(f32[]{:T(128)} %get-tuple-element.35, f32[]{:T(128)} %get-tuple-element.34), channel_id=1, replica_groups=mesh['cell'=8,'view'=4] {'cell','view'}, use_global_device_ids=true, to_apply=%region_10.11 | all-reduce | flops 2 | bytes 16 | tf_op jit(solution)/shard_map/psum | solution.py:142
  408.3 17.4 %fusion.342 = f32[2048,1,14]{2,1,0:T(1,128)S(1)} fusion(f32[14,2048,1]{0,2,1:T(1,128)S(1)} %bitcast.424, f32[14,14,2048]{0,1,2:T(8,128)} %copy.448), kind=kOutput, calls=%fused_computation.632 | convolution fusion | flops 4816896 | bytes 1835008 | tf_op jit(solution)/shard_map/ijg,jg->ig/dot_general | solution.py:139
  427.7 40.6 %psum.30 = f32[]{:T(128)} all-reduce(f32[]{:T(128)} %multiply_reduce_fusion.4), channel_id=1, replica_groups=mesh['cell'=8,'view'=4] {'cell','view'}, use_global_device_ids=true, to_apply=%region_21.22 | all-reduce | flops 1 | bytes 8 | tf_op jit(solution)/shard_map/psum | solution.py:142
  469.6 2.6 multiply_add_fusion.7
  472.2 12.1 %gather_fusion.10 = f32[3072,14]{1,0:T(8,128)} fusion(f32[14,2048]{0,1:T(8,128)} %multiply_add_fusion.7, s32[3072]{0:T(1024)S(1)} %broadcast_clamp_fusion.1), kind=kCustom, calls=%fused_computation.10 | custom fusion | bytes 356352 | tf_op jit(solution)/shard_map/gather | solution.py:120
  484.2 2.6 copy.428
  486.9 14.7 %all_to_all.32 = f32[14,32,96]{2,0,1:T(8,128)} all-to-all(f32[14,32,96]{2,0,1:T(8,128)} %bitcast.448), channel_id=1, replica_groups=mesh['cell'=8,'view'=4] {'cell','view'}, dimensions={1} | all-to-all | bytes 344064 | tf_op jit(solution)/shard_map/all_to_all | solution.py:114
  501.6 2.6 copy.429
  504.2 12.4 %gather_fusion.11 = f32[3072,14]{1,0:T(8,128)} fusion(f32[14,3072]{0,1:T(8,128)} %bitcast.427, s32[3072]{0:T(1024)S(1)} %copy-done.91), kind=kCustom, calls=%fused_computation.11 | custom fusion | bytes 356352 | tf_op jit(solution)/shard_map/gather | solution.py:121
  516.6 2.6 copy.430
  519.2 3.3 add_reduce_fusion.4
  544.1 13.7 %fusion.64 = f32[48,64,256]{2,1,0:T(8,128)S(1)} fusion(f32[48,256,64]{1,2,0:T(8,128)S(1)} %copy-done.176, f32[48,64]{1,0:T(8,128)S(1)} %copy-done.157, f32[48,64]{1,0:T(8,128)S(1)} %get-tuple-element.185, f32[48,64]{1,0:T(8,128)S(1)} %copy-done.108, f32[48,64]{1,0:T(8,128)S(1)} %get-tuple-element.202, f32[48,64]{1,0:T(8,128)S(1)} %get-tuple-element.184, ...), kind=kOutput, calls=%fused_computation.133 | convolution fusion | flops 663752704 | bytes 6477824 | tf_op jit(solution)/shard_map/transpose(jvp(transpose(jvp(jk,bkp->bjp))))/dot_general | solution.py:94
  557.8 2.4 fusion.345
  562.5 2.3 fusion.344
  566.8 3.3 fusion.343
  574.0 2.7 fusion.228
  576.8 3.0 collective-permute-done.5
  579.9 13.3 %fusion.66 = (f32[48,64]{1,0:T(8,128)S(1)}, f32[48,64]{1,0:T(8,128)S(1)}, f32[48,64]{1,0:T(8,128)S(1)}, f32[48,64]{1,0:T(8,128)S(1)}, f32[48,64]{1,0:T(8,128)S(1)}, /*index=5*/f32[48,64]{1,0:T(8,128)S(1)}) fusion(f32[48,64]{1,0:T(8,128)S(1)} %copy-done.86, f32[48,64]{1,0:T(8,128)S(1)} %copy-done.146, f32[256]{0:T(256)S(1)} %copy-done.168, ...), kind=kOutput, calls=%fused_computation.135 | convolution fusion | flops 651937792 | bytes 6502400 | tf_op jit(solution)/shard_map/transpose(jvp(jk,bkp->bjp))/dot_general | solution.py:94
  593.3 2.7 fusion.222
  596.9 8.1 %gather_fusion.14 = f32[3072,14]{1,0:T(8,128)S(1)} fusion(f32[14,3072]{0,1:T(8,128)S(1)} %bitcast.430, s32[3072]{0:T(1024)S(1)} %copy-done.88), kind=kCustom, calls=%fused_computation.14 | custom fusion | bytes 356352 | tf_op jit(solution)/shard_map/gather | solution.py:124
  605.5 12.1 %all_to_all.33 = f32[14,32,96]{2,0,1:T(8,128)S(1)} all-to-all(f32[14,32,96]{2,0,1:T(8,128)S(1)} %copy.437), channel_id=1, replica_groups=mesh['cell'=8,'view'=4] {'cell','view'}, dimensions={1} | all-to-all | bytes 344064 | tf_op jit(solution)/shard_map/all_to_all | solution.py:117
  618.5 2.6 copy.439
  621.1 18.3 %scatter_custom_fusion.2 = f32[2048,14]{1,0:T(8,128)} fusion(s32[3072]{0:T(1024)} %reshape.2786, f32[3072,14]{1,0:T(8,128)} %copy.439, f32[]{:T(128)} %constant.25.clone.1), kind=kCustom, calls=%fused_computation.294 | custom fusion | flops 43008 | bytes 115200 | tf_op jit(solution)/shard_map/scatter-add | solution.py:126
  641.5 38.5 %psum.31 = f32[]{:T(128)} all-reduce(f32[]{:T(128)} %multiply_reduce_fusion.3), channel_id=1, replica_groups=mesh['cell'=8,'view'=4] {'cell','view'}, use_global_device_ids=true, to_apply=%region_30.31 | all-reduce | flops 1 | bytes 8 | tf_op jit(solution)/shard_map/psum | solution.py:165
  681.3 2.8 multiply_subtract_fusion
  (534 shorter events, 115.2 us)
Async XLA Ops:
  0.6 19.3 %copy-start.104 = (s32[48,64]{1,0:T(8,128)S(1)}, s32[48,64]{1,0:T(8,128)}, u32[]{:S(2)}) copy-start(s32[48,64]{1,0:T(8,128)} %param.12) | copy-start | bytes 36868
  0.6 19.5 %copy-start.161 = (f32[2,48]{1,0:T(2,128)S(1)}, f32[2,48]{1,0:T(2,128)}, u32[]{:S(2)}) copy-start(f32[2,48]{1,0:T(2,128)} %param.8) | copy-start | bytes 1156
  0.7 19.5 %copy-start.162 = (s32[48]{0:T(128)S(1)}, s32[48]{0:T(128)}, u32[]{:S(2)}) copy-start(s32[48]{0:T(128)} %param.13) | copy-start | bytes 580
  12.1 17.7 %all-to-all-start = ((f32[14,32,96]{2,0,1:T(8,128)}), f32[14,32,96]{2,0,1:T(8,128)S(1)}, u32[]{:S(2)}, u32[]{:S(2)}) async-start(f32[14,32,96]{2,0,1:T(8,128)} %bitcast.2), calls=%async_computation | async-start | bytes 524288 | tf_op jit(solution)/shard_map/all_to_all | solution.py:114
  20.1 23.4 %copy-start.89 = (s32[3072]{0:T(1024)}, s32[3072]{0:T(1024)S(1)}, u32[]{:S(2)}) copy-start(s32[3072]{0:T(1024)S(1)} %broadcast_clamp_fusion) | copy-start | bytes 36868
  29.8 15.9 %copy-start.163 = (f32[256]{0:T(256)S(1)}, f32[256]{0:T(256)}, u32[]{:S(2)}) copy-start(f32[256]{0:T(256)} %fusion.299) | copy-start | bytes 3076
  43.8 12.1 %copy-start.135 = (f32[48,64]{1,0:T(8,128)}, f32[48,64]{1,0:T(8,128)S(1)}, u32[]{:S(2)}) copy-start(f32[48,64]{1,0:T(8,128)S(1)} %broadcast_multiply_fusion.3) | copy-start | bytes 36868
  57.6 8.7 %collective-permute-start = (f32[48,256]{1,0:T(8,128)S(1)}, f32[48,256]{1,0:T(8,128)S(1)}, u32[]{:S(2)}, u32[]{:S(2)}) collective-permute-start(f32[48,256]{1,0:T(8,128)S(1)} %bitcast.471), channel_id=1, source_target_pairs={{0,3},{1,0},{2,1},{3,2},{4,7},{5,4},{6,5},{7,6},{8,11},{9,8},{10,9... | collective-permute-start | bytes 147464 | tf_op jit(solution)/shard_map/ppermute | solution.py:18
  69.7 16.3 %collective-permute-start.1 = (f32[48,256]{1,0:T(8,128)}, f32[48,256]{1,0:T(8,128)}, u32[]{:S(2)}, u32[]{:S(2)}) collective-permute-start(f32[48,256]{1,0:T(8,128)} %gather_fusion.3), channel_id=1, source_target_pairs={{0,1},{1,2},{2,3},{3,0},{4,5},{5,6},{6,7},{7,4},{8,9},{9,10},{10,1... | collective-permute-start | bytes 147464 | tf_op jit(solution)/shard_map/ppermute | solution.py:18
  74.5 15.1 %copy-start.69 = (f32[48,64]{1,0:T(8,128)S(1)}, f32[48,64]{1,0:T(8,128)}, u32[]{:S(2)}) copy-start(f32[48,64]{1,0:T(8,128)} %copy-done.68) | copy-start | bytes 36868
  74.5 15.1 %copy-start.75 = (f32[48,64]{1,0:T(8,128)S(1)}, f32[48,64]{1,0:T(8,128)}, u32[]{:S(2)}) copy-start(f32[48,64]{1,0:T(8,128)} %copy-done.74) | copy-start | bytes 36868
  74.5 15.1 %copy-start.81 = (f32[48,64]{1,0:T(8,128)S(1)}, f32[48,64]{1,0:T(8,128)}, u32[]{:S(2)}) copy-start(f32[48,64]{1,0:T(8,128)} %copy-done.80) | copy-start | bytes 36868
  75.9 27.6 %copy-start.56 = (f32[1,48,64]{2,1,0:T(8,128)}, f32[1,48,64]{2,1,0:T(8,128)S(1)}, u32[]{:S(2)}) copy-start(f32[1,48,64]{2,1,0:T(8,128)S(1)} %div.471) | copy-start | bytes 36868
  76.0 27.3 %copy-start.16 = (f32[1,48,64]{2,1,0:T(8,128)}, f32[1,48,64]{2,1,0:T(8,128)S(1)}, u32[]{:S(2)}) copy-start(f32[1,48,64]{2,1,0:T(8,128)S(1)} %exp.339) | copy-start | bytes 36868
  76.8 26.7 %copy-start.19 = (f32[1,48,64]{2,1,0:T(8,128)}, f32[1,48,64]{2,1,0:T(8,128)S(1)}, u32[]{:S(2)}) copy-start(f32[1,48,64]{2,1,0:T(8,128)S(1)} %exp.340) | copy-start | bytes 36868
  77.6 25.8 %copy-start.22 = (f32[1,48,64]{2,1,0:T(8,128)}, f32[1,48,64]{2,1,0:T(8,128)S(1)}, u32[]{:S(2)}) copy-start(f32[1,48,64]{2,1,0:T(8,128)S(1)} %exp.341) | copy-start | bytes 36868
  89.7 13.4 %copy-start.98 = (f32[1,48,64]{2,1,0:T(8,128)S(1)}, f32[1,48,64]{2,1,0:T(8,128)}, u32[]{:S(2)}) copy-start(f32[1,48,64]{2,1,0:T(8,128)} %mul.5873) | copy-start | bytes 36868
  89.7 13.4 %copy-start.99 = (f32[1,48,64]{2,1,0:T(8,128)S(1)}, f32[1,48,64]{2,1,0:T(8,128)}, u32[]{:S(2)}) copy-start(f32[1,48,64]{2,1,0:T(8,128)} %mul.5874) | copy-start | bytes 36868
  89.7 13.4 %copy-start.100 = (f32[1,48,64]{2,1,0:T(8,128)S(1)}, f32[1,48,64]{2,1,0:T(8,128)}, u32[]{:S(2)}) copy-start(f32[1,48,64]{2,1,0:T(8,128)} %mul.5877) | copy-start | bytes 36868
  89.8 13.4 %copy-start.101 = (f32[1,48,64]{2,1,0:T(8,128)S(1)}, f32[1,48,64]{2,1,0:T(8,128)}, u32[]{:S(2)}) copy-start(f32[1,48,64]{2,1,0:T(8,128)} %mul.5882) | copy-start | bytes 36868
  89.8 13.4 %copy-start.102 = (f32[1,48,64]{2,1,0:T(8,128)S(1)}, f32[1,48,64]{2,1,0:T(8,128)}, u32[]{:S(2)}) copy-start(f32[1,48,64]{2,1,0:T(8,128)} %mul.5883) | copy-start | bytes 36868
  89.8 13.4 %copy-start.103 = (f32[1,48,64]{2,1,0:T(8,128)S(1)}, f32[1,48,64]{2,1,0:T(8,128)}, u32[]{:S(2)}) copy-start(f32[1,48,64]{2,1,0:T(8,128)} %mul.5886) | copy-start | bytes 36868
  89.8 13.8 %copy-start.52 = (f32[48,4,64]{2,0,1:T(8,128)S(1)}, f32[48,4,64]{2,0,1:T(8,128)}, u32[]{:S(2)}) copy-start(f32[48,4,64]{2,0,1:T(8,128)} %copy.510) | copy-start | bytes 147460
  103.3 19.6 %copy-start.34 = (f32[1,48,64]{2,1,0:T(8,128)}, f32[1,48,64]{2,1,0:T(8,128)S(1)}, u32[]{:S(2)}) copy-start(f32[1,48,64]{2,1,0:T(8,128)S(1)} %get-tuple-element.129) | copy-start | bytes 36868
  103.3 19.6 %copy-start.37 = (f32[1,48,64]{2,1,0:T(8,128)}, f32[1,48,64]{2,1,0:T(8,128)S(1)}, u32[]{:S(2)}) copy-start(f32[1,48,64]{2,1,0:T(8,128)S(1)} %get-tuple-element.132) | copy-start | bytes 36868
  103.3 19.6 %copy-start.40 = (f32[1,48,64]{2,1,0:T(8,128)}, f32[1,48,64]{2,1,0:T(8,128)S(1)}, u32[]{:S(2)}) copy-start(f32[1,48,64]{2,1,0:T(8,128)S(1)} %get-tuple-element.125) | copy-start | bytes 36868
  103.3 19.6 %copy-start.43 = (f32[1,48,64]{2,1,0:T(8,128)}, f32[1,48,64]{2,1,0:T(8,128)S(1)}, u32[]{:S(2)}) copy-start(f32[1,48,64]{2,1,0:T(8,128)S(1)} %get-tuple-element.126) | copy-start | bytes 36868
  103.3 19.6 %copy-start.46 = (f32[1,48,64]{2,1,0:T(8,128)}, f32[1,48,64]{2,1,0:T(8,128)S(1)}, u32[]{:S(2)}) copy-start(f32[1,48,64]{2,1,0:T(8,128)S(1)} %get-tuple-element.127) | copy-start | bytes 36868
  103.3 19.6 %copy-start.49 = (f32[1,48,64]{2,1,0:T(8,128)}, f32[1,48,64]{2,1,0:T(8,128)S(1)}, u32[]{:S(2)}) copy-start(f32[1,48,64]{2,1,0:T(8,128)S(1)} %get-tuple-element.128) | copy-start | bytes 36868
  104.3 24.8 %copy-start.131 = (s32[1,32,96]{2,1,0:T(8,128)S(1)}, s32[1,32,96]{2,1,0:T(8,128)}, u32[]{:S(2)}) copy-start(s32[1,32,96]{2,1,0:T(8,128)} %param.11) | copy-start | bytes 36868
  122.9 19.2 %all-to-all-start.1 = ((f32[14,32,96]{2,0,1:T(8,128)}), f32[14,32,96]{2,0,1:T(8,128)}, u32[]{:S(2)}, u32[]{:S(2)}) async-start(f32[14,32,96]{2,0,1:T(8,128)} %copy.413), calls=%async_computation.1 | async-start | bytes 524288 | tf_op jit(solution)/shard_map/all_to_all | solution.py:117
  183.9 33.4 %copy-start.90 = (s32[3072]{0:T(1024)S(1)}, s32[3072]{0:T(1024)}, u32[]{:S(2)}) copy-start(s32[3072]{0:T(1024)} %copy-done.89) | copy-start | bytes 36868
  198.6 39.7 %copy-start.54 = (f32[48,64]{1,0:T(8,128)S(1)}, f32[48,64]{1,0:T(8,128)}, u32[]{:S(2)}) copy-start(f32[48,64]{1,0:T(8,128)} %copy-done.53) | copy-start | bytes 36868
  198.6 41.8 %copy-start.70 = (f32[48,64]{1,0:T(8,128)S(1)}, f32[48,64]{1,0:T(8,128)}, u32[]{:S(2)}) copy-start(f32[48,64]{1,0:T(8,128)} %copy-done.68) | copy-start | bytes 36868
  198.6 41.8 %copy-start.76 = (f32[48,64]{1,0:T(8,128)S(1)}, f32[48,64]{1,0:T(8,128)}, u32[]{:S(2)}) copy-start(f32[48,64]{1,0:T(8,128)} %copy-done.74) | copy-start | bytes 36868
  214.7 26.3 %copy-start.95 = (f32[1,3072]{1,0:T(1,128)S(1)}, f32[1,3072]{1,0:T(1,128)}, u32[]{:S(2)}) copy-start(f32[1,3072]{1,0:T(1,128)} %get-tuple-element.154) | copy-start | bytes 36868
  214.7 37.1 %copy-start.82 = (f32[48,64]{1,0:T(8,128)S(1)}, f32[48,64]{1,0:T(8,128)}, u32[]{:S(2)}) copy-start(f32[48,64]{1,0:T(8,128)} %copy-done.80) | copy-start | bytes 36868
  229.5 25.6 %copy-start.8 = (f32[48,64]{1,0:T(8,128)S(1)}, f32[48,64]{1,0:T(8,128)}, u32[]{:S(2)}) copy-start(f32[48,64]{1,0:T(8,128)} %copy-done.7) | copy-start | bytes 36868
  229.5 25.6 %copy-start.11 = (f32[48,64]{1,0:T(8,128)S(1)}, f32[48,64]{1,0:T(8,128)}, u32[]{:S(2)}) copy-start(f32[48,64]{1,0:T(8,128)} %copy-done.10) | copy-start | bytes 36868
  229.5 25.7 %copy-start.14 = (f32[48,64]{1,0:T(8,128)S(1)}, f32[48,64]{1,0:T(8,128)}, u32[]{:S(2)}) copy-start(f32[48,64]{1,0:T(8,128)} %copy-done.13) | copy-start | bytes 36868
  229.5 25.7 %copy-start.60 = (f32[48,64]{1,0:T(8,128)S(1)}, f32[48,64]{1,0:T(8,128)}, u32[]{:S(2)}) copy-start(f32[48,64]{1,0:T(8,128)} %copy-done.59) | copy-start | bytes 36868
  229.5 25.7 %copy-start.63 = (f32[48,64]{1,0:T(8,128)S(1)}, f32[48,64]{1,0:T(8,128)}, u32[]{:S(2)}) copy-start(f32[48,64]{1,0:T(8,128)} %copy-done.62) | copy-start | bytes 36868
  256.2 14.4 %copy-start.32 = (f32[48,64,1]{1,0,2:T(8,128)S(1)}, f32[48,64,1]{1,0,2:T(8,128)}, u32[]{:S(2)}) copy-start(f32[48,64,1]{1,0,2:T(8,128)} %copy-done.31) | copy-start | bytes 36868
  278.4 5.1 collective-permute-start.2
  287.0 6.2 collective-permute-start.3
  293.3 13.4 %copy-start.57 = (f32[1,48,64]{2,1,0:T(8,128)S(1)}, f32[1,48,64]{2,1,0:T(8,128)}, u32[]{:S(2)}) copy-start(f32[1,48,64]{2,1,0:T(8,128)} %copy-done.56) | copy-start | bytes 36868
  408.3 17.4 %copy-start.2 = (f32[14,2048]{0,1:T(8,128)}, f32[14,2048]{0,1:T(8,128)S(1)}, u32[]{:S(2)}) copy-start(f32[14,2048]{0,1:T(8,128)S(1)} %bitcast_subtract_fusion) | copy-start | bytes 344068
  472.2 32.0 %copy-start.91 = (s32[3072]{0:T(1024)S(1)}, s32[3072]{0:T(1024)}, u32[]{:S(2)}) copy-start(s32[3072]{0:T(1024)} %copy-done.89) | copy-start | bytes 36868
  486.9 39.3 %copy-start.96 = (f32[1,3072]{1,0:T(1,128)S(1)}, f32[1,3072]{1,0:T(1,128)}, u32[]{:S(2)}) copy-start(f32[1,3072]{1,0:T(1,128)} %get-tuple-element.154) | copy-start | bytes 36868
  486.9 39.3 %copy-start.97 = (f32[1,3072]{1,0:T(1,128)S(1)}, f32[1,3072]{1,0:T(1,128)}, u32[]{:S(2)}) copy-start(f32[1,3072]{1,0:T(1,128)} %get-tuple-element.156) | copy-start | bytes 36868
  501.6 38.7 %copy-start.84 = (f32[48,64]{1,0:T(8,128)S(1)}, f32[48,64]{1,0:T(8,128)}, u32[]{:S(2)}) copy-start(f32[48,64]{1,0:T(8,128)} %copy-done.80) | copy-start | bytes 36868
  516.6 27.1 %copy-start.55 = (f32[48,64]{1,0:T(8,128)S(1)}, f32[48,64]{1,0:T(8,128)}, u32[]{:S(2)}) copy-start(f32[48,64]{1,0:T(8,128)} %copy-done.53) | copy-start | bytes 36868
  516.6 27.1 %copy-start.9 = (f32[48,64]{1,0:T(8,128)S(1)}, f32[48,64]{1,0:T(8,128)}, u32[]{:S(2)}) copy-start(f32[48,64]{1,0:T(8,128)} %copy-done.7) | copy-start | bytes 36868
  516.6 27.1 %copy-start.12 = (f32[48,64]{1,0:T(8,128)S(1)}, f32[48,64]{1,0:T(8,128)}, u32[]{:S(2)}) copy-start(f32[48,64]{1,0:T(8,128)} %copy-done.10) | copy-start | bytes 36868
  516.6 27.1 %copy-start.15 = (f32[48,64]{1,0:T(8,128)S(1)}, f32[48,64]{1,0:T(8,128)}, u32[]{:S(2)}) copy-start(f32[48,64]{1,0:T(8,128)} %copy-done.13) | copy-start | bytes 36868
  516.6 27.1 %copy-start.61 = (f32[48,64]{1,0:T(8,128)S(1)}, f32[48,64]{1,0:T(8,128)}, u32[]{:S(2)}) copy-start(f32[48,64]{1,0:T(8,128)} %copy-done.59) | copy-start | bytes 36868
  516.6 27.1 %copy-start.64 = (f32[48,64]{1,0:T(8,128)S(1)}, f32[48,64]{1,0:T(8,128)}, u32[]{:S(2)}) copy-start(f32[48,64]{1,0:T(8,128)} %copy-done.62) | copy-start | bytes 36868
  544.1 13.7 %copy-start.33 = (f32[48,64,1]{1,0,2:T(8,128)S(1)}, f32[48,64,1]{1,0,2:T(8,128)}, u32[]{:S(2)}) copy-start(f32[48,64,1]{1,0,2:T(8,128)} %copy-done.31) | copy-start | bytes 36868
  564.8 5.3 collective-permute-start.4
  573.6 6.2 collective-permute-start.5
  579.9 13.4 %copy-start.58 = (f32[1,48,64]{2,1,0:T(8,128)S(1)}, f32[1,48,64]{2,1,0:T(8,128)}, u32[]{:S(2)}) copy-start(f32[1,48,64]{2,1,0:T(8,128)} %copy-done.56) | copy-start | bytes 36868
  605.0 34.3 %copy-start.1 = (f32[14,2048]{0,1:T(8,128)S(1)}, f32[14,2048]{0,1:T(8,128)}, u32[]{:S(2)}) copy-start(f32[14,2048]{0,1:T(8,128)} %multiply_add_fusion.7) | copy-start | bytes 344068
  605.5 75.7 %copy-start = (f32[2048,1,14]{2,1,0:T(1,128)S(1)}, f32[2048,1,14]{2,1,0:T(1,128)}, u32[]{:S(2)}) copy-start(f32[2048,1,14]{2,1,0:T(1,128)} %fusion.338) | copy-start | bytes 344068
  605.5 75.7 %copy-start.3 = (f32[14,2048]{0,1:T(8,128)S(1)}, f32[14,2048]{0,1:T(8,128)}, u32[]{:S(2)}) copy-start(f32[14,2048]{0,1:T(8,128)} %copy-done.2) | copy-start | bytes 344068
  (122 other events, 476.2 us)
where the time goes:
time: 701 us; the launch traced here: 689 us
  local copies, waits for them, and re-layouts  215 us (31%)
  blocking collectives  173 us (25%)
  matrix products  160 us (23%)
  other arithmetic  105 us (15%)
  starting transfers between devices  22.1 us (3%)
  between operations  7.35 us (1%)
    psum x2, blocking collectives, global_inner(): return lax.psum(jnp.sum(first * second), ('cell', 'view'))  79.2 us
    dot_general x6, matrix products, render(): jnp.einsum('jk,bkp->bjp', earlier, log_keep, precision=lax.Precision.HIGH...  78.2 us
    all_to_all x4, blocking collectives, route(): lax.all_to_all(outgoing, ('cell', 'view'), split_axis=1, concat_axis=1, t...  55.7 us
    scatter-add x3, other arithmetic, collect(): jax.ops.segment_sum(returned.reshape(14, -1).T, send_ids.reshape(-1), num...  54.9 us
    gather x6, local copies, waits for them, and re-layouts, deliver(): received = route(values[:, send_ids], True)  38.6 us
    psum x1, blocking collectives, local(): lax.psum(jnp.sum(direction * normal_image), ('cell', 'view'))  38.5 us
    gather x6, local copies, waits for them, and re-layouts, deliver(): return received.reshape(14, -1)[:, entries].reshape(14, tiles_here, 64)  38.4 us
    dot_general x2, matrix products, apply_scaling(): jnp.einsum('ijg,jg->ig', preconditioner, vector, precision=lax.Precision....  35.2 us
  transfers between devices with their start and end apart: 8, of which 2 were waited for; matrix products, arithmetic and copies ran while one was open for 8% of the time, Pallas kernels for 0%

commit v1 on v0

v1 whole, which is shorter than its diff:
```python
import functools
import math

import jax
import jax.numpy as jnp
from jax import lax
from jax.experimental import pallas as pl
from jax.experimental.pallas import tpu as pltpu
from jax.sharding import PartitionSpec as P

ITERS = 2
DAMPING = 0.5
PRIOR_WEIGHT = 0.3
DILATION = 0.3

F32 = jnp.float32
BF16 = jnp.bfloat16
LANES = 128
ROWS = 16
SCALAR = 6
ACTIVE = (0, 1, 2, 3, 4, 5, 6, 8, 9, 10, 11, 12)
KSLOTS = 64
PIXELS = 256
ATTRS = 14


def camera_axes():
    tilt_cos, tilt_sin = (math.cos(0.3), math.sin(0.3))
    turn_cos, turn_sin = (math.cos(0.2), math.sin(0.2))
    return (
        (turn_cos, turn_sin * tilt_sin, turn_sin * tilt_cos),
        (0.0, tilt_cos, -tilt_sin),
        (-turn_sin, turn_cos * tilt_sin, turn_cos * tilt_cos),
    )


CAM = camera_axes()


def payload_rows(slots):
    return -(-len(ACTIVE) * slots // LANES)


def iota(shape, dim):
    return lax.broadcasted_iota(jnp.int32, shape, dim)


def split(value, parts):
    pieces = []
    for _ in range(parts - 1):
        piece = value.astype(BF16)
        pieces.append(piece)
        value = value - piece.astype(F32)
    pieces.append(value.astype(BF16))
    return pieces


def dot(a, b):
    return jnp.dot(a, b, preferred_element_type=F32)


def dot_nt(a, b):
    return lax.dot_general(a, b, (((1,), (1,)), ((), ())), preferred_element_type=F32)


def total(value):
    return jnp.sum(jnp.sum(value, axis=0, keepdims=True), axis=1, keepdims=True)


def pack(feature, out_ref, count, slots):
    depth = payload_rows(slots)
    lane = iota((count, LANES), 1)
    rows = [jnp.zeros((count, LANES), F32) for _ in range(depth)]
    for place, row in enumerate(ACTIVE):
        value = feature(row)
        at, offset = divmod(place * slots, LANES)
        end = offset + slots
        if offset:
            value = pltpu.roll(value, offset, 1)
        rows[at] = jnp.where((lane >= offset) & (lane < end), value, rows[at])
        if end > LANES:
            rows[at + 1] = jnp.where(lane < end - LANES, value, rows[at + 1])
    for at in range(depth):
        out_ref[pl.ds(at, count, stride=depth), :] = rows[at]


def unpack(in_ref, count, slots):
    depth = payload_rows(slots)
    lane = iota((count, LANES), 1)
    rows = [in_ref[pl.ds(at, count, stride=depth), :] for at in range(depth)]
    features = {}
    for place, row in enumerate(ACTIVE):
        at, offset = divmod(place * slots, LANES)
        value = rows[at]
        if offset + slots > LANES:
            value = jnp.where(lane >= offset, value, rows[at + 1])
        if offset:
            value = pltpu.roll(value, LANES - offset, 1)
        features[row] = jnp.where(lane < slots, value, 0.0)
    return features


def put_features(features, ref, count):
    ref[...] = jnp.zeros(ref.shape, F32)
    for row, value in features.items():
        ref[pl.ds(row, count, stride=ROWS), :] = value


def gather(source_ref, chunks, index_a, index_b, blocks, parts, lhs_ref, out_ref):
    for part, piece in enumerate(split(source_ref[...], parts)):
        lhs_ref[:, part * LANES : (part + 1) * LANES] = piece

    def body(step, carry):
        first = 2 * step
        which_a = jnp.concatenate([index_a[pl.ds(first + i, 1), :] for i in range(2)], axis=1)
        which_b = jnp.concatenate([index_b[pl.ds(first + i, 1), :] for i in range(2)], axis=1)
        onehot = jnp.where(iota((LANES, 2 * LANES), 0) == which_b, 1.0, 0.0).astype(BF16)
        product = dot(lhs_ref[...], jnp.concatenate([onehot] * parts, axis=0))
        picked = jnp.zeros((ROWS, 2 * LANES), F32)
        for a in range(chunks):
            picked = jnp.where(which_a == a, product[a * ROWS : (a + 1) * ROWS], picked)
        start = pl.multiple_of(first * ROWS, 2 * ROWS)
        out_ref[pl.ds(start, ROWS), :] = picked[:, :LANES]
        out_ref[pl.ds(start + ROWS, ROWS), :] = picked[:, LANES:]
        return carry

    lax.fori_loop(0, blocks // 2, body, 0)


def scatter(source_ref, chunks, index_a, index_b, blocks, acc_ref):
    acc_ref[...] = jnp.zeros(acc_ref.shape, F32)
    together = 4

    def body(step, carry):
        left, right = [], []
        for i in range(together):
            at = step * together + i
            value = source_ref[pl.ds(pl.multiple_of(at * ROWS, ROWS), ROWS), :]
            pieces = split(value, 2)
            which = jnp.broadcast_to(index_a[pl.ds(at, 1), :], (ROWS, LANES)).astype(F32).astype(BF16)
            onehot = jnp.where(iota((LANES, LANES), 0) == index_b[pl.ds(at, 1), :], 1.0, 0.0).astype(BF16)
            columns = []
            for piece in pieces:
                columns.append(
                    jnp.concatenate(
                        [
                            jnp.where(which == jnp.asarray(a, BF16), piece, jnp.zeros_like(piece))
                            for a in range(chunks)
                        ],
                        axis=0,
                    )
                )
                right.append(onehot)
            left += columns
        acc_ref[...] += dot_nt(jnp.concatenate(left, axis=1), jnp.concatenate(right, axis=1))
        return carry

    lax.fori_loop(0, blocks // together, body, 0)


def geometry(attr):
    e3, e5, e8 = jnp.exp(attr(3)), jnp.exp(attr(5)), jnp.exp(attr(8))
    a4, a6, a7, a9 = attr(4), attr(6), attr(7), attr(9)
    m = [
        (
            CAM[r][0] * e3 + CAM[r][1] * a4 + CAM[r][2] * a6,
            CAM[r][1] * e5 + CAM[r][2] * a7,
            CAM[r][2] * e8,
        )
        for r in range(2)
    ]
    sxx = m[0][0] * m[0][0] + m[0][1] * m[0][1] + m[0][2] * m[0][2] + DILATION
    sxy = m[0][0] * m[1][0] + m[0][1] * m[1][1] + m[0][2] * m[1][2]
    syy = m[1][0] * m[1][0] + m[1][1] * m[1][1] + m[1][2] * m[1][2] + DILATION
    inverse = 1.0 / (sxx * syy - sxy * sxy)
    return {
        "e": (e3, e5, e8),
        "m": m,
        "q": (syy * inverse, -sxy * inverse, sxx * inverse),
        "fade": 1.0 / (1.0 + jnp.exp(a9)),
        "a9": a9,
    }


def place(value):
    return [CAM[r][0] * value(0) + CAM[r][1] * value(1) + CAM[r][2] * value(2) for r in range(3)]


def project(attr, geo):
    x, y, z = place(attr)
    a9 = geo["a9"]
    shade = math.log(0.99) - (jnp.maximum(-a9, 0.0) + jnp.log(1.0 + jnp.exp(-jnp.abs(a9))))
    rows = {0: x, 1: y, 12: z, 2: geo["q"][0], 3: geo["q"][1], 4: geo["q"][2], 5: shade}
    for band in range(4):
        rows[8 + band] = attr(10 + band)
    return rows


def project_tangent(v, geo):
    x, y, z = place(v)
    (e3, e5, e8), m, (qxx, qxy, qyy) = geo["e"], geo["m"], geo["q"]
    v3, v5, v8 = e3 * v(3), e5 * v(5), e8 * v(8)
    d = [
        (
            CAM[r][0] * v3 + CAM[r][1] * v(4) + CAM[r][2] * v(6),
            CAM[r][1] * v5 + CAM[r][2] * v(7),
            CAM[r][2] * v8,
        )
        for r in range(2)
    ]
    sxx = 2.0 * (m[0][0] * d[0][0] + m[0][1] * d[0][1] + m[0][2] * d[0][2])
    syy = 2.0 * (m[1][0] * d[1][0] + m[1][1] * d[1][1] + m[1][2] * d[1][2])
    sxy = sum(m[0][c] * d[1][c] + d[0][c] * m[1][c] for c in range(3))
    rows = {
        0: x,
        1: y,
        12: z,
        2: -(qxx * qxx * sxx + 2.0 * qxx * qxy * sxy + qxy * qxy * syy),
        3: -(qxx * qxy * sxx + (qxx * qyy + qxy * qxy) * sxy + qxy * qyy * syy),
        4: -(qxy * qxy * sxx + 2.0 * qxy * qyy * sxy + qyy * qyy * syy),
        5: geo["fade"] * v(9),
    }
    for band in range(4):
        rows[8 + band] = v(10 + band)
    return rows


def project_cotangent(t, geo):
    (e3, e5, e8), m, (qxx, qxy, qyy) = geo["e"], geo["m"], geo["q"]
    bxx, bxy, byy = t(2), t(3), t(4)
    sxx = -(qxx * qxx * bxx + qxx * qxy * bxy + qxy * qxy * byy)
    sxy = -(2.0 * qxx * qxy * bxx + (qxx * qyy + qxy * qxy) * bxy + 2.0 * qxy * qyy * byy)
    syy = -(qxy * qxy * bxx + qxy * qyy * bxy + qyy * qyy * byy)
    n0 = [2.0 * sxx * m[0][c] + sxy * m[1][c] for c in range(3)]
    n1 = [2.0 * syy * m[1][c] + sxy * m[0][c] for c in range(3)]
    x, y, z = t(0), t(1), t(12)
    out = {j: CAM[0][j] * x + CAM[1][j] * y + CAM[2][j] * z for j in range(3)}
    out[3] = e3 * (CAM[0][0] * n0[0] + CAM[1][0] * n1[0])
    out[4] = CAM[0][1] * n0[0] + CAM[1][1] * n1[0]
    out[5] = e5 * (CAM[0][1] * n0[1] + CAM[1][1] * n1[1])
    out[6] = CAM[0][2] * n0[0] + CAM[1][2] * n1[0]
    out[7] = CAM[0][2] * n0[1] + CAM[1][2] * n1[1]
    out[8] = e8 * (CAM[0][2] * n0[2] + CAM[1][2] * n1[2])
    out[9] = geo["fade"] * t(5)
    for band in range(4):
        out[10 + band] = t(8 + band)
    return out


def to_chunks(ref, chunk_ref, chunks):
    for a in range(chunks):
        chunk_ref[a * ROWS : a * ROWS + ATTRS, :] = ref[:, a * LANES : (a + 1) * LANES]


def reader(ref, count):
    return lambda row: ref[pl.ds(row, count, stride=ROWS), :]


def chunk(ref, a):
    return ref[a * ROWS : a * ROWS + ATTRS, :]


def send_rows(rows, scalar, meta, sa_ref, sb_ref, source_ref, lhs_ref, sent_ref, out_ref, parts):
    chunks, devices, slots = meta
    put_features(rows, source_ref, chunks)
    gather(source_ref, chunks, sa_ref, sb_ref, devices, parts, lhs_ref, sent_ref)

    def feature(row):
        if row == SCALAR:
            return jnp.broadcast_to(scalar, (devices, LANES))
        return sent_ref[pl.ds(row, devices, stride=ROWS), :]

    pack(feature, out_ref, devices, slots)


def first_owner(meta, attr_ref, sa_ref, sb_ref, out_ref, chunk_ref, source_ref, lhs_ref, sent_ref):
    chunks = meta[0]
    to_chunks(attr_ref, chunk_ref, chunks)
    attr = reader(chunk_ref, chunks)
    rows = project(attr, geometry(attr))
    send_rows(rows, jnp.zeros((1, 1), F32), meta, sa_ref, sb_ref, source_ref, lhs_ref, sent_ref, out_ref, 3)


def receive_cotangent(meta, recv_ref, sa_ref, sb_ref, sent_ref, acc_ref, grad_ref, geo):
    chunks, devices, slots = meta
    features = unpack(recv_ref, devices, slots)
    put_features(features, sent_ref, devices)
    scatter(sent_ref, chunks, sa_ref, sb_ref, devices, acc_ref)
    for j, value in project_cotangent(reader(acc_ref, chunks), geo).items():
        grad_ref[pl.ds(j, chunks, stride=ROWS), :] = value
    return features[SCALAR]


def first_lane(value):
    return total(jnp.where(iota(value.shape, 1) == 0, value, 0.0))


def apply_scaling(pre_ref, source_ref, a):
    result = None
    for i in range(ATTRS):
        term = pre_ref[i, :, a * LANES : (a + 1) * LANES] * source_ref[a * ROWS + i : a * ROWS + i + 1, :]
        result = term if result is None else result + term
    return result


def owner_step(
    meta, first, recv_ref, attr_ref, pre_ref, sa_ref, sb_ref, *rest
):
    if first:
        (out_ref, res_out, dir_out, chunk_ref, source_ref, lhs_ref, sent_ref, acc_ref, grad_ref, dir_ref) = rest
    else:
        (
            res_in, dir_in, sc_ref,
            out_ref, res_out, sol_out, dir_out,
            chunk_ref, source_ref, lhs_ref, sent_ref, acc_ref, grad_ref, dir_ref,
        ) = rest
    chunks, devices, slots = meta
    to_chunks(attr_ref, chunk_ref, chunks)
    attr = reader(chunk_ref, chunks)
    geo = geometry(attr)
    scalars = receive_cotangent(meta, recv_ref, sa_ref, sb_ref, sent_ref, acc_ref, grad_ref, geo)
    if not first:
        step = sc_ref[0:1, 0:1] / first_lane(scalars)
    norm = jnp.zeros((ATTRS, LANES), F32)
    for a in range(chunks):
        here = slice(a * LANES, (a + 1) * LANES)
        if first:
            residual = -chunk(grad_ref, a)
        else:
            before = dir_in[:, here]
            image = chunk(grad_ref, a) + DAMPING * before
            residual = res_in[:, here] - step * image
            sol_out[:, here] = step * before
        res_out[:, here] = residual
        grad_ref[a * ROWS : a * ROWS + ATTRS, :] = residual
        scaled = apply_scaling(pre_ref, grad_ref, a)
        dir_out[:, here] = scaled
        dir_ref[a * ROWS : a * ROWS + ATTRS, :] = scaled
        norm = norm + residual * scaled
    rows = project_tangent(reader(dir_ref, chunks), geo)
    send_rows(rows, total(norm), meta, sa_ref, sb_ref, source_ref, lhs_ref, sent_ref, out_ref, 2)


def last_owner(
    meta, recv_ref, attr_ref, sa_ref, sb_ref, res_in, sol_in, dir_in, sc_ref,
    sol_out, res_out, chunk_ref, sent_ref, acc_ref, grad_ref,
):
    chunks, devices, slots = meta
    to_chunks(attr_ref, chunk_ref, chunks)
    geo = geometry(reader(chunk_ref, chunks))
    scalars = receive_cotangent(meta, recv_ref, sa_ref, sb_ref, sent_ref, acc_ref, grad_ref, geo)
    step = sc_ref[0:1, 0:1] / first_lane(scalars)
    for a in range(chunks):
        here = slice(a * LANES, (a + 1) * LANES)
        direction = dir_in[:, here]
        image = chunk(grad_ref, a) + DAMPING * direction
        sol_out[:, here] = sol_in[:, here] + step * direction
        res_out[:, here] = res_in[:, here] - step * image


def pixel_basis(shape, pixel_dim, term_dim):
    pixel, term = iota(shape, pixel_dim), iota(shape, term_dim) & 7
    x = (pixel & 15).astype(F32) - 7.5
    y = (pixel >> 4).astype(F32) - 7.5
    value = jnp.zeros(shape, F32)
    for m, field in enumerate((jnp.ones(shape, F32), x, y, x * x, x * y, y * y)):
        value = jnp.where(term == m, field, value)
    return value


def triangle(rows, later):
    shape = (rows, LANES)
    row, column = iota(shape, 0) & (LANES - 1), iota(shape, 1)
    same = (row >> 6) == (column >> 6)
    order = (row > column) if later else (row < column)
    return jnp.where(same & order, 1.0, 0.0).astype(BF16)


def put_terms(terms, ref, blocks):
    ref[...] = jnp.zeros(ref.shape, F32)
    for m, term in enumerate(terms):
        for part, piece in enumerate(split(term, 3)):
            ref[pl.ds(part * 8 + m, blocks, stride=32), :] = piece.astype(F32)


def forward_basis():
    return jnp.where(iota((PIXELS, 32), 1) < 24, pixel_basis((PIXELS, 32), 0, 1), 0.0).astype(BF16)


def two_tiles(value):
    low = iota((8, LANES), 1) < KSLOTS
    return jnp.concatenate([jnp.where(low, value, 0.0), jnp.where(low, 0.0, value)], axis=0)


def stacked_lhs(value):
    high, low = split(value, 2)
    return jnp.concatenate(
        [jnp.concatenate([high, high], axis=1), jnp.concatenate([low, jnp.zeros_like(low)], axis=1)], axis=0
    )


def fold(value):
    half = value.shape[0] // 2
    return value[:half] + value[half:]


def local_place(theta, ax_ref, ay_ref):
    return theta(0) - ax_ref[...] - 8.0, theta(1) - ay_ref[...] - 8.0


def send_order(pr_ref, depth, ds_ref):
    tiles = depth.shape[0]
    onehot = jnp.where(iota((tiles, tiles), 0) == pr_ref[...], 1.0, 0.0).astype(BF16)
    ds_ref[...] = sum(dot(onehot, piece) for piece in split(depth, 3))


def receive_rows(meta, recv_ref, ta_ref, tb_ref, source_ref, lhs_ref, out_ref, parts):
    blocks, devices, slots = meta
    features = unpack(recv_ref, devices, slots)
    put_features(features, source_ref, devices)
    gather(source_ref, devices, ta_ref, tb_ref, blocks, parts, lhs_ref, out_ref)
    return features[SCALAR]


def tile_forward(
    meta, recv_ref, ta_ref, tb_ref, ax_ref, ay_ref, target_ref, pr_ref,
    theta_ref, w_ref, rho_ref, j_ref, d_ref, ds_ref,
    source_ref, lhs_ref, term_ref,
):
    blocks, devices, slots = meta
    receive_rows(meta, recv_ref, ta_ref, tb_ref, source_ref, lhs_ref, theta_ref, 3)
    theta = reader(theta_ref, blocks)
    dx, dy = local_place(theta, ax_ref, ay_ref)
    qxx, qxy, qyy = theta(2), theta(3), theta(4)
    gx, gy = qxx * dx + qxy * dy, qxy * dx + qyy * dy
    terms = (theta(5) - 0.5 * (dx * gx + dy * gy), gx, gy, -0.5 * qxx, -qxy, -0.5 * qyy)
    put_terms(terms, term_ref, blocks)
    basis = forward_basis()
    earlier = triangle(3 * LANES, False)

    def body(block, carry):
        coefficients = term_ref[pl.ds(pl.multiple_of(block * 32, 32), 32), :].astype(BF16)
        exponent = dot(basis, coefficients)
        coverage = jnp.exp(exponent)
        log_keep = jnp.log(1.0 - coverage)
        before = dot(jnp.concatenate(split(log_keep, 3), axis=1), earlier)
        weight = jnp.exp(before) * coverage
        w_ref[block] = weight
        rho_ref[block] = jnp.exp(exponent - log_keep)
        start = pl.multiple_of(block * ROWS, ROWS)
        left = stacked_lhs(two_tiles(theta_ref[pl.ds(start + 8, 8), :]))
        image = fold(dot_nt(left, jnp.concatenate(split(weight, 2), axis=1)))
        j_ref[pl.ds(start, ROWS), :] = image
        j_ref[pl.ds(start, 4), :] = image[0:4] - target_ref[2 * block]
        j_ref[pl.ds(start + 8, 4), :] = image[8:12] - target_ref[2 * block + 1]
        d_ref[pl.ds(2 * block, 1), :] = image[4:5]
        d_ref[pl.ds(2 * block + 1, 1), :] = image[12:13]
        return carry

    lax.fori_loop(0, blocks, body, 0)
    send_order(pr_ref, d_ref[...], ds_ref)


def tile_tangent(meta, first, recv_ref, ta_ref, tb_ref, ax_ref, ay_ref, pr_ref, theta_ref, w_ref, rho_ref, *rest):
    if first:
        j_ref, d_ref, ds_ref, sc_ref, source_ref, lhs_ref, term_ref, dot_ref = rest
    else:
        j_in, d_in, sc_in, j_ref, d_ref, ds_ref, sc_ref, source_ref, lhs_ref, term_ref, dot_ref = rest
    blocks, devices, slots = meta
    norm = first_lane(receive_rows(meta, recv_ref, ta_ref, tb_ref, source_ref, lhs_ref, dot_ref, 2))
    if not first:
        ratio = norm / sc_in[0:1, 0:1]
        sc_ref[8:16, :] = jnp.broadcast_to(ratio, (8, LANES))
    else:
        sc_ref[8:16, :] = jnp.zeros((8, LANES), F32)
    sc_ref[0:8, :] = jnp.broadcast_to(norm, (8, LANES))
    theta, tangent = reader(theta_ref, blocks), reader(dot_ref, blocks)
    dx, dy = local_place(theta, ax_ref, ay_ref)
    qxx, qxy, qyy = theta(2), theta(3), theta(4)
    gx, gy = qxx * dx + qxy * dy, qxy * dx + qyy * dy
    tx, ty, txx, txy, tyy = (tangent(row) for row in range(5))
    hx = txx * dx + txy * dy + qxx * tx + qxy * ty
    hy = txy * dx + tyy * dy + qxy * tx + qyy * ty
    constant = tangent(5) - 0.5 * (tx * gx + dx * hx + ty * gy + dy * hy)
    put_terms((constant, hx, hy, -0.5 * txx, -txy, -0.5 * tyy), term_ref, blocks)
    basis = forward_basis()
    earlier = triangle(2 * LANES, False)

    def body(block, carry):
        coefficients = term_ref[pl.ds(pl.multiple_of(block * 32, 32), 32), :].astype(BF16)
        change = dot(basis, coefficients)
        weight = w_ref[block]
        before = dot(jnp.concatenate(split(rho_ref[block] * change, 2), axis=1), earlier)
        weight_change = weight * (change - before)
        start = pl.multiple_of(block * ROWS, ROWS)
        left = stacked_lhs(two_tiles(theta_ref[pl.ds(start + 8, 8), :]))
        left_change = stacked_lhs(two_tiles(dot_ref[pl.ds(start + 8, 8), :]))
        image = fold(
            dot_nt(left, jnp.concatenate(split(weight_change, 2), axis=1))
            + dot_nt(left_change, jnp.concatenate(split(weight, 2), axis=1))
        )
        if not first:
            image = image + ratio * j_in[pl.ds(start, ROWS), :]
        j_ref[pl.ds(start, ROWS), :] = image
        d_ref[pl.ds(2 * block, 1), :] = image[4:5]
        d_ref[pl.ds(2 * block + 1, 1), :] = image[12:13]
        return carry

    lax.fori_loop(0, blocks, body, 0)
    send_order(pr_ref, d_ref[...], ds_ref)


def tile_pull(
    meta, mode, j_ref, d_ref, next_ref, past_ref, pc_ref, ta_ref, tb_ref, ax_ref, ay_ref, theta_ref, w_ref, rho_ref, *rest
):
    if mode == 0:
        out_ref, depth_ref, term_ref, bar_ref, acc_ref = rest
    elif mode == 1:
        dir_in, out_ref, depth_ref, term_ref, bar_ref, acc_ref = rest
    else:
        scaled_in, dir_in, sc_ref, out_ref, dir_out, depth_ref, term_ref, bar_ref, acc_ref = rest
    blocks, devices, slots = meta
    tiles = 2 * blocks
    depth = d_ref[...]
    onehot = jnp.where(iota((tiles, tiles), 1) == pc_ref[...], 1.0, 0.0).astype(BF16)
    partner = sum(dot(onehot, piece) for piece in split(next_ref[...], 3))
    prior = PRIOR_WEIGHT * (depth - partner)
    prior_past = PRIOR_WEIGHT * (past_ref[...] - depth)
    depth_ref[...] = PRIOR_WEIGHT * prior - PRIOR_WEIGHT * prior_past
    later = triangle(2 * LANES, True)
    moments = pixel_basis((ROWS, PIXELS), 1, 0)
    moments = jnp.where(iota((ROWS, PIXELS), 0) < 8, moments, 0.0).astype(BF16)
    moments = jnp.concatenate([moments, moments], axis=1)
    row = iota((ROWS, PIXELS), 0)
    low = iota((8, LANES), 1) < KSLOTS

    def body(block, energy):
        start = pl.multiple_of(block * ROWS, ROWS)
        image = j_ref[pl.ds(start, ROWS), :]
        energy = energy + jnp.where((row & 7) < 4, image * image, 0.0)
        cotangent = jnp.where(row == 4, depth_ref[pl.ds(2 * block, 1), :], image)
        cotangent = jnp.where(row == 12, depth_ref[pl.ds(2 * block + 1, 1), :], cotangent)
        weight = w_ref[block]
        colours = two_tiles(theta_ref[pl.ds(start + 8, 8), :])
        cot_high, cot_low = split(cotangent, 2)
        col_high, col_low = split(colours, 2)
        across = jnp.concatenate([cot_high.astype(F32), cot_low.astype(F32), cot_high.astype(F32)], axis=0).T
        pulled = dot(across.astype(BF16), jnp.concatenate([col_high, col_high, col_low], axis=0))
        share = weight * pulled
        after = dot(jnp.concatenate(split(share, 2), axis=1), later)
        bar = share - rho_ref[block] * after
        bar_moments = dot(moments, jnp.concatenate(split(bar, 2), axis=0))
        left = jnp.concatenate(
            [
                jnp.concatenate([cot_high, cot_high], axis=1),
                jnp.concatenate([cot_low, jnp.zeros_like(cot_low)], axis=1),
            ],
            axis=0,
        )
        colour_bar = fold(dot(left, jnp.concatenate(split(weight, 2), axis=0)))
        term_ref[pl.ds(start, 8), :] = bar_moments[0:8]
        bar_ref[pl.ds(start + 8, 8), :] = jnp.where(low, colour_bar[0:8], colour_bar[8:16])
        return energy

    energy = lax.fori_loop(0, blocks, body, jnp.zeros((ROWS, PIXELS), F32))
    scalar = jnp.zeros((1, 1), F32)
    if mode:
        if mode == 1:
            direction = dir_in[...]
        else:
            direction = scaled_in[...] + sc_ref[8:9, 0:1] * dir_in[...]
            dir_out[...] = direction
        scalar = total(energy) + total(prior * prior) + DAMPING * total(direction * direction)
    theta, bars = reader(theta_ref, blocks), reader(term_ref, blocks)
    dx, dy = local_place(theta, ax_ref, ay_ref)
    qxx, qxy, qyy = theta(2), theta(3), theta(4)
    gx, gy = qxx * dx + qxy * dy, qxy * dx + qyy * dy
    b0 = bars(0)
    hx, hy = bars(1) - 0.5 * dx * b0, bars(2) - 0.5 * dy * b0
    values = (
        -0.5 * gx * b0 + qxx * hx + qxy * hy,
        -0.5 * gy * b0 + qxy * hx + qyy * hy,
        dx * hx - 0.5 * bars(3),
        dy * hx + dx * hy - bars(4),
        dy * hy - 0.5 * bars(5),
        b0,
        jnp.zeros_like(b0),
        jnp.zeros_like(b0),
    )
    for line, value in enumerate(values):
        bar_ref[pl.ds(line, blocks, stride=ROWS), :] = value
    scatter(bar_ref, devices, ta_ref, tb_ref, blocks, acc_ref)

    def feature(line):
        if line == SCALAR:
            return jnp.broadcast_to(scalar, (devices, LANES))
        return acc_ref[pl.ds(line, devices, stride=ROWS), :]

    pack(feature, out_ref, devices, slots)


def call(body, outs, scratch, name, *args):
    return pl.pallas_call(
        body,
        out_shape=[jax.ShapeDtypeStruct(shape, F32) for shape in outs],
        scratch_shapes=[pltpu.VMEM(shape, dtype) for shape, dtype in scratch],
        compiler_params=pltpu.CompilerParams(vmem_limit_bytes=VMEM_LIMIT),
        name=name,
    )(*args)


VMEM_LIMIT = 40 * 1024 * 1024


def local(attributes, tile_anchor, target, preconditioner, send_index, tile_list, pair_index):
    view_count = lax.axis_size("view")
    devices = lax.axis_size("cell") * view_count
    slots = send_index.shape[2]
    gaussians = attributes.shape[1]
    tiles = tile_list.shape[0]
    chunks, blocks = gaussians // LANES, tiles * KSLOTS // LANES
    depth = payload_rows(slots)

    ids = jnp.pad(send_index[0], ((0, 0), (0, LANES - slots)), constant_values=-1)
    sa, sb = ids >> 7, jnp.where(ids < 0, -1, ids & (LANES - 1))
    entries = tile_list.reshape(blocks, LANES)
    ta, tb = entries // slots, entries % slots
    anchors = jnp.broadcast_to(tile_anchor[:, :, None], (2, tiles, KSLOTS)).reshape(2, blocks, LANES)
    ax, ay = anchors[0], anchors[1]
    pair_row, pair_column = pair_index.reshape(1, tiles), pair_index.reshape(tiles, 1)

    owner_meta = (chunks, devices, slots)
    tile_meta = (blocks, devices, slots)
    payload = (devices * depth, LANES)
    field = (blocks, PIXELS, LANES)
    owned = (ATTRS, gaussians)
    images, maps, scalars = (blocks * ROWS, PIXELS), (tiles, PIXELS), (16, LANES)
    chunked = ((chunks * ROWS, LANES), F32)
    arrived = ((devices * ROWS, LANES), F32)
    listed = ((blocks * ROWS, LANES), F32)
    terms = ((blocks * 32, LANES), F32)

    def exchange(value):
        value = value.reshape(devices, 1, depth * LANES)
        value = lax.all_to_all(value, ("cell", "view"), split_axis=0, concat_axis=0, tiled=True)
        return value.reshape(payload)

    def shifted(value, by):
        return lax.ppermute(value, "view", [(i, (i + by) % view_count) for i in range(view_count)])

    def owner_scratch(parts):
        return [chunked, chunked, ((chunks * ROWS, parts * LANES), BF16), arrived]

    def tile_scratch(parts):
        return [arrived, ((devices * ROWS, parts * LANES), BF16), terms]

    def pull(mode, image, maps_here, extra, outs):
        here, ordered = maps_here
        return call(
            functools.partial(tile_pull, tile_meta, mode),
            [payload] + outs,
            [(maps, F32), listed, listed, arrived],
            "pull",
            image, here, shifted(here, -1), shifted(ordered, 1), pair_column, ta, tb, ax, ay, theta, weight, rho, *extra,
        )

    (sent,) = call(functools.partial(first_owner, owner_meta), [payload], owner_scratch(3), "project", attributes, sa, sb)
    theta, weight, rho, image, here, ordered = call(
        functools.partial(tile_forward, tile_meta),
        [listed[0], field, field, images, maps, maps],
        tile_scratch(3),
        "forward",
        exchange(sent), ta, tb, ax, ay, target, pair_row,
    )
    (sent,) = pull(0, image, (here, ordered), (), [])
    sent, residual, direction = call(
        functools.partial(owner_step, owner_meta, True),
        [payload, owned, owned],
        owner_scratch(2) + [chunked, chunked, chunked],
        "gradient",
        exchange(sent), attributes, preconditioner, sa, sb,
    )
    image, here, ordered, first_sums = call(
        functools.partial(tile_tangent, tile_meta, True),
        [images, maps, maps, scalars],
        tile_scratch(2) + [listed],
        "tangent",
        exchange(sent), ta, tb, ax, ay, pair_row, theta, weight, rho,
    )
    (sent,) = pull(1, image, (here, ordered), (direction,), [])
    sent, residual, update, scaled = call(
        functools.partial(owner_step, owner_meta, False),
        [payload, owned, owned, owned],
        owner_scratch(2) + [chunked, chunked, chunked],
        "step",
        exchange(sent), attributes, preconditioner, sa, sb, residual, direction, first_sums,
    )
    image, here, ordered, sums = call(
        functools.partial(tile_tangent, tile_meta, False),
        [images, maps, maps, scalars],
        tile_scratch(2) + [listed],
        "tangent_next",
        exchange(sent), ta, tb, ax, ay, pair_row, theta, weight, rho, image, here, first_sums,
    )
    sent, direction = pull(2, image, (here, ordered), (scaled, direction, sums), [owned])
    update, residual = call(
        functools.partial(last_owner, owner_meta),
        [owned, owned],
        [chunked, arrived, chunked, chunked],
        "finish",
        exchange(sent), attributes, sa, sb, residual, update, direction, sums,
    )
    return (update, residual)


def solution(mesh):
    in_specs = (
        P(None, ("cell", "view")),
        P(None, ("cell", "view")),
        P(("cell", "view"), None, None),
        P(None, None, ("cell", "view")),
        P(("cell", "view"), None, None),
        P(("cell", "view"), None),
        P(("cell", "view")),
    )
    out_specs = (P(None, ("cell", "view")), P(None, ("cell", "view")))
    return jax.shard_map(local, mesh=mesh, in_specs=in_specs, out_specs=out_specs, check_vma=False)
```

time: 701 us -> 219 us (0.31); the launches traced: 689 us -> 218 us
  local copies, waits for them, and re-layouts: 215 us -> 10 us
  matrix products: 160 us -> 0 us
  Pallas kernels: 0 us -> 116 us
  blocking collectives: 173 us -> 59.2 us
  other arithmetic: 105 us -> 2.24 us
    dot_general x27 -> x0, matrix products: 160 us -> none  [the longest x6 78.2 us: render(): jnp.einsum('jk,bkp->bjp', earlier, log_keep, precision=lax.Precision.HIGH...]
    gather x21 -> x0, local copies, waits for them, and re-layouts: 119 us -> none  [the longest x6 38.6 us: deliver(): received = route(values[:, send_ids], True)]
    psum x3 -> x0, blocking collectives: 118 us -> none  [the longest x2 79.2 us: global_inner(): return lax.psum(jnp.sum(first * second), ('cell', 'view'))]
    pallas_call x0 -> x10, Pallas kernels: none -> 116 us  [call(): pl.pallas_call(body, out_shape=[jax.ShapeDtypeStruct(shape, F32) for shap...]
    scatter-add x3 -> x0, other arithmetic: 54.9 us -> none  [collect(): jax.ops.segment_sum(returned.reshape(14, -1).T, send_ids.reshape(-1), num...]
    mul x28 -> x0, local copies, waits for them, and re-layouts: 24.3 us -> none  [the longest x6 8.26 us: render(): camera[axis_row][inner_index] * factor_rows[inner_index][column_index]]
    reshape x11 -> x1, local copies, waits for them, and re-layouts: 14.3 us -> 0.74 us  [local(): pair_index.reshape(tiles, 1)]
    unnamed x360 -> x26, local copies, waits for them, and re-layouts: 21.2 us -> 7.76 us
  transfers between devices with their start and end apart: 8 -> 7, of which waited for: 2 -> 4; matrix products, arithmetic and copies ran while one was open for 8% -> 2% of each run, Pallas kernels for 0% -> 0%
where the time goes in v1:
time: 219 us; the launch traced here: 218 us
  Pallas kernels  116 us (53%)
  blocking collectives  59.2 us (27%)
  starting transfers between devices  18.9 us (9%)
  waiting for transfers between devices  11.2 us (5%)
  local copies, waits for them, and re-layouts  10 us (5%)
  other arithmetic  2.24 us (1%)
    pallas_call x10, Pallas kernels, call(): pl.pallas_call(body, out_shape=[jax.ShapeDtypeStruct(shape, F32) for shap...  116 us
    all_to_all x5, blocking collectives, exchange(): lax.all_to_all(value, ('cell', 'view'), split_axis=0, concat_axis=0, tile...  59.2 us
    ppermute x6, starting transfers between devices, shifted(): lax.ppermute(value, 'view', [(i, (i + by) % view_count) for i in range(vi...  11.6 us
    unnamed x26, local copies, waits for them, and re-layouts  7.76 us
    all_to_all x1, starting transfers between devices, exchange(): lax.all_to_all(value, ('cell', 'view'), split_axis=0, concat_axis=0, tile...  7.32 us
    ppermute x6, waiting for transfers between devices, shifted(): lax.ppermute(value, 'view', [(i, (i + by) % view_count) for i in range(vi...  5.67 us
    all_to_all x1, waiting for transfers between devices, exchange(): lax.all_to_all(value, ('cell', 'view'), split_axis=0, concat_axis=0, tile...  5.53 us
  transfers between devices with their start and end apart: 7, of which 4 were waited for; matrix products, arithmetic and copies ran while one was open for 2% of the time, Pallas kernels for 0%

profile of v1, /device:TPU:0, one launch (start us, length us, event | category | flops | bytes accessed | tf_op | source)
XLA Modules:
  0.0 218.3 jit_solution(17544879524265945384)
XLA Ops:
  0.6 0.7 and_select_fusion
  1.4 0.0 copy-start.6
  1.4 0.0 copy-start.4
  1.4 0.9 copy-done.4
  2.3 4.5 %project.1 = f32[288,128]{1,0:T(8,128)} custom-call(f32[14,2048]{1,0:T(8,128)S(1)} %copy-done.4, s32[32,128]{1,0:T(8,128)S(1)} %get-tuple-element.53.sa_ref, s32[32,128]{1,0:T(8,128)S(1)} %get-tuple-element.52.sb_ref), custom_call_target="tpu_custom_call" | custom-call | tf_op jit(solution)/shard_map/project/pallas_call | solution.py:603
  6.8 0.0 copy-done.6
  6.8 7.3 %all-to-all-start = ((f32[32,1,1152]{2,1,0:T(1,128)}), f32[32,1,1152]{2,1,0:T(1,128)S(1)}, u32[]{:S(2)}, u32[]{:S(2)}) async-start(f32[32,1,1152]{2,1,0:T(1,128)} %bitcast.1), calls=%async_computation | async-start | bytes 294912 | tf_op jit(solution)/shard_map/all_to_all | solution.py:645
  14.1 0.8 sign_compare_fusion
  14.9 0.8 broadcast_remainder_fusion
  15.7 0.1 ne.27
  15.7 0.8 slice_reduce_fusion
  16.5 0.1 broadcast_in_dim.24
  16.6 0.1 broadcast_in_dim.25
  16.7 0.1 broadcast_in_dim.26.ay_ref
  16.8 0.1 broadcast_in_dim.21
  16.9 0.1 broadcast_in_dim.22
  17.0 0.1 broadcast_in_dim.23.ax_ref
  17.1 0.1 rem.19
  17.1 0.1 div.10
  17.2 5.5 %all-to-all-done = f32[32,1,1152]{2,1,0:T(1,128)S(1)} async-done(((f32[32,1,1152]{2,1,0:T(1,128)}), f32[32,1,1152]{2,1,0:T(1,128)S(1)}, u32[]{:S(2)}, u32[]{:S(2)}) %all-to-all-start) | async-done | bytes 147488 | tf_op jit(solution)/shard_map/all_to_all | solution.py:645
  22.8 0.0 copy-start.10
  22.8 0.9 copy-done.10
  23.7 0.0 copy-start.11
  23.7 0.7 copy-done.11
  24.3 16.6 %forward.1 = (f32[384,128]{1,0:T(8,128)S(1)}, f32[24,256,128]{2,1,0:T(8,128)S(1)}, f32[24,256,128]{2,1,0:T(8,128)S(1)}, f32[384,256]{1,0:T(8,128)S(1)}, f32[48,256]{1,0:T(8,128)}, /*index=5*/f32[48,256]{1,0:T(8,128)}) custom-call(f32[288,128]{1,0:T(8,128)S(1)} %bitcast.18, s32[24,128]{1,0:T(8,128)S(1)} %get-tuple-element.55.ta_ref, ...), custom_call_target="tpu_custom_call" | custom-call | tf_op jit(solution)/shard_map/forward/pallas_call | solution.py:603
  41.0 0.0 copy-start
  41.0 1.6 copy-done
  42.6 0.0 copy-start.8
  42.6 0.7 copy-done.8
  43.3 0.0 collective-permute-start.1
  43.3 3.8 %collective-permute-start = (f32[48,256]{1,0:T(8,128)}, f32[48,256]{1,0:T(8,128)S(1)}, u32[]{:S(2)}, u32[]{:S(2)}) collective-permute-start(f32[48,256]{1,0:T(8,128)} %get-tuple-element.26.d_ref), channel_id=1, source_target_pairs={{0,3},{1,0},{2,1},{3,2},{4,7},{5,4},{6,5},{7,6},{8,11},{9,8},{10,9... | collective-permute-start | bytes 147464 | tf_op jit(solution)/shard_map/ppermute | solution.py:649
  47.1 0.7 copy.16.pc_ref
  47.9 1.5 collective-permute-done.1.past_ref
  49.4 0.0 collective-permute-done.next_ref
  49.4 0.0 copy-start.1
  49.4 1.9 copy-done.1
  51.3 1.0 copy-done.9
  52.3 0.0 copy-start.12
  52.3 17.1 %pull.3 = f32[288,128]{1,0:T(8,128)S(1)} custom-call(f32[384,256]{1,0:T(8,128)S(1)} %copy-done.9, f32[48,256]{1,0:T(8,128)} %get-tuple-element.26.d_ref, f32[48,256]{1,0:T(8,128)S(1)} %collective-permute-done.next_ref, f32[48,256]{1,0:T(8,128)S(1)} %collective-permute-done.1.past_ref, s32[48,1]{1,0:T(8,128)S(1)} %copy.16.pc_ref, ...), custom_call_target="tpu_custom_call" | custom-call | tf_op jit(solution)/shard_map/pull/pallas_call | solution.py:603
  69.5 12.8 %all_to_all.30 = f32[32,1,1152]{2,1,0:T(1,128)S(1)} all-to-all(f32[32,1,1152]{2,1,0:T(1,128)S(1)} %bitcast.21), channel_id=1, replica_groups=mesh['cell'=8,'view'=4] {'cell','view'}, dimensions={0} | all-to-all | bytes 294912 | tf_op jit(solution)/shard_map/all_to_all | solution.py:645
  82.3 0.0 copy-done.3
  82.3 0.0 copy-done.5
  82.3 0.0 copy-done.7
  82.3 6.3 %gradient.1 = (f32[288,128]{1,0:T(8,128)S(1)}, f32[14,2048]{1,0:T(8,128)S(1)}, f32[14,2048]{1,0:T(8,128)S(1)}) custom-call(f32[288,128]{1,0:T(8,128)S(1)} %bitcast.17, f32[14,2048]{1,0:T(8,128)S(1)} %copy-done.5, f32[14,14,2048]{2,1,0:T(8,128)S(1)} %copy-done.3, s32[32,128]{1,0:T(8,128)S(1)} %copy-done.7, s32[32,128]{1,0:T(8,128)S(1)} %get-tuple-element.52.sb_ref), custom_call_target="tpu_custom_call" | custom-call | tf_op jit(solution)/shard_map/gradient/pallas_call | solution.py:603
  88.6 10.3 %all_to_all.31 = f32[32,1,1152]{2,1,0:T(1,128)S(1)} all-to-all(f32[32,1,1152]{2,1,0:T(1,128)S(1)} %bitcast.25), channel_id=1, replica_groups=mesh['cell'=8,'view'=4] {'cell','view'}, dimensions={0} | all-to-all | bytes 294912 | tf_op jit(solution)/shard_map/all_to_all | solution.py:645
  98.9 0.0 copy-done.2
  98.9 0.0 copy-done.12
  98.9 14.5 %tangent.1 = (f32[384,256]{1,0:T(8,128)S(1)}, f32[48,256]{1,0:T(8,128)S(1)}, f32[48,256]{1,0:T(8,128)S(1)}, f32[16,128]{1,0:T(8,128)S(1)}) custom-call(f32[288,128]{1,0:T(8,128)S(1)} %bitcast.16, s32[24,128]{1,0:T(8,128)S(1)} %get-tuple-element.55.ta_ref, s32[24,128]{1,0:T(8,128)S(1)} %get-tuple-element.54.tb_ref, f32[24,128]{1,0:T(8,128)S(1)} %broadcast_in_dim.23.ax_ref, ...), custom_call_target="tpu_custom_call" | custom-call | tf_op jit(solution)/shard_map/tangent/pallas_call | solution.py:603
  113.5 0.1 collective-permute-start.3
  113.6 3.8 %collective-permute-start.2 = (f32[48,256]{1,0:T(8,128)S(1)}, f32[48,256]{1,0:T(8,128)S(1)}, u32[]{:S(2)}, u32[]{:S(2)}) collective-permute-start(f32[48,256]{1,0:T(8,128)S(1)} %get-tuple-element.33.d_ref.rest_1_), channel_id=1, source_target_pairs={{0,3},{1,0},{2,1},{3,2},{4,7},{5,4},{6,5},{7,6},{8,11},{9,8},{10,9... | collective-permute-start | bytes 147464 | tf_op jit(solution)/shard_map/ppermute | solution.py:649
  117.4 2.1 collective-permute-done.3.past_ref
  119.4 0.0 collective-permute-done.2.next_ref
  119.4 16.3 %pull.4 = f32[288,128]{1,0:T(8,128)S(1)} custom-call(f32[384,256]{1,0:T(8,128)S(1)} %get-tuple-element.32.j_ref.rest_0_, f32[48,256]{1,0:T(8,128)S(1)} %get-tuple-element.33.d_ref.rest_1_, f32[48,256]{1,0:T(8,128)S(1)} %collective-permute-done.2.next_ref, f32[48,256]{1,0:T(8,128)S(1)} %collective-permute-done.3.past_ref, s32[48,1]{1,0:T(8,128)S(1)} %copy.16.pc_ref, ...), custom_call_target="tpu_custom_call" | custom-call | tf_op jit(solution)/shard_map/pull/pallas_call | solution.py:603
  135.7 12.8 %all_to_all.32 = f32[32,1,1152]{2,1,0:T(1,128)S(1)} all-to-all(f32[32,1,1152]{2,1,0:T(1,128)S(1)} %bitcast.22), channel_id=1, replica_groups=mesh['cell'=8,'view'=4] {'cell','view'}, dimensions={0} | all-to-all | bytes 294912 | tf_op jit(solution)/shard_map/all_to_all | solution.py:645
  148.5 6.3 %step.1 = (f32[288,128]{1,0:T(8,128)S(1)}, f32[14,2048]{1,0:T(8,128)S(1)}, f32[14,2048]{1,0:T(8,128)S(1)}, f32[14,2048]{1,0:T(8,128)S(1)}) custom-call(f32[288,128]{1,0:T(8,128)S(1)} %bitcast.15, f32[14,2048]{1,0:T(8,128)S(1)} %copy-done.5, f32[14,14,2048]{2,1,0:T(8,128)S(1)} %copy-done.3, s32[32,128]{1,0:T(8,128)S(1)} %copy-done.7, ...), custom_call_target="tpu_custom_call" | custom-call | tf_op jit(solution)/shard_map/step/pallas_call | solution.py:603
  154.8 10.3 %all_to_all.33 = f32[32,1,1152]{2,1,0:T(1,128)S(1)} all-to-all(f32[32,1,1152]{2,1,0:T(1,128)S(1)} %bitcast.24), channel_id=1, replica_groups=mesh['cell'=8,'view'=4] {'cell','view'}, dimensions={0} | all-to-all | bytes 294912 | tf_op jit(solution)/shard_map/all_to_all | solution.py:645
  165.1 14.5 %tangent_next.1 = (f32[384,256]{1,0:T(8,128)S(1)}, f32[48,256]{1,0:T(8,128)S(1)}, f32[48,256]{1,0:T(8,128)S(1)}, f32[16,128]{1,0:T(8,128)S(1)}) custom-call(f32[288,128]{1,0:T(8,128)S(1)} %bitcast.20, s32[24,128]{1,0:T(8,128)S(1)} %get-tuple-element.55.ta_ref, s32[24,128]{1,0:T(8,128)S(1)} %get-tuple-element.54.tb_ref, ...), custom_call_target="tpu_custom_call" | custom-call | tf_op jit(solution)/shard_map/tangent_next/pallas_call | solution.py:603
  179.7 0.1 collective-permute-start.5
  179.7 3.8 %collective-permute-start.4 = (f32[48,256]{1,0:T(8,128)S(1)}, f32[48,256]{1,0:T(8,128)S(1)}, u32[]{:S(2)}, u32[]{:S(2)}) collective-permute-start(f32[48,256]{1,0:T(8,128)S(1)} %get-tuple-element.40.d_ref), channel_id=1, source_target_pairs={{0,3},{1,0},{2,1},{3,2},{4,7},{5,4},{6,5},{7,6},{8,11},{9,8},{10,9... | collective-permute-start | bytes 147464 | tf_op jit(solution)/shard_map/ppermute | solution.py:649
  183.6 2.1 collective-permute-done.5.past_ref
  185.6 0.0 collective-permute-done.4.next_ref
  185.6 16.3 %pull.5 = (f32[288,128]{1,0:T(8,128)S(1)}, f32[14,2048]{1,0:T(8,128)S(1)}) custom-call(f32[384,256]{1,0:T(8,128)S(1)} %get-tuple-element.39.j_ref, f32[48,256]{1,0:T(8,128)S(1)} %get-tuple-element.40.d_ref, f32[48,256]{1,0:T(8,128)S(1)} %collective-permute-done.4.next_ref, f32[48,256]{1,0:T(8,128)S(1)} %collective-permute-done.5.past_ref, ...), custom_call_target="tpu_custom_call" | custom-call | tf_op jit(solution)/shard_map/pull/pallas_call | solution.py:603
  201.9 12.9 %all_to_all.34 = f32[32,1,1152]{2,1,0:T(1,128)S(1)} all-to-all(f32[32,1,1152]{2,1,0:T(1,128)S(1)} %bitcast.23), channel_id=1, replica_groups=mesh['cell'=8,'view'=4] {'cell','view'}, dimensions={0} | all-to-all | bytes 294912 | tf_op jit(solution)/shard_map/all_to_all | solution.py:645
  214.8 3.6 %finish.1 = (f32[14,2048]{1,0:T(8,128)}, f32[14,2048]{1,0:T(8,128)}) custom-call(f32[288,128]{1,0:T(8,128)S(1)} %bitcast.19, f32[14,2048]{1,0:T(8,128)S(1)} %copy-done.5, s32[32,128]{1,0:T(8,128)S(1)} %copy-done.7, s32[32,128]{1,0:T(8,128)S(1)} %get-tuple-element.52.sb_ref, f32[14,2048]{1,0:T(8,128)S(1)} %get-tuple-element.45.res_in, ...), custom_call_target="tpu_custom_call" | custom-call | tf_op jit(solution)/shard_map/finish/pallas_call | solution.py:603
  (6 shorter events, 0.0 us)
Async XLA Ops:
  1.4 5.5 %copy-start.6 = (s32[32,128]{1,0:T(8,128)}, s32[32,128]{1,0:T(8,128)S(1)}, u32[]{:S(2)}) copy-start(s32[32,128]{1,0:T(8,128)S(1)} %get-tuple-element.53.sa_ref) | copy-start | bytes 49156
  1.4 0.9 copy-start.4
  6.8 15.9 %all-to-all-start = ((f32[32,1,1152]{2,1,0:T(1,128)}), f32[32,1,1152]{2,1,0:T(1,128)S(1)}, u32[]{:S(2)}, u32[]{:S(2)}) async-start(f32[32,1,1152]{2,1,0:T(1,128)} %bitcast.1), calls=%async_computation | async-start | bytes 294912 | tf_op jit(solution)/shard_map/all_to_all | solution.py:645
  22.8 0.9 copy-start.10
  23.7 0.7 copy-start.11
  41.0 1.6 copy-start
  42.6 0.7 copy-start.8
  43.3 6.1 %collective-permute-start.1 = (f32[48,256]{1,0:T(8,128)}, f32[48,256]{1,0:T(8,128)S(1)}, u32[]{:S(2)}, u32[]{:S(2)}) collective-permute-start(f32[48,256]{1,0:T(8,128)} %get-tuple-element.27), channel_id=1, source_target_pairs={{0,1},{1,2},{2,3},{3,0},{4,5},{5,6},{6,7},{7,4},{8,9},{9,10},{10,1... | collective-permute-start | bytes 147464 | tf_op jit(solution)/shard_map/ppermute | solution.py:649
  43.3 6.1 %collective-permute-start = (f32[48,256]{1,0:T(8,128)}, f32[48,256]{1,0:T(8,128)S(1)}, u32[]{:S(2)}, u32[]{:S(2)}) collective-permute-start(f32[48,256]{1,0:T(8,128)} %get-tuple-element.26.d_ref), channel_id=1, source_target_pairs={{0,3},{1,0},{2,1},{3,2},{4,7},{5,4},{6,5},{7,6},{8,11},{9,8},{10,9... | collective-permute-start | bytes 147464 | tf_op jit(solution)/shard_map/ppermute | solution.py:649
  49.4 1.9 copy-start.1
  51.3 1.0 copy-start.9
  52.3 30.0 %copy-start.3 = (f32[14,14,2048]{2,1,0:T(8,128)S(1)}, f32[14,14,2048]{2,1,0:T(8,128)}, u32[]{:S(2)}) copy-start(f32[14,14,2048]{2,1,0:T(8,128)} %pre_ref.3) | copy-start | bytes 4816900
  52.3 30.0 %copy-start.5 = (f32[14,2048]{1,0:T(8,128)S(1)}, f32[14,2048]{1,0:T(8,128)}, u32[]{:S(2)}) copy-start(f32[14,2048]{1,0:T(8,128)} %attr_ref.7) | copy-start | bytes 344068
  52.3 30.0 %copy-start.7 = (s32[32,128]{1,0:T(8,128)S(1)}, s32[32,128]{1,0:T(8,128)}, u32[]{:S(2)}) copy-start(s32[32,128]{1,0:T(8,128)} %copy-done.6) | copy-start | bytes 49156
  52.3 46.6 %copy-start.2 = (f32[24,256,128]{2,1,0:T(8,128)S(1)}, f32[24,256,128]{2,1,0:T(8,128)}, u32[]{:S(2)}) copy-start(f32[24,256,128]{2,1,0:T(8,128)} %copy-done) | copy-start | bytes 9437188
  52.3 46.6 %copy-start.12 = (s32[48]{0:T(128)S(1)}, s32[48]{0:T(128)}, u32[]{:S(2)}) copy-start(s32[48]{0:T(128)} %param.13) | copy-start | bytes 580
  113.5 5.9 %collective-permute-start.3 = (f32[48,256]{1,0:T(8,128)S(1)}, f32[48,256]{1,0:T(8,128)S(1)}, u32[]{:S(2)}, u32[]{:S(2)}) collective-permute-start(f32[48,256]{1,0:T(8,128)S(1)} %get-tuple-element.34), channel_id=1, source_target_pairs={{0,1},{1,2},{2,3},{3,0},{4,5},{5,6},{6,7},{7,4},{8,9},{9,10},{10,1... | collective-permute-start | bytes 147464 | tf_op jit(solution)/shard_map/ppermute | solution.py:649
  113.6 5.9 %collective-permute-start.2 = (f32[48,256]{1,0:T(8,128)S(1)}, f32[48,256]{1,0:T(8,128)S(1)}, u32[]{:S(2)}, u32[]{:S(2)}) collective-permute-start(f32[48,256]{1,0:T(8,128)S(1)} %get-tuple-element.33.d_ref.rest_1_), channel_id=1, source_target_pairs={{0,3},{1,0},{2,1},{3,2},{4,7},{5,4},{6,5},{7,6},{8,11},{9,8},{10,9... | collective-permute-start | bytes 147464 | tf_op jit(solution)/shard_map/ppermute | solution.py:649
  179.7 5.9 %collective-permute-start.5 = (f32[48,256]{1,0:T(8,128)S(1)}, f32[48,256]{1,0:T(8,128)S(1)}, u32[]{:S(2)}, u32[]{:S(2)}) collective-permute-start(f32[48,256]{1,0:T(8,128)S(1)} %get-tuple-element.41), channel_id=1, source_target_pairs={{0,1},{1,2},{2,3},{3,0},{4,5},{5,6},{6,7},{7,4},{8,9},{9,10},{10,1... | collective-permute-start | bytes 147464 | tf_op jit(solution)/shard_map/ppermute | solution.py:649
  179.7 5.9 %collective-permute-start.4 = (f32[48,256]{1,0:T(8,128)S(1)}, f32[48,256]{1,0:T(8,128)S(1)}, u32[]{:S(2)}, u32[]{:S(2)}) collective-permute-start(f32[48,256]{1,0:T(8,128)S(1)} %get-tuple-element.40.d_ref), channel_id=1, source_target_pairs={{0,3},{1,0},{2,1},{3,2},{4,7},{5,4},{6,5},{7,6},{8,11},{9,8},{10,9... | collective-permute-start | bytes 147464 | tf_op jit(solution)/shard_map/ppermute | solution.py:649

commit v2 on v1

v2 whole, which is shorter than its diff:
```python
import functools
import math

import jax
import jax.numpy as jnp
from jax import lax
from jax.experimental import pallas as pl
from jax.experimental.pallas import tpu as pltpu
from jax.sharding import PartitionSpec as P

ITERS = 2
DAMPING = 0.5
PRIOR_WEIGHT = 0.3
DILATION = 0.3

F32 = jnp.float32
BF16 = jnp.bfloat16
LANES = 128
ROWS = 16
SCALAR = 6
ACTIVE = (0, 1, 2, 3, 4, 5, 6, 8, 9, 10, 11, 12)
KSLOTS = 64
PIXELS = 256
WIDE = 2 * LANES
TOGETHER = 4
ATTRS = 14


def camera_axes():
    tilt_cos, tilt_sin = (math.cos(0.3), math.sin(0.3))
    turn_cos, turn_sin = (math.cos(0.2), math.sin(0.2))
    return (
        (turn_cos, turn_sin * tilt_sin, turn_sin * tilt_cos),
        (0.0, tilt_cos, -tilt_sin),
        (-turn_sin, turn_cos * tilt_sin, turn_cos * tilt_cos),
    )


CAM = camera_axes()


def payload_rows(slots):
    return -(-len(ACTIVE) * slots // LANES)


def iota(shape, dim):
    return lax.broadcasted_iota(jnp.int32, shape, dim)


def split(value, parts):
    pieces = []
    for _ in range(parts - 1):
        piece = value.astype(BF16)
        pieces.append(piece)
        value = value - piece.astype(F32)
    pieces.append(value.astype(BF16))
    return pieces


def dot(a, b):
    return jnp.dot(a, b, preferred_element_type=F32)


def dot_nt(a, b):
    return lax.dot_general(a, b, (((1,), (1,)), ((), ())), preferred_element_type=F32)


def total(value):
    return jnp.sum(jnp.sum(value, axis=0, keepdims=True), axis=1, keepdims=True)


def pack(feature, out_ref, count, slots):
    depth = payload_rows(slots)
    lane = iota((count, LANES), 1)
    rows = [jnp.zeros((count, LANES), F32) for _ in range(depth)]
    for place, row in enumerate(ACTIVE):
        value = feature(row)
        at, offset = divmod(place * slots, LANES)
        end = offset + slots
        if offset:
            value = pltpu.roll(value, offset, 1)
        rows[at] = jnp.where((lane >= offset) & (lane < end), value, rows[at])
        if end > LANES:
            rows[at + 1] = jnp.where(lane < end - LANES, value, rows[at + 1])
    for at in range(depth):
        out_ref[pl.ds(at, count, stride=depth), :] = rows[at]


def unpack(in_ref, count, slots):
    depth = payload_rows(slots)
    lane = iota((count, LANES), 1)
    rows = [in_ref[pl.ds(at, count, stride=depth), :] for at in range(depth)]
    features = {}
    for place, row in enumerate(ACTIVE):
        at, offset = divmod(place * slots, LANES)
        value = rows[at]
        if offset + slots > LANES:
            value = jnp.where(lane >= offset, value, rows[at + 1])
        if offset:
            value = pltpu.roll(value, LANES - offset, 1)
        features[row] = jnp.where(lane < slots, value, 0.0)
    return features


def put_features(features, ref, count):
    ref[...] = jnp.zeros(ref.shape, F32)
    for row, value in features.items():
        ref[pl.ds(row, count, stride=ROWS), :] = value


def put_halves(chunk_index, lane, count, valid, a_ref, b_ref):
    half = count // 2
    upper = chunk_index >= half
    a_ref[...] = jnp.where(valid, jnp.where(upper, chunk_index - half, chunk_index), -1)
    b_ref[...] = jnp.where(valid, jnp.where(upper, LANES + lane, lane), -1)


def put_onehot(index_b, blocks, out_ref):
    wide = iota((WIDE, LANES), 0)
    for i in range(blocks):
        hit = jnp.where(wide == index_b[i : i + 1, :], 1.0, 0.0)
        out_ref[:, i * LANES : (i + 1) * LANES] = hit.astype(BF16)


def rows_of(index_ref, step):
    first = step * TOGETHER
    return jnp.concatenate([index_ref[pl.ds(first + i, 1), :] for i in range(TOGETHER)], axis=1)


def lanes_of(ref, step):
    width = TOGETHER * LANES
    return ref[:, pl.ds(pl.multiple_of(step * width, width), width)]


def gather(source_ref, chunks, index_a, onehot_ref, blocks, parts, lhs_ref, out_ref):
    half = chunks // 2
    for part, piece in enumerate(split(source_ref[...], parts)):
        for side in range(2):
            lhs_ref[:, part * WIDE + side * LANES : part * WIDE + (side + 1) * LANES] = piece[
                side * half * ROWS : (side + 1) * half * ROWS
            ]

    def body(step, carry):
        which = rows_of(index_a, step)
        onehot = lanes_of(onehot_ref, step)
        product = dot(lhs_ref[...], jnp.concatenate([onehot] * parts, axis=0))
        picked = product[:ROWS]
        for a in range(1, half):
            picked = jnp.where(which == a, product[a * ROWS : (a + 1) * ROWS], picked)
        for i in range(TOGETHER):
            start = pl.multiple_of((step * TOGETHER + i) * ROWS, ROWS)
            out_ref[pl.ds(start, ROWS), :] = picked[:, i * LANES : (i + 1) * LANES]
        return carry

    lax.fori_loop(0, blocks // TOGETHER, body, 0, unroll=2)


def scatter(source_ref, chunks, index_a, onehot_ref, blocks, acc_ref):
    half = chunks // 2
    acc_ref[...] = jnp.zeros(acc_ref.shape, F32)

    def body(step, carry):
        left = [[], []]
        for i in range(TOGETHER):
            at = step * TOGETHER + i
            value = source_ref[pl.ds(pl.multiple_of(at * ROWS, ROWS), ROWS), :]
            which = jnp.broadcast_to(index_a[pl.ds(at, 1), :], (ROWS, LANES)).astype(F32).astype(BF16)
            masks = [which == jnp.asarray(a, BF16) for a in range(half)]
            for part, piece in enumerate(split(value, 2)):
                nothing = jnp.zeros_like(piece)
                left[part].append(jnp.concatenate([jnp.where(mask, piece, nothing) for mask in masks], axis=0))
        onehot = lanes_of(onehot_ref, step)
        product = dot_nt(jnp.concatenate(left[0] + left[1], axis=1), jnp.concatenate([onehot, onehot], axis=1))
        for side in range(2):
            acc_ref[side] += column(product, side)
        return carry

    lax.fori_loop(0, blocks // TOGETHER, body, 0, unroll=2)


def wide_reader(ref, count):
    half = count // 2
    return lambda row: jnp.concatenate(
        [ref[side, pl.ds(row, half, stride=ROWS), :] for side in range(2)], axis=0
    )


def geometry(attr):
    e3, e5, e8 = jnp.exp(attr(3)), jnp.exp(attr(5)), jnp.exp(attr(8))
    a4, a6, a7, a9 = attr(4), attr(6), attr(7), attr(9)
    m = [
        (
            CAM[r][0] * e3 + CAM[r][1] * a4 + CAM[r][2] * a6,
            CAM[r][1] * e5 + CAM[r][2] * a7,
            CAM[r][2] * e8,
        )
        for r in range(2)
    ]
    sxx = m[0][0] * m[0][0] + m[0][1] * m[0][1] + m[0][2] * m[0][2] + DILATION
    sxy = m[0][0] * m[1][0] + m[0][1] * m[1][1] + m[0][2] * m[1][2]
    syy = m[1][0] * m[1][0] + m[1][1] * m[1][1] + m[1][2] * m[1][2] + DILATION
    inverse = 1.0 / (sxx * syy - sxy * sxy)
    return {
        "e": (e3, e5, e8),
        "m": m,
        "q": (syy * inverse, -sxy * inverse, sxx * inverse),
        "fade": 1.0 / (1.0 + jnp.exp(a9)),
        "a9": a9,
    }


def place(value):
    return [CAM[r][0] * value(0) + CAM[r][1] * value(1) + CAM[r][2] * value(2) for r in range(3)]


def project(attr, geo):
    x, y, z = place(attr)
    a9 = geo["a9"]
    shade = math.log(0.99) - (jnp.maximum(-a9, 0.0) + jnp.log(1.0 + jnp.exp(-jnp.abs(a9))))
    rows = {0: x, 1: y, 12: z, 2: geo["q"][0], 3: geo["q"][1], 4: geo["q"][2], 5: shade}
    for band in range(4):
        rows[8 + band] = attr(10 + band)
    return rows


def project_tangent(v, geo):
    x, y, z = place(v)
    (e3, e5, e8), m, (qxx, qxy, qyy) = geo["e"], geo["m"], geo["q"]
    v3, v5, v8 = e3 * v(3), e5 * v(5), e8 * v(8)
    d = [
        (
            CAM[r][0] * v3 + CAM[r][1] * v(4) + CAM[r][2] * v(6),
            CAM[r][1] * v5 + CAM[r][2] * v(7),
            CAM[r][2] * v8,
        )
        for r in range(2)
    ]
    sxx = 2.0 * (m[0][0] * d[0][0] + m[0][1] * d[0][1] + m[0][2] * d[0][2])
    syy = 2.0 * (m[1][0] * d[1][0] + m[1][1] * d[1][1] + m[1][2] * d[1][2])
    sxy = sum(m[0][c] * d[1][c] + d[0][c] * m[1][c] for c in range(3))
    rows = {
        0: x,
        1: y,
        12: z,
        2: -(qxx * qxx * sxx + 2.0 * qxx * qxy * sxy + qxy * qxy * syy),
        3: -(qxx * qxy * sxx + (qxx * qyy + qxy * qxy) * sxy + qxy * qyy * syy),
        4: -(qxy * qxy * sxx + 2.0 * qxy * qyy * sxy + qyy * qyy * syy),
        5: geo["fade"] * v(9),
    }
    for band in range(4):
        rows[8 + band] = v(10 + band)
    return rows


def project_cotangent(t, geo):
    (e3, e5, e8), m, (qxx, qxy, qyy) = geo["e"], geo["m"], geo["q"]
    bxx, bxy, byy = t(2), t(3), t(4)
    sxx = -(qxx * qxx * bxx + qxx * qxy * bxy + qxy * qxy * byy)
    sxy = -(2.0 * qxx * qxy * bxx + (qxx * qyy + qxy * qxy) * bxy + 2.0 * qxy * qyy * byy)
    syy = -(qxy * qxy * bxx + qxy * qyy * bxy + qyy * qyy * byy)
    n0 = [2.0 * sxx * m[0][c] + sxy * m[1][c] for c in range(3)]
    n1 = [2.0 * syy * m[1][c] + sxy * m[0][c] for c in range(3)]
    x, y, z = t(0), t(1), t(12)
    out = {j: CAM[0][j] * x + CAM[1][j] * y + CAM[2][j] * z for j in range(3)}
    out[3] = e3 * (CAM[0][0] * n0[0] + CAM[1][0] * n1[0])
    out[4] = CAM[0][1] * n0[0] + CAM[1][1] * n1[0]
    out[5] = e5 * (CAM[0][1] * n0[1] + CAM[1][1] * n1[1])
    out[6] = CAM[0][2] * n0[0] + CAM[1][2] * n1[0]
    out[7] = CAM[0][2] * n0[1] + CAM[1][2] * n1[1]
    out[8] = e8 * (CAM[0][2] * n0[2] + CAM[1][2] * n1[2])
    out[9] = geo["fade"] * t(5)
    for band in range(4):
        out[10 + band] = t(8 + band)
    return out


def to_chunks(ref, chunk_ref, chunks):
    for a in range(chunks):
        chunk_ref[a * ROWS : a * ROWS + ATTRS, :] = ref[:, a * LANES : (a + 1) * LANES]


def reader(ref, count):
    return lambda row: ref[pl.ds(row, count, stride=ROWS), :]


def chunk(ref, a):
    return ref[a * ROWS : a * ROWS + ATTRS, :]


def send_rows(rows, scalar, meta, sa_ref, so_ref, source_ref, lhs_ref, sent_ref, out_ref, parts):
    chunks, devices, slots = meta
    put_features(rows, source_ref, chunks)
    gather(source_ref, chunks, sa_ref, so_ref, devices, parts, lhs_ref, sent_ref)

    def feature(row):
        if row == SCALAR:
            return jnp.broadcast_to(scalar, (devices, LANES))
        return sent_ref[pl.ds(row, devices, stride=ROWS), :]

    pack(feature, out_ref, devices, slots)


def first_owner(
    meta, attr_ref, send_ref, out_ref, sa_ref, so_ref, chunk_ref, source_ref, lhs_ref, sent_ref, ids_ref, sb_ref
):
    chunks, devices, slots = meta
    ids_ref[...] = jnp.full(ids_ref.shape, -1, jnp.int32)
    ids_ref[:, :slots] = send_ref[...]
    ids = ids_ref[...]
    put_halves(ids >> 7, ids & (LANES - 1), chunks, ids >= 0, sa_ref, sb_ref)
    put_onehot(sb_ref, devices, so_ref)
    to_chunks(attr_ref, chunk_ref, chunks)
    attr = reader(chunk_ref, chunks)
    rows = project(attr, geometry(attr))
    send_rows(rows, jnp.zeros((1, 1), F32), meta, sa_ref, so_ref, source_ref, lhs_ref, sent_ref, out_ref, 3)


def receive_cotangent(meta, recv_ref, sa_ref, so_ref, sent_ref, acc_ref, grad_ref, geo):
    chunks, devices, slots = meta
    features = unpack(recv_ref, devices, slots)
    put_features(features, sent_ref, devices)
    scatter(sent_ref, chunks, sa_ref, so_ref, devices, acc_ref)
    for j, value in project_cotangent(wide_reader(acc_ref, chunks), geo).items():
        grad_ref[pl.ds(j, chunks, stride=ROWS), :] = value
    return features[SCALAR]


def first_lane(value):
    return total(jnp.where(iota(value.shape, 1) == 0, value, 0.0))


def apply_scaling(pre_ref, source_ref, a):
    result = None
    for i in range(ATTRS):
        term = pre_ref[i, :, a * LANES : (a + 1) * LANES] * source_ref[a * ROWS + i : a * ROWS + i + 1, :]
        result = term if result is None else result + term
    return result


def owner_step(
    meta, first, recv_ref, attr_ref, pre_ref, sa_ref, so_ref, *rest
):
    if first:
        (out_ref, res_out, dir_out, chunk_ref, source_ref, lhs_ref, sent_ref, acc_ref, grad_ref, dir_ref) = rest
    else:
        (
            res_in, dir_in, sc_ref,
            out_ref, res_out, sol_out, dir_out,
            chunk_ref, source_ref, lhs_ref, sent_ref, acc_ref, grad_ref, dir_ref,
        ) = rest
    chunks, devices, slots = meta
    to_chunks(attr_ref, chunk_ref, chunks)
    attr = reader(chunk_ref, chunks)
    geo = geometry(attr)
    scalars = receive_cotangent(meta, recv_ref, sa_ref, so_ref, sent_ref, acc_ref, grad_ref, geo)
    if not first:
        step = sc_ref[0:1, 0:1] / first_lane(scalars)
    norm = jnp.zeros((ATTRS, LANES), F32)
    for a in range(chunks):
        here = slice(a * LANES, (a + 1) * LANES)
        if first:
            residual = -chunk(grad_ref, a)
        else:
            before = dir_in[:, here]
            image = chunk(grad_ref, a) + DAMPING * before
            residual = res_in[:, here] - step * image
            sol_out[:, here] = step * before
        res_out[:, here] = residual
        grad_ref[a * ROWS : a * ROWS + ATTRS, :] = residual
        scaled = apply_scaling(pre_ref, grad_ref, a)
        dir_out[:, here] = scaled
        dir_ref[a * ROWS : a * ROWS + ATTRS, :] = scaled
        norm = norm + residual * scaled
    rows = project_tangent(reader(dir_ref, chunks), geo)
    send_rows(rows, total(norm), meta, sa_ref, so_ref, source_ref, lhs_ref, sent_ref, out_ref, 2)


def last_owner(
    meta, recv_ref, attr_ref, sa_ref, so_ref, res_in, sol_in, dir_in, sc_ref,
    sol_out, res_out, chunk_ref, sent_ref, acc_ref, grad_ref,
):
    chunks, devices, slots = meta
    to_chunks(attr_ref, chunk_ref, chunks)
    geo = geometry(reader(chunk_ref, chunks))
    scalars = receive_cotangent(meta, recv_ref, sa_ref, so_ref, sent_ref, acc_ref, grad_ref, geo)
    step = sc_ref[0:1, 0:1] / first_lane(scalars)
    for a in range(chunks):
        here = slice(a * LANES, (a + 1) * LANES)
        direction = dir_in[:, here]
        image = chunk(grad_ref, a) + DAMPING * direction
        sol_out[:, here] = sol_in[:, here] + step * direction
        res_out[:, here] = res_in[:, here] - step * image


def pixel_basis(shape, pixel_dim, term_dim):
    pixel, term = iota(shape, pixel_dim), iota(shape, term_dim) & 7
    x = (pixel & 15).astype(F32) - 7.5
    y = (pixel >> 4).astype(F32) - 7.5
    value = jnp.zeros(shape, F32)
    for m, field in enumerate((jnp.ones(shape, F32), x, y, x * x, x * y, y * y)):
        value = jnp.where(term == m, field, value)
    return value


def triangle(rows, later):
    shape = (rows, LANES)
    row, column = iota(shape, 0) & (LANES - 1), iota(shape, 1)
    same = (row >> 6) == (column >> 6)
    order = (row > column) if later else (row < column)
    return jnp.where(same & order, 1.0, 0.0).astype(BF16)


def put_terms(terms, ref, blocks):
    ref[...] = jnp.zeros(ref.shape, F32)
    for m, term in enumerate(terms):
        for part, piece in enumerate(split(term, 3)):
            ref[pl.ds(part * 8 + m, blocks, stride=32), :] = piece.astype(F32)


def tables(
    meta, list_ref, anchor_ref, ta_ref, ax_ref, ay_ref, onehot_ref, basis_ref, moment_ref, early_ref, late_ref,
    wide_ref, tb_ref,
):
    blocks, devices, slots = meta
    wide_ref[:, :KSLOTS] = list_ref[...]
    even, odd = (wide_ref[pl.ds(side, blocks, stride=2), :] for side in range(2))
    lane = iota((blocks, LANES), 1)
    entries = jnp.where(lane < KSLOTS, even, pltpu.roll(odd, KSLOTS, 1))
    source = ((entries.astype(F32) + 0.5) * (1.0 / slots)).astype(jnp.int32)
    put_halves(source, entries - slots * source, devices, entries >= 0, ta_ref, tb_ref)
    put_onehot(tb_ref, blocks, onehot_ref)
    tile, block = iota((blocks, 2 * blocks), 1), iota((blocks, 2 * blocks), 0)
    for axis, ref in enumerate((ax_ref, ay_ref)):
        sides = [
            jnp.sum(jnp.where(tile == 2 * block + side, anchor_ref[axis : axis + 1, :], 0.0), axis=1, keepdims=True)
            for side in range(2)
        ]
        ref[...] = jnp.where(lane < KSLOTS, sides[0], sides[1])
    basis = pixel_basis((PIXELS, 32), 0, 1)
    basis_ref[...] = jnp.where(iota((PIXELS, 32), 1) < 24, basis, 0.0).astype(BF16)
    moments = pixel_basis((ROWS, PIXELS), 1, 0)
    moments = jnp.where(iota((ROWS, PIXELS), 0) < 8, moments, 0.0).astype(BF16)
    moment_ref[...] = jnp.concatenate([moments, moments], axis=1)
    early_ref[...] = triangle(3 * LANES, False)
    late_ref[...] = triangle(2 * LANES, True)


def two_tiles(value):
    low = iota((8, LANES), 1) < KSLOTS
    return jnp.concatenate([jnp.where(low, value, 0.0), jnp.where(low, 0.0, value)], axis=0)


def stacked_lhs(value):
    high, low = split(value, 2)
    return jnp.concatenate(
        [jnp.concatenate([high, high], axis=1), jnp.concatenate([low, jnp.zeros_like(low)], axis=1)], axis=0
    )


def fold(value):
    half = value.shape[0] // 2
    return value[:half] + value[half:]


def side_by_side(value, parts):
    return jnp.concatenate(split(value, parts), axis=1)


def local_place(theta, ax_ref, ay_ref):
    return theta(0) - ax_ref[...] - 8.0, theta(1) - ay_ref[...] - 8.0


def send_order(pr_ref, depth, ds_ref):
    tiles = depth.shape[0]
    onehot = jnp.where(iota((tiles, tiles), 0) == pr_ref[...], 1.0, 0.0).astype(BF16)
    ds_ref[...] = sum(dot(onehot, piece) for piece in split(depth, 3))


def receive_rows(meta, recv_ref, ta_ref, to_ref, source_ref, lhs_ref, out_ref, parts):
    blocks, devices, slots = meta
    features = unpack(recv_ref, devices, slots)
    put_features(features, source_ref, devices)
    gather(source_ref, devices, ta_ref, to_ref, blocks, parts, lhs_ref, out_ref)
    return features[SCALAR]


def coefficients(term_ref, first):
    return jnp.concatenate(
        [
            term_ref[pl.ds(pl.multiple_of((first + i) * 32, 32), 32), :].astype(BF16)
            for i in range(TOGETHER)
        ],
        axis=1,
    )


def column(value, i):
    return value[:, i * LANES : (i + 1) * LANES]


def row_block(value, i):
    return value[i * PIXELS : (i + 1) * PIXELS]


def starts(first):
    return [pl.multiple_of((first + i) * ROWS, ROWS) for i in range(TOGETHER)]


def tile_forward(
    meta, recv_ref, ta_ref, to_ref, basis_ref, early_ref, ax_ref, ay_ref, target_ref, pr_ref,
    theta_ref, w_ref, ws_ref, rho_ref, left_ref, j_ref, d_ref, ds_ref,
    source_ref, lhs_ref, term_ref,
):
    blocks, devices, slots = meta
    receive_rows(meta, recv_ref, ta_ref, to_ref, source_ref, lhs_ref, theta_ref, 3)
    theta = reader(theta_ref, blocks)
    dx, dy = local_place(theta, ax_ref, ay_ref)
    qxx, qxy, qyy = theta(2), theta(3), theta(4)
    gx, gy = qxx * dx + qxy * dy, qxy * dx + qyy * dy
    terms = (theta(5) - 0.5 * (dx * gx + dy * gy), gx, gy, -0.5 * qxx, -qxy, -0.5 * qyy)
    put_terms(terms, term_ref, blocks)

    def body(step, carry):
        first = step * TOGETHER
        each = range(TOGETHER)
        product = dot(basis_ref[...], coefficients(term_ref, first))
        exponents = [column(product, i) for i in each]
        coverages = [jnp.exp(value) for value in exponents]
        logs = [jnp.log(1.0 - value) for value in coverages]
        for i in each:
            rho_ref[first + i] = jnp.exp(exponents[i] - logs[i])
        before = dot(jnp.concatenate([side_by_side(value, 3) for value in logs], axis=0), early_ref[...])
        lefts = []
        for i, start in enumerate(starts(first)):
            left = stacked_lhs(two_tiles(theta_ref[pl.ds(start + 8, 8), :]))
            left_ref[pl.ds(pl.multiple_of((first + i) * 32, 32), 32), :] = left
            lefts.append(left)
        images = []
        for i in each:
            weight = jnp.exp(row_block(before, i)) * coverages[i]
            w_ref[first + i] = weight
            pieces = side_by_side(weight, 2)
            ws_ref[first + i] = pieces
            images.append(fold(dot_nt(lefts[i], pieces)))
        for i, start in enumerate(starts(first)):
            image = images[i]
            j_ref[pl.ds(start, ROWS), :] = image
            j_ref[pl.ds(start, 4), :] = image[0:4] - target_ref[2 * (first + i)]
            j_ref[pl.ds(start + 8, 4), :] = image[8:12] - target_ref[2 * (first + i) + 1]
            d_ref[pl.ds(2 * (first + i), 1), :] = image[4:5]
            d_ref[pl.ds(2 * (first + i) + 1, 1), :] = image[12:13]
        return carry

    lax.fori_loop(0, blocks // TOGETHER, body, 0)
    send_order(pr_ref, d_ref[...], ds_ref)


def tile_tangent(
    meta, first_time, recv_ref, ta_ref, to_ref, basis_ref, early_ref, ax_ref, ay_ref, pr_ref,
    theta_ref, w_ref, ws_ref, rho_ref, left_ref, *rest
):
    if first_time:
        j_ref, d_ref, ds_ref, sc_ref, source_ref, lhs_ref, term_ref, dot_ref = rest
    else:
        j_in, sc_in, j_ref, d_ref, ds_ref, sc_ref, source_ref, lhs_ref, term_ref, dot_ref = rest
    blocks, devices, slots = meta
    norm = first_lane(receive_rows(meta, recv_ref, ta_ref, to_ref, source_ref, lhs_ref, dot_ref, 2))
    if not first_time:
        ratio = norm / sc_in[0:1, 0:1]
        sc_ref[8:16, :] = jnp.broadcast_to(ratio, (8, LANES))
    else:
        sc_ref[8:16, :] = jnp.zeros((8, LANES), F32)
    sc_ref[0:8, :] = jnp.broadcast_to(norm, (8, LANES))
    theta, tangent = reader(theta_ref, blocks), reader(dot_ref, blocks)
    dx, dy = local_place(theta, ax_ref, ay_ref)
    qxx, qxy, qyy = theta(2), theta(3), theta(4)
    gx, gy = qxx * dx + qxy * dy, qxy * dx + qyy * dy
    tx, ty, txx, txy, tyy = (tangent(row) for row in range(5))
    hx = txx * dx + txy * dy + qxx * tx + qxy * ty
    hy = txy * dx + tyy * dy + qxy * tx + qyy * ty
    constant = tangent(5) - 0.5 * (tx * gx + dx * hx + ty * gy + dy * hy)
    put_terms((constant, hx, hy, -0.5 * txx, -txy, -0.5 * tyy), term_ref, blocks)

    def body(step, carry):
        first = step * TOGETHER
        each = range(TOGETHER)
        product = dot(basis_ref[...], coefficients(term_ref, first))
        changes = [column(product, i) for i in each]
        scaled = [side_by_side(rho_ref[first + i] * changes[i], 2) for i in each]
        before = dot(jnp.concatenate(scaled, axis=0), early_ref[: 2 * LANES, :])
        images = []
        for i, start in enumerate(starts(first)):
            change = w_ref[first + i] * (changes[i] - row_block(before, i))
            left = left_ref[pl.ds(pl.multiple_of((first + i) * 32, 32), 32), :]
            left_change = stacked_lhs(two_tiles(dot_ref[pl.ds(start + 8, 8), :]))
            images.append(
                fold(
                    dot_nt(
                        jnp.concatenate([left, left_change], axis=1),
                        jnp.concatenate([side_by_side(change, 2), ws_ref[first + i]], axis=1),
                    )
                )
            )
        for i, start in enumerate(starts(first)):
            image = images[i]
            if not first_time:
                image = image + ratio * j_in[pl.ds(start, ROWS), :]
            j_ref[pl.ds(start, ROWS), :] = image
            d_ref[pl.ds(2 * (first + i), 1), :] = image[4:5]
            d_ref[pl.ds(2 * (first + i) + 1, 1), :] = image[12:13]
        return carry

    lax.fori_loop(0, blocks // TOGETHER, body, 0)
    send_order(pr_ref, d_ref[...], ds_ref)


def tile_pull(
    meta, mode, j_ref, d_ref, next_ref, past_ref, pr_ref, ta_ref, to_ref, moment_ref, late_ref, ax_ref, ay_ref,
    theta_ref, w_ref, ws_ref, rho_ref, left_ref, *rest
):
    if mode == 0:
        out_ref, cot_ref, turned_ref, term_ref, bar_ref, acc_ref = rest
    elif mode == 1:
        dir_in, out_ref, cot_ref, turned_ref, term_ref, bar_ref, acc_ref = rest
    else:
        scaled_in, dir_in, sc_ref, out_ref, dir_out, cot_ref, turned_ref, term_ref, bar_ref, acc_ref = rest
    blocks, devices, slots = meta
    tiles = 2 * blocks
    depth = d_ref[...]
    onehot = jnp.where(iota((tiles, tiles), 0) == pr_ref[...], 1.0, 0.0).T.astype(BF16)
    partner = sum(dot(onehot, piece) for piece in split(next_ref[...], 3))
    prior = PRIOR_WEIGHT * (depth - partner)
    depth_bar = PRIOR_WEIGHT * prior - PRIOR_WEIGHT * (PRIOR_WEIGHT * (past_ref[...] - depth))
    image = j_ref[...]
    cot_ref[...] = image
    for tile in range(tiles):
        cot_ref[tile * 8 + 4 : tile * 8 + 5, :] = depth_bar[tile : tile + 1, :]
    scalar = jnp.zeros((1, 1), F32)
    if mode:
        if mode == 1:
            direction = dir_in[...]
        else:
            direction = scaled_in[...] + sc_ref[8:9, 0:1] * dir_in[...]
            dir_out[...] = direction
        energy = jnp.where((iota(image.shape, 0) & 7) < 4, image * image, 0.0)
        scalar = total(energy) + total(prior * prior) + DAMPING * total(direction * direction)
    span = TOGETHER * ROWS
    for step in range(blocks // TOGETHER):
        high, low = split(cot_ref[step * span : (step + 1) * span, :], 2)
        high, low = high.astype(F32), low.astype(F32)
        turned_ref[step] = jnp.concatenate([high, low, high, jnp.zeros_like(high)], axis=0).T.astype(BF16)
    low_lanes = iota((8, LANES), 1) < KSLOTS

    def body(step, carry):
        first = step * TOGETHER
        each = range(TOGETHER)
        nothing = jnp.zeros((ROWS, LANES), BF16)
        columns = []
        for i in each:
            left = left_ref[pl.ds(pl.multiple_of((first + i) * 32, 32), 32), :]
            pieces = (left[:ROWS, :LANES], left[:ROWS, :LANES], left[ROWS:, :LANES], nothing)
            columns.append(
                jnp.concatenate([piece if other == i else nothing for piece in pieces for other in each], axis=0)
            )
        pulled = dot(turned_ref[step], jnp.concatenate(columns, axis=1))
        shares = [w_ref[first + i] * column(pulled, i) for i in each]
        after = dot(jnp.concatenate([side_by_side(share, 2) for share in shares], axis=0), late_ref[...])
        bars = [shares[i] - rho_ref[first + i] * row_block(after, i) for i in each]
        moments = dot(
            moment_ref[...],
            jnp.concatenate([jnp.concatenate(split(bar, 2), axis=0) for bar in bars], axis=1),
        )
        for i, start in enumerate(starts(first)):
            cot_high, cot_low = split(cot_ref[pl.ds(start, ROWS), :], 2)
            left = jnp.concatenate(
                [
                    jnp.concatenate([cot_high, cot_high], axis=1),
                    jnp.concatenate([cot_low, jnp.zeros_like(cot_low)], axis=1),
                ],
                axis=0,
            )
            pieces = ws_ref[first + i]
            colour_bar = fold(dot(left, jnp.concatenate([pieces[:, :LANES], pieces[:, LANES:]], axis=0)))
            bar_ref[pl.ds(start + 8, 8), :] = jnp.where(low_lanes, colour_bar[0:8], colour_bar[8:16])
            term_ref[pl.ds(start, 8), :] = column(moments, i)[0:8]
        return carry

    lax.fori_loop(0, blocks // TOGETHER, body, 0)
    theta, bars = reader(theta_ref, blocks), reader(term_ref, blocks)
    dx, dy = local_place(theta, ax_ref, ay_ref)
    qxx, qxy, qyy = theta(2), theta(3), theta(4)
    gx, gy = qxx * dx + qxy * dy, qxy * dx + qyy * dy
    b0 = bars(0)
    hx, hy = bars(1) - 0.5 * dx * b0, bars(2) - 0.5 * dy * b0
    values = (
        -0.5 * gx * b0 + qxx * hx + qxy * hy,
        -0.5 * gy * b0 + qxy * hx + qyy * hy,
        dx * hx - 0.5 * bars(3),
        dy * hx + dx * hy - bars(4),
        dy * hy - 0.5 * bars(5),
        b0,
        jnp.zeros_like(b0),
        jnp.zeros_like(b0),
    )
    for line, value in enumerate(values):
        bar_ref[pl.ds(line, blocks, stride=ROWS), :] = value
    scatter(bar_ref, devices, ta_ref, to_ref, blocks, acc_ref)
    summed = wide_reader(acc_ref, devices)

    def feature(line):
        if line == SCALAR:
            return jnp.broadcast_to(scalar, (devices, LANES))
        return summed(line)

    pack(feature, out_ref, devices, slots)


def call(body, outs, scratch, name, *args):
    return pl.pallas_call(
        body,
        out_shape=[jax.ShapeDtypeStruct(shape, dtype) for shape, dtype in outs],
        scratch_shapes=[pltpu.VMEM(shape, dtype) for shape, dtype in scratch],
        compiler_params=pltpu.CompilerParams(vmem_limit_bytes=VMEM_LIMIT),
        name=name,
    )(*args)


VMEM_LIMIT = 40 * 1024 * 1024


def local(attributes, tile_anchor, target, preconditioner, send_index, tile_list, pair_index):
    view_count = lax.axis_size("view")
    devices = lax.axis_size("cell") * view_count
    slots = send_index.shape[2]
    gaussians = attributes.shape[1]
    tiles = tile_list.shape[0]
    chunks, blocks = gaussians // LANES, tiles * KSLOTS // LANES
    depth = payload_rows(slots)

    pair_row = pair_index.reshape(1, tiles)

    owner_meta = (chunks, devices, slots)
    tile_meta = (blocks, devices, slots)
    shape = (devices * depth, LANES)
    payload = (shape, F32)
    field = ((blocks, PIXELS, LANES), F32)
    owned = ((ATTRS, gaussians), F32)
    images, maps, scalars = ((blocks * ROWS, PIXELS), F32), ((tiles, PIXELS), F32), ((16, LANES), F32)
    chunked = ((chunks * ROWS, LANES), F32)
    summed = ((2, chunks // 2 * ROWS, LANES), F32)
    arrived = ((devices * ROWS, LANES), F32)
    listed = ((blocks * ROWS, LANES), F32)
    terms = ((blocks * 32, LANES), F32)

    def exchange(value):
        value = value.reshape(devices, 1, depth * LANES)
        value = lax.all_to_all(value, ("cell", "view"), split_axis=0, concat_axis=0, tiled=True)
        return value.reshape(shape)

    def shifted(value, by):
        return lax.ppermute(value, "view", [(i, (i + by) % view_count) for i in range(view_count)])

    def owner_scratch(parts):
        return [chunked, chunked, ((chunks // 2 * ROWS, parts * WIDE), BF16), arrived]

    def tile_scratch(parts):
        return [arrived, ((devices // 2 * ROWS, parts * WIDE), BF16), terms]

    def pull(mode, image, maps_here, extra, outs):
        here, ordered = maps_here
        return call(
            functools.partial(tile_pull, tile_meta, mode),
            [payload] + outs,
            [
                images,
                ((blocks // TOGETHER, PIXELS, 4 * TOGETHER * ROWS), BF16),
                listed,
                listed,
                ((2, devices // 2 * ROWS, LANES), F32),
            ],
            "pull",
            image, here, shifted(here, -1), shifted(ordered, 1), pair_row, ta, onehot, moments, late, ax, ay,
            theta, weight, pieces, rho, left, *extra,
        )

    indices = ((devices, LANES), jnp.int32)
    sent, sa, sends = call(
        functools.partial(first_owner, owner_meta),
        [payload, indices, ((WIDE, devices * LANES), BF16)],
        owner_scratch(3) + [indices, indices],
        "project",
        attributes, send_index[0],
    )
    listing = ((blocks, LANES), jnp.int32)
    ta, ax, ay, onehot, basis, moments, early, late = call(
        functools.partial(tables, tile_meta),
        [
            listing,
            ((blocks, LANES), F32),
            ((blocks, LANES), F32),
            ((WIDE, blocks * LANES), BF16),
            ((PIXELS, 32), BF16),
            ((ROWS, 2 * PIXELS), BF16),
            ((3 * LANES, LANES), BF16),
            ((2 * LANES, LANES), BF16),
        ],
        [((tiles, LANES), jnp.int32), listing],
        "tables",
        tile_list, tile_anchor,
    )
    theta, weight, pieces, rho, left, image, here, ordered = call(
        functools.partial(tile_forward, tile_meta),
        [listed, field, ((blocks, PIXELS, WIDE), BF16), field, ((blocks * 32, WIDE), BF16), images, maps, maps],
        tile_scratch(3),
        "forward",
        exchange(sent), ta, onehot, basis, early, ax, ay, target, pair_row,
    )
    (sent,) = pull(0, image, (here, ordered), (), [])
    sent, residual, direction = call(
        functools.partial(owner_step, owner_meta, True),
        [payload, owned, owned],
        owner_scratch(2) + [summed, chunked, chunked],
        "gradient",
        exchange(sent), attributes, preconditioner, sa, sends,
    )
    image, here, ordered, first_sums = call(
        functools.partial(tile_tangent, tile_meta, True),
        [images, maps, maps, scalars],
        tile_scratch(2) + [listed],
        "tangent",
        exchange(sent), ta, onehot, basis, early, ax, ay, pair_row, theta, weight, pieces, rho, left,
    )
    (sent,) = pull(1, image, (here, ordered), (direction,), [])
    sent, residual, update, scaled = call(
        functools.partial(owner_step, owner_meta, False),
        [payload, owned, owned, owned],
        owner_scratch(2) + [summed, chunked, chunked],
        "step",
        exchange(sent), attributes, preconditioner, sa, sends, residual, direction, first_sums,
    )
    image, here, ordered, sums = call(
        functools.partial(tile_tangent, tile_meta, False),
        [images, maps, maps, scalars],
        tile_scratch(2) + [listed],
        "tangent_next",
        exchange(sent), ta, onehot, basis, early, ax, ay, pair_row, theta, weight, pieces, rho, left, image, first_sums,
    )
    sent, direction = pull(2, image, (here, ordered), (scaled, direction, sums), [owned])
    update, residual = call(
        functools.partial(last_owner, owner_meta),
        [owned, owned],
        [chunked, arrived, summed, chunked],
        "finish",
        exchange(sent), attributes, sa, sends, residual, update, direction, sums,
    )
    return (update, residual)


def solution(mesh):
    in_specs = (
        P(None, ("cell", "view")),
        P(None, ("cell", "view")),
        P(("cell", "view"), None, None),
        P(None, None, ("cell", "view")),
        P(("cell", "view"), None, None),
        P(("cell", "view"), None),
        P(("cell", "view")),
    )
    out_specs = (P(None, ("cell", "view")), P(None, ("cell", "view")))
    return jax.shard_map(local, mesh=mesh, in_specs=in_specs, out_specs=out_specs, check_vma=False)
```

time: 219 us -> 155 us (0.71)
  Pallas kernels: 116 us -> 57.3 us
  local copies, waits for them, and re-layouts: 10 us -> 5.95 us
  other arithmetic: 2.24 us -> 0 us
    pallas_call x10 -> x11, Pallas kernels: 116 us -> 57.3 us  [call(): pl.pallas_call(body, out_shape=[jax.ShapeDtypeStruct(shape, dtype) for sh...]
    unnamed x26 -> x22, local copies, waits for them, and re-layouts: 7.76 us -> 5.95 us
  transfers between devices with their start and end apart: 7 -> 7, of which waited for: 4 -> 4; matrix products, arithmetic and copies ran while one was open for 2% -> 0% of each run, Pallas kernels for 0% -> 1%
where the time goes in v2:
time: 155 us
  blocking collectives  59.2 us (38%)
  Pallas kernels  57.3 us (37%)
  starting transfers between devices  18.9 us (12%)
  waiting for transfers between devices  12.4 us (8%)
  local copies, waits for them, and re-layouts  5.95 us (4%)
    all_to_all x5, blocking collectives, exchange(): lax.all_to_all(value, ('cell', 'view'), split_axis=0, concat_axis=0, tile...  59.2 us
    pallas_call x11, Pallas kernels, call(): pl.pallas_call(body, out_shape=[jax.ShapeDtypeStruct(shape, dtype) for sh...  57.3 us
    ppermute x6, starting transfers between devices, shifted(): lax.ppermute(value, 'view', [(i, (i + by) % view_count) for i in range(vi...  11.6 us
    all_to_all x1, starting transfers between devices, exchange(): lax.all_to_all(value, ('cell', 'view'), split_axis=0, concat_axis=0, tile...  7.32 us
    all_to_all x1, waiting for transfers between devices, exchange(): lax.all_to_all(value, ('cell', 'view'), split_axis=0, concat_axis=0, tile...  6.24 us
    ppermute x6, waiting for transfers between devices, shifted(): lax.ppermute(value, 'view', [(i, (i + by) % view_count) for i in range(vi...  6.2 us
    unnamed x22, local copies, waits for them, and re-layouts  5.95 us
  transfers between devices with their start and end apart: 7, of which 4 were waited for; matrix products, arithmetic and copies ran while one was open for 0% of the time, Pallas kernels for 1%

profile of v2, /device:TPU:0, one launch (start us, length us, event | category | flops | bytes accessed | tf_op | source)
XLA Modules:
  0.0 154.6 jit_solution(17413292759769594406)
XLA Ops:
  0.6 0.0 copy-start.3
  0.6 0.9 copy-done.3
  1.5 0.0 copy-start.9
  1.5 0.7 copy-done.9
  2.3 3.3 %project.1 = (f32[288,128]{1,0:T(8,128)}, s32[32,128]{1,0:T(8,128)S(1)}, bf16[256,4096]{1,0:T(8,128)(2,1)S(1)}) custom-call(f32[14,2048]{1,0:T(8,128)S(1)} %copy-done.3, s32[32,96]{1,0:T(8,128)S(1)} %bitcast.31), custom_call_target="tpu_custom_call" | custom-call | tf_op jit(solution)/shard_map/project/pallas_call | solution.py:719
  5.6 0.0 copy-start
  5.6 1.3 copy-done
  6.9 7.3 %all-to-all-start = ((f32[32,1,1152]{2,1,0:T(1,128)}), f32[32,1,1152]{2,1,0:T(1,128)S(1)}, u32[]{:S(2)}, u32[]{:S(2)}) async-start(f32[32,1,1152]{2,1,0:T(1,128)} %bitcast.1), calls=%async_computation | async-start | bytes 294912 | tf_op jit(solution)/shard_map/all_to_all | solution.py:757
  14.3 0.0 copy-start.6
  14.3 0.7 copy-done.6
  15.0 0.0 copy-start.10
  15.0 0.7 copy-done.10
  15.7 0.9 tables.1
  16.6 6.2 %all-to-all-done = f32[32,1,1152]{2,1,0:T(1,128)S(1)} async-done(((f32[32,1,1152]{2,1,0:T(1,128)}), f32[32,1,1152]{2,1,0:T(1,128)S(1)}, u32[]{:S(2)}, u32[]{:S(2)}) %all-to-all-start) | async-done | bytes 147488 | tf_op jit(solution)/shard_map/all_to_all | solution.py:757
  22.9 0.0 copy-start.5
  22.9 0.9 copy-done.5
  23.8 0.0 copy-start.7
  23.8 0.7 copy-done.7
  24.5 6.9 %forward.1 = (f32[384,128]{1,0:T(8,128)S(1)}, f32[24,256,128]{2,1,0:T(8,128)S(1)}, bf16[24,256,256]{2,1,0:T(8,128)(2,1)S(1)}, f32[24,256,128]{2,1,0:T(8,128)S(1)...) custom-call(f32[288,128]{1,0:T(8,128)S(1)} %bitcast.14, ...), custom_call_target="tpu_custom_call" | custom-call | tf_op jit(solution)/shard_map/forward/pallas_call | solution.py:719
  31.3 0.1 collective-permute-start.1
  31.4 3.8 %collective-permute-start = (f32[48,256]{1,0:T(8,128)S(1)}, f32[48,256]{1,0:T(8,128)S(1)}, u32[]{:S(2)}, u32[]{:S(2)}) collective-permute-start(f32[48,256]{1,0:T(8,128)S(1)} %get-tuple-element.46.d_ref), channel_id=1, source_target_pairs={{0,3},{1,0},{2,1},{3,2},{4,7},{5,4},{6,5},{7,6},{8,11},{9,8},{10,9... | collective-permute-start | bytes 147464 | tf_op jit(solution)/shard_map/ppermute | solution.py:761
  35.2 2.1 %collective-permute-done.1.past_ref = f32[48,256]{1,0:T(8,128)S(1)} collective-permute-done((f32[48,256]{1,0:T(8,128)S(1)}, f32[48,256]{1,0:T(8,128)S(1)}, u32[]{:S(2)}, u32[]{:S(2)}) %collective-permute-start.1) | collective-permute-done | bytes 49184 | tf_op jit(solution)/shard_map/ppermute | solution.py:761
  37.3 0.0 collective-permute-done.next_ref
  37.3 0.0 copy-start.1
  37.3 0.0 copy-start.2
  37.3 0.0 copy-start.4
  37.3 7.2 %pull.3 = f32[288,128]{1,0:T(8,128)S(1)} custom-call(f32[384,256]{1,0:T(8,128)S(1)} %get-tuple-element.45.j_ref, f32[48,256]{1,0:T(8,128)S(1)} %get-tuple-element.46.d_ref, f32[48,256]{1,0:T(8,128)S(1)} %collective-permute-done.next_ref, f32[48,256]{1,0:T(8,128)S(1)} %collective-permute-done.1.past_ref, s32[1,48]{1,0:T(1,128)S(1)} %bitcast.26, ...), custom_call_target="tpu_custom_call" | custom-call | tf_op jit(solution)/shard_map/pull/pallas_call | solution.py:719
  44.5 12.8 %all_to_all.30 = f32[32,1,1152]{2,1,0:T(1,128)S(1)} all-to-all(f32[32,1,1152]{2,1,0:T(1,128)S(1)} %bitcast.20), channel_id=1, replica_groups=mesh['cell'=8,'view'=4] {'cell','view'}, dimensions={0} | all-to-all | bytes 294912 | tf_op jit(solution)/shard_map/all_to_all | solution.py:757
  57.3 0.0 copy-done.1
  57.3 0.0 copy-done.2
  57.3 0.0 copy-done.4
  57.3 3.9 %gradient.1 = (f32[288,128]{1,0:T(8,128)S(1)}, f32[14,2048]{1,0:T(8,128)S(1)}, f32[14,2048]{1,0:T(8,128)S(1)}) custom-call(f32[288,128]{1,0:T(8,128)S(1)} %bitcast.16, f32[14,2048]{1,0:T(8,128)S(1)} %copy-done.4, f32[14,14,2048]{2,1,0:T(8,128)S(1)} %copy-done.2, s32[32,128]{1,0:T(8,128)S(1)} %get-tuple-element.55.sa_ref, bf16[256,4096]{1,0:T(8,128)(2,1)S(1)} %copy-done.1), custom_call_target="tpu_custom_call" | custom-call | tf_op jit(solution)/shard_map/gradient/pallas_call | solution.py:719
  61.3 10.3 %all_to_all.31 = f32[32,1,1152]{2,1,0:T(1,128)S(1)} all-to-all(f32[32,1,1152]{2,1,0:T(1,128)S(1)} %bitcast.24), channel_id=1, replica_groups=mesh['cell'=8,'view'=4] {'cell','view'}, dimensions={0} | all-to-all | bytes 294912 | tf_op jit(solution)/shard_map/all_to_all | solution.py:757
  71.6 6.8 %tangent.1 = (f32[384,256]{1,0:T(8,128)S(1)}, f32[48,256]{1,0:T(8,128)S(1)}, f32[48,256]{1,0:T(8,128)S(1)}, f32[16,128]{1,0:T(8,128)S(1)}) custom-call(f32[288,128]{1,0:T(8,128)S(1)} %bitcast.19, s32[24,128]{1,0:T(8,128)S(1)} %get-tuple-element.39.ta_ref, bf16[256,3072]{1,0:T(8,128)(2,1)S(1)} %get-tuple-element.40.to_ref, ...), custom_call_target="tpu_custom_call" | custom-call | tf_op jit(solution)/shard_map/tangent/pallas_call | solution.py:719
  78.4 0.1 collective-permute-start.3
  78.4 3.8 %collective-permute-start.2 = (f32[48,256]{1,0:T(8,128)S(1)}, f32[48,256]{1,0:T(8,128)S(1)}, u32[]{:S(2)}, u32[]{:S(2)}) collective-permute-start(f32[48,256]{1,0:T(8,128)S(1)} %get-tuple-element.59.d_ref), channel_id=1, source_target_pairs={{0,3},{1,0},{2,1},{3,2},{4,7},{5,4},{6,5},{7,6},{8,11},{9,8},{10,9... | collective-permute-start | bytes 147464 | tf_op jit(solution)/shard_map/ppermute | solution.py:761
  82.2 2.1 %collective-permute-done.3.past_ref = f32[48,256]{1,0:T(8,128)S(1)} collective-permute-done((f32[48,256]{1,0:T(8,128)S(1)}, f32[48,256]{1,0:T(8,128)S(1)}, u32[]{:S(2)}, u32[]{:S(2)}) %collective-permute-start.3) | collective-permute-done | bytes 49184 | tf_op jit(solution)/shard_map/ppermute | solution.py:761
  84.3 0.0 collective-permute-done.2.next_ref
  84.3 7.3 %pull.4 = f32[288,128]{1,0:T(8,128)S(1)} custom-call(f32[384,256]{1,0:T(8,128)S(1)} %get-tuple-element.58.j_ref.rest_0_, f32[48,256]{1,0:T(8,128)S(1)} %get-tuple-element.59.d_ref, f32[48,256]{1,0:T(8,128)S(1)} %collective-permute-done.2.next_ref, f32[48,256]{1,0:T(8,128)S(1)} %collective-permute-done.3.past_ref, s32[1,48]{1,0:T(1,128)S(1)} %bitcast.28, ...), custom_call_target="tpu_custom_call" | custom-call | tf_op jit(solution)/shard_map/pull/pallas_call | solution.py:719
  91.6 0.0 copy-start.8
  91.6 12.8 %all_to_all.32 = f32[32,1,1152]{2,1,0:T(1,128)S(1)} all-to-all(f32[32,1,1152]{2,1,0:T(1,128)S(1)} %bitcast.21), channel_id=1, replica_groups=mesh['cell'=8,'view'=4] {'cell','view'}, dimensions={0} | all-to-all | bytes 294912 | tf_op jit(solution)/shard_map/all_to_all | solution.py:757
  104.4 3.9 %step.1 = (f32[288,128]{1,0:T(8,128)S(1)}, f32[14,2048]{1,0:T(8,128)S(1)}, f32[14,2048]{1,0:T(8,128)S(1)}, f32[14,2048]{1,0:T(8,128)S(1)}) custom-call(f32[288,128]{1,0:T(8,128)S(1)} %bitcast.15, f32[14,2048]{1,0:T(8,128)S(1)} %copy-done.4, f32[14,14,2048]{2,1,0:T(8,128)S(1)} %copy-done.2, s32[32,128]{1,0:T(8,128)S(1)} %get-tuple-element.55.sa_ref, ...), custom_call_target="tpu_custom_call" | custom-call | tf_op jit(solution)/shard_map/step/pallas_call | solution.py:719
  108.4 10.3 %all_to_all.33 = f32[32,1,1152]{2,1,0:T(1,128)S(1)} all-to-all(f32[32,1,1152]{2,1,0:T(1,128)S(1)} %bitcast.23), channel_id=1, replica_groups=mesh['cell'=8,'view'=4] {'cell','view'}, dimensions={0} | all-to-all | bytes 294912 | tf_op jit(solution)/shard_map/all_to_all | solution.py:757
  118.7 0.0 copy-done.8
  118.7 6.8 %tangent_next.1 = (f32[384,256]{1,0:T(8,128)S(1)}, f32[48,256]{1,0:T(8,128)S(1)}, f32[48,256]{1,0:T(8,128)S(1)}, f32[16,128]{1,0:T(8,128)S(1)}) custom-call(f32[288,128]{1,0:T(8,128)S(1)} %bitcast.18, s32[24,128]{1,0:T(8,128)S(1)} %get-tuple-element.39.ta_ref, bf16[256,3072]{1,0:T(8,128)(2,1)S(1)} %get-tuple-element.40.to_ref, ...), custom_call_target="tpu_custom_call" | custom-call | tf_op jit(solution)/shard_map/tangent_next/pallas_call | solution.py:719
  125.5 0.1 collective-permute-start.5
  125.6 3.8 %collective-permute-start.4 = (f32[48,256]{1,0:T(8,128)S(1)}, f32[48,256]{1,0:T(8,128)S(1)}, u32[]{:S(2)}, u32[]{:S(2)}) collective-permute-start(f32[48,256]{1,0:T(8,128)S(1)} %get-tuple-element.66.d_ref), channel_id=1, source_target_pairs={{0,3},{1,0},{2,1},{3,2},{4,7},{5,4},{6,5},{7,6},{8,11},{9,8},{10,9... | collective-permute-start | bytes 147464 | tf_op jit(solution)/shard_map/ppermute | solution.py:761
  129.4 2.1 %collective-permute-done.5.past_ref = f32[48,256]{1,0:T(8,128)S(1)} collective-permute-done((f32[48,256]{1,0:T(8,128)S(1)}, f32[48,256]{1,0:T(8,128)S(1)}, u32[]{:S(2)}, u32[]{:S(2)}) %collective-permute-start.5) | collective-permute-done | bytes 49184 | tf_op jit(solution)/shard_map/ppermute | solution.py:761
  131.5 0.0 collective-permute-done.4.next_ref
  131.5 7.2 %pull.5 = (f32[288,128]{1,0:T(8,128)S(1)}, f32[14,2048]{1,0:T(8,128)S(1)}) custom-call(f32[384,256]{1,0:T(8,128)S(1)} %get-tuple-element.65.j_ref, f32[48,256]{1,0:T(8,128)S(1)} %get-tuple-element.66.d_ref, f32[48,256]{1,0:T(8,128)S(1)} %collective-permute-done.4.next_ref, f32[48,256]{1,0:T(8,128)S(1)} %collective-permute-done.5.past_ref, ...), custom_call_target="tpu_custom_call" | custom-call | tf_op jit(solution)/shard_map/pull/pallas_call | solution.py:719
  138.7 12.8 %all_to_all.34 = f32[32,1,1152]{2,1,0:T(1,128)S(1)} all-to-all(f32[32,1,1152]{2,1,0:T(1,128)S(1)} %bitcast.22), channel_id=1, replica_groups=mesh['cell'=8,'view'=4] {'cell','view'}, dimensions={0} | all-to-all | bytes 294912 | tf_op jit(solution)/shard_map/all_to_all | solution.py:757
  151.6 3.0 %finish.1 = (f32[14,2048]{1,0:T(8,128)}, f32[14,2048]{1,0:T(8,128)}) custom-call(f32[288,128]{1,0:T(8,128)S(1)} %bitcast.17, f32[14,2048]{1,0:T(8,128)S(1)} %copy-done.4, s32[32,128]{1,0:T(8,128)S(1)} %get-tuple-element.55.sa_ref, bf16[256,4096]{1,0:T(8,128)(2,1)S(1)} %copy-done.1, f32[14,2048]{1,0:T(8,128)S(1)} %get-tuple-element.71.res_in, ...), custom_call_target="tpu_custom_call" | custom-call | tf_op jit(solution)/shard_map/finish/pallas_call | solution.py:719
Async XLA Ops:
  0.6 0.9 copy-start.3
  1.5 0.7 copy-start.9
  5.6 1.3 copy-start
  6.9 15.9 %all-to-all-start = ((f32[32,1,1152]{2,1,0:T(1,128)}), f32[32,1,1152]{2,1,0:T(1,128)S(1)}, u32[]{:S(2)}, u32[]{:S(2)}) async-start(f32[32,1,1152]{2,1,0:T(1,128)} %bitcast.1), calls=%async_computation | async-start | bytes 294912 | tf_op jit(solution)/shard_map/all_to_all | solution.py:757
  14.3 0.7 copy-start.6
  15.0 0.7 copy-start.10
  22.9 0.9 copy-start.5
  23.8 0.7 copy-start.7
  31.3 5.9 %collective-permute-start.1 = (f32[48,256]{1,0:T(8,128)S(1)}, f32[48,256]{1,0:T(8,128)S(1)}, u32[]{:S(2)}, u32[]{:S(2)}) collective-permute-start(f32[48,256]{1,0:T(8,128)S(1)} %get-tuple-element.47), channel_id=1, source_target_pairs={{0,1},{1,2},{2,3},{3,0},{4,5},{5,6},{6,7},{7,4},{8,9},{9,10},{10,1... | collective-permute-start | bytes 147464 | tf_op jit(solution)/shard_map/ppermute | solution.py:761
  31.4 5.9 %collective-permute-start = (f32[48,256]{1,0:T(8,128)S(1)}, f32[48,256]{1,0:T(8,128)S(1)}, u32[]{:S(2)}, u32[]{:S(2)}) collective-permute-start(f32[48,256]{1,0:T(8,128)S(1)} %get-tuple-element.46.d_ref), channel_id=1, source_target_pairs={{0,3},{1,0},{2,1},{3,2},{4,7},{5,4},{6,5},{7,6},{8,11},{9,8},{10,9... | collective-permute-start | bytes 147464 | tf_op jit(solution)/shard_map/ppermute | solution.py:761
  37.3 20.1 %copy-start.1 = (bf16[256,4096]{1,0:T(8,128)(2,1)S(1)}, bf16[256,4096]{1,0:T(8,128)(2,1)}, u32[]{:S(2)}) copy-start(bf16[256,4096]{1,0:T(8,128)(2,1)} %copy-done) | copy-start | bytes 6291460
  37.3 20.1 %copy-start.2 = (f32[14,14,2048]{2,1,0:T(8,128)S(1)}, f32[14,14,2048]{2,1,0:T(8,128)}, u32[]{:S(2)}) copy-start(f32[14,14,2048]{2,1,0:T(8,128)} %pre_ref.3) | copy-start | bytes 4816900
  37.3 20.1 %copy-start.4 = (f32[14,2048]{1,0:T(8,128)S(1)}, f32[14,2048]{1,0:T(8,128)}, u32[]{:S(2)}) copy-start(f32[14,2048]{1,0:T(8,128)} %attr_ref.7) | copy-start | bytes 344068
  78.4 5.9 %collective-permute-start.3 = (f32[48,256]{1,0:T(8,128)S(1)}, f32[48,256]{1,0:T(8,128)S(1)}, u32[]{:S(2)}, u32[]{:S(2)}) collective-permute-start(f32[48,256]{1,0:T(8,128)S(1)} %get-tuple-element.60), channel_id=1, source_target_pairs={{0,1},{1,2},{2,3},{3,0},{4,5},{5,6},{6,7},{7,4},{8,9},{9,10},{10,1... | collective-permute-start | bytes 147464 | tf_op jit(solution)/shard_map/ppermute | solution.py:761
  78.4 5.9 %collective-permute-start.2 = (f32[48,256]{1,0:T(8,128)S(1)}, f32[48,256]{1,0:T(8,128)S(1)}, u32[]{:S(2)}, u32[]{:S(2)}) collective-permute-start(f32[48,256]{1,0:T(8,128)S(1)} %get-tuple-element.59.d_ref), channel_id=1, source_target_pairs={{0,3},{1,0},{2,1},{3,2},{4,7},{5,4},{6,5},{7,6},{8,11},{9,8},{10,9... | collective-permute-start | bytes 147464 | tf_op jit(solution)/shard_map/ppermute | solution.py:761
  91.6 27.1 %copy-start.8 = (s32[48]{0:T(128)S(1)}, s32[48]{0:T(128)}, u32[]{:S(2)}) copy-start(s32[48]{0:T(128)} %param.13) | copy-start | bytes 580
  125.5 5.9 %collective-permute-start.5 = (f32[48,256]{1,0:T(8,128)S(1)}, f32[48,256]{1,0:T(8,128)S(1)}, u32[]{:S(2)}, u32[]{:S(2)}) collective-permute-start(f32[48,256]{1,0:T(8,128)S(1)} %get-tuple-element.67), channel_id=1, source_target_pairs={{0,1},{1,2},{2,3},{3,0},{4,5},{5,6},{6,7},{7,4},{8,9},{9,10},{10,1... | collective-permute-start | bytes 147464 | tf_op jit(solution)/shard_map/ppermute | solution.py:761
  125.6 5.9 %collective-permute-start.4 = (f32[48,256]{1,0:T(8,128)S(1)}, f32[48,256]{1,0:T(8,128)S(1)}, u32[]{:S(2)}, u32[]{:S(2)}) collective-permute-start(f32[48,256]{1,0:T(8,128)S(1)} %get-tuple-element.66.d_ref), channel_id=1, source_target_pairs={{0,3},{1,0},{2,1},{3,2},{4,7},{5,4},{6,5},{7,6},{8,11},{9,8},{10,9... | collective-permute-start | bytes 147464 | tf_op jit(solution)/shard_map/ppermute | solution.py:761

commit v3 on v2

--- a/solution.py
+++ b/solution.py
@@ -23,6 +23,7 @@
 PIXELS = 256
 WIDE = 2 * LANES
 TOGETHER = 4
+GROUP = 8
 ATTRS = 14
 
 
@@ -132,6 +133,10 @@
     return ref[:, pl.ds(pl.multiple_of(step * width, width), width)]
 
 
+def whole(blocks):
+    return min(blocks // TOGETHER, 8)
+
+
 def gather(source_ref, chunks, index_a, onehot_ref, blocks, parts, lhs_ref, out_ref):
     half = chunks // 2
     for part, piece in enumerate(split(source_ref[...], parts)):
@@ -152,10 +157,10 @@
             out_ref[pl.ds(start, ROWS), :] = picked[:, i * LANES : (i + 1) * LANES]
         return carry
 
-    lax.fori_loop(0, blocks // TOGETHER, body, 0, unroll=2)
-
-
-def scatter(source_ref, chunks, index_a, onehot_ref, blocks, acc_ref):
+    lax.fori_loop(0, blocks // TOGETHER, body, 0, unroll=whole(blocks))
+
+
+def scatter(source_ref, chunks, index_a, onehot_ref, blocks, acc_ref, unroll):
     half = chunks // 2
     acc_ref[...] = jnp.zeros(acc_ref.shape, F32)
 
@@ -175,7 +180,7 @@
             acc_ref[side] += column(product, side)
         return carry
 
-    lax.fori_loop(0, blocks // TOGETHER, body, 0, unroll=2)
+    lax.fori_loop(0, blocks // TOGETHER, body, 0, unroll=unroll)
 
 
 def wide_reader(ref, count):
@@ -315,11 +320,11 @@
     send_rows(rows, jnp.zeros((1, 1), F32), meta, sa_ref, so_ref, source_ref, lhs_ref, sent_ref, out_ref, 3)
 
 
-def receive_cotangent(meta, recv_ref, sa_ref, so_ref, sent_ref, acc_ref, grad_ref, geo):
+def receive_cotangent(meta, recv_ref, sa_ref, so_ref, sent_ref, acc_ref, grad_ref, geo, unroll):
     chunks, devices, slots = meta
     features = unpack(recv_ref, devices, slots)
     put_features(features, sent_ref, devices)
-    scatter(sent_ref, chunks, sa_ref, so_ref, devices, acc_ref)
+    scatter(sent_ref, chunks, sa_ref, so_ref, devices, acc_ref, unroll)
     for j, value in project_cotangent(wide_reader(acc_ref, chunks), geo).items():
         grad_ref[pl.ds(j, chunks, stride=ROWS), :] = value
     return features[SCALAR]
@@ -352,7 +357,7 @@
     to_chunks(attr_ref, chunk_ref, chunks)
     attr = reader(chunk_ref, chunks)
     geo = geometry(attr)
-    scalars = receive_cotangent(meta, recv_ref, sa_ref, so_ref, sent_ref, acc_ref, grad_ref, geo)
+    scalars = receive_cotangent(meta, recv_ref, sa_ref, so_ref, sent_ref, acc_ref, grad_ref, geo, 4)
     if not first:
         step = sc_ref[0:1, 0:1] / first_lane(scalars)
     norm = jnp.zeros((ATTRS, LANES), F32)
@@ -382,7 +387,7 @@
     chunks, devices, slots = meta
     to_chunks(attr_ref, chunk_ref, chunks)
     geo = geometry(reader(chunk_ref, chunks))
-    scalars = receive_cotangent(meta, recv_ref, sa_ref, so_ref, sent_ref, acc_ref, grad_ref, geo)
+    scalars = receive_cotangent(meta, recv_ref, sa_ref, so_ref, sent_ref, acc_ref, grad_ref, geo, whole(devices))
     step = sc_ref[0:1, 0:1] / first_lane(scalars)
     for a in range(chunks):
         here = slice(a * LANES, (a + 1) * LANES)
@@ -413,8 +418,7 @@
 def put_terms(terms, ref, blocks):
     ref[...] = jnp.zeros(ref.shape, F32)
     for m, term in enumerate(terms):
-        for part, piece in enumerate(split(term, 3)):
-            ref[pl.ds(part * 8 + m, blocks, stride=32), :] = piece.astype(F32)
+        ref[pl.ds(m, blocks, stride=8), :] = term
 
 
 def tables(
@@ -485,13 +489,12 @@
 
 
 def coefficients(term_ref, first):
-    return jnp.concatenate(
-        [
-            term_ref[pl.ds(pl.multiple_of((first + i) * 32, 32), 32), :].astype(BF16)
-            for i in range(TOGETHER)
-        ],
-        axis=1,
-    )
+    columns = []
+    for i in range(GROUP):
+        value = term_ref[pl.ds(pl.multiple_of((first + i) * 8, 8), 8), :]
+        pieces = [piece.astype(F32) for piece in split(value, 3)] + [jnp.zeros_like(value)]
+        columns.append(jnp.concatenate(pieces, axis=0).astype(BF16))
+    return jnp.concatenate(columns, axis=1)
 
 
 def column(value, i):
@@ -502,8 +505,8 @@
     return value[i * PIXELS : (i + 1) * PIXELS]
 
 
-def starts(first):
-    return [pl.multiple_of((first + i) * ROWS, ROWS) for i in range(TOGETHER)]
+def starts(first, count=TOGETHER):
+    return [pl.multiple_of((first + i) * ROWS, ROWS) for i in range(count)]
 
 
 def tile_forward(
@@ -521,8 +524,8 @@
     put_terms(terms, term_ref, blocks)
 
     def body(step, carry):
-        first = step * TOGETHER
-        each = range(TOGETHER)
+        first = step * GROUP
+        each = range(GROUP)
         product = dot(basis_ref[...], coefficients(term_ref, first))
         exponents = [column(product, i) for i in each]
         coverages = [jnp.exp(value) for value in exponents]
@@ -531,7 +534,7 @@
             rho_ref[first + i] = jnp.exp(exponents[i] - logs[i])
         before = dot(jnp.concatenate([side_by_side(value, 3) for value in logs], axis=0), early_ref[...])
         lefts = []
-        for i, start in enumerate(starts(first)):
+        for i, start in enumerate(starts(first, GROUP)):
             left = stacked_lhs(two_tiles(theta_ref[pl.ds(start + 8, 8), :]))
             left_ref[pl.ds(pl.multiple_of((first + i) * 32, 32), 32), :] = left
             lefts.append(left)
@@ -542,7 +545,7 @@
             pieces = side_by_side(weight, 2)
             ws_ref[first + i] = pieces
             images.append(fold(dot_nt(lefts[i], pieces)))
-        for i, start in enumerate(starts(first)):
+        for i, start in enumerate(starts(first, GROUP)):
             image = images[i]
             j_ref[pl.ds(start, ROWS), :] = image
             j_ref[pl.ds(start, 4), :] = image[0:4] - target_ref[2 * (first + i)]
@@ -551,7 +554,7 @@
             d_ref[pl.ds(2 * (first + i) + 1, 1), :] = image[12:13]
         return carry
 
-    lax.fori_loop(0, blocks // TOGETHER, body, 0)
+    lax.fori_loop(0, blocks // GROUP, body, 0)
     send_order(pr_ref, d_ref[...], ds_ref)
 
 
@@ -582,14 +585,14 @@
     put_terms((constant, hx, hy, -0.5 * txx, -txy, -0.5 * tyy), term_ref, blocks)
 
     def body(step, carry):
-        first = step * TOGETHER
-        each = range(TOGETHER)
+        first = step * GROUP
+        each = range(GROUP)
         product = dot(basis_ref[...], coefficients(term_ref, first))
         changes = [column(product, i) for i in each]
         scaled = [side_by_side(rho_ref[first + i] * changes[i], 2) for i in each]
         before = dot(jnp.concatenate(scaled, axis=0), early_ref[: 2 * LANES, :])
         images = []
-        for i, start in enumerate(starts(first)):
+        for i, start in enumerate(starts(first, GROUP)):
             change = w_ref[first + i] * (changes[i] - row_block(before, i))
             left = left_ref[pl.ds(pl.multiple_of((first + i) * 32, 32), 32), :]
             left_change = stacked_lhs(two_tiles(dot_ref[pl.ds(start + 8, 8), :]))
@@ -601,7 +604,7 @@
                     )
                 )
             )
-        for i, start in enumerate(starts(first)):
+        for i, start in enumerate(starts(first, GROUP)):
             image = images[i]
             if not first_time:
                 image = image + ratio * j_in[pl.ds(start, ROWS), :]
@@ -610,7 +613,7 @@
             d_ref[pl.ds(2 * (first + i) + 1, 1), :] = image[12:13]
         return carry
 
-    lax.fori_loop(0, blocks // TOGETHER, body, 0)
+    lax.fori_loop(0, blocks // GROUP, body, 0)
     send_order(pr_ref, d_ref[...], ds_ref)
 
 
@@ -647,8 +650,8 @@
     span = TOGETHER * ROWS
     for step in range(blocks // TOGETHER):
         high, low = split(cot_ref[step * span : (step + 1) * span, :], 2)
-        high, low = high.astype(F32), low.astype(F32)
-        turned_ref[step] = jnp.concatenate([high, low, high, jnp.zeros_like(high)], axis=0).T.astype(BF16)
+        turned = jnp.concatenate([high.astype(F32), low.astype(F32)], axis=0).T.astype(BF16)
+        turned_ref[step] = jnp.concatenate([turned, turned], axis=1)
     low_lanes = iota((8, LANES), 1) < KSLOTS
 
     def body(step, carry):
@@ -685,7 +688,7 @@
             term_ref[pl.ds(start, 8), :] = column(moments, i)[0:8]
         return carry
 
-    lax.fori_loop(0, blocks // TOGETHER, body, 0)
+    lax.fori_loop(0, blocks // TOGETHER, body, 0, unroll=3)
     theta, bars = reader(theta_ref, blocks), reader(term_ref, blocks)
     dx, dy = local_place(theta, ax_ref, ay_ref)
     qxx, qxy, qyy = theta(2), theta(3), theta(4)
@@ -704,7 +707,7 @@
     )
     for line, value in enumerate(values):
         bar_ref[pl.ds(line, blocks, stride=ROWS), :] = value
-    scatter(bar_ref, devices, ta_ref, to_ref, blocks, acc_ref)
+    scatter(bar_ref, devices, ta_ref, to_ref, blocks, acc_ref, whole(blocks))
     summed = wide_reader(acc_ref, devices)
 
     def feature(line):
@@ -750,7 +753,7 @@
     summed = ((2, chunks // 2 * ROWS, LANES), F32)
     arrived = ((devices * ROWS, LANES), F32)
     listed = ((blocks * ROWS, LANES), F32)
-    terms = ((blocks * 32, LANES), F32)
+    terms = ((blocks * 8, LANES), F32)
 
     def exchange(value):
         value = value.reshape(devices, 1, depth * LANES)

time: 155 us -> 143 us (0.923)
  Pallas kernels: 57.3 us -> 45.5 us
    pallas_call x11, Pallas kernels: 57.3 us -> 45.5 us  [call(): pl.pallas_call(body, out_shape=[jax.ShapeDtypeStruct(shape, dtype) for sh...]
where the time goes in v3:
time: 143 us
  blocking collectives  59.2 us (41%)
  Pallas kernels  45.5 us (32%)
  starting transfers between devices  18.9 us (13%)
  waiting for transfers between devices  12.4 us (9%)
  local copies, waits for them, and re-layouts  5.95 us (4%)
    all_to_all x5, blocking collectives, exchange(): lax.all_to_all(value, ('cell', 'view'), split_axis=0, concat_axis=0, tile...  59.2 us
    pallas_call x11, Pallas kernels, call(): pl.pallas_call(body, out_shape=[jax.ShapeDtypeStruct(shape, dtype) for sh...  45.5 us
    ppermute x6, starting transfers between devices, shifted(): lax.ppermute(value, 'view', [(i, (i + by) % view_count) for i in range(vi...  11.6 us
    all_to_all x1, starting transfers between devices, exchange(): lax.all_to_all(value, ('cell', 'view'), split_axis=0, concat_axis=0, tile...  7.32 us
    all_to_all x1, waiting for transfers between devices, exchange(): lax.all_to_all(value, ('cell', 'view'), split_axis=0, concat_axis=0, tile...  6.24 us
    ppermute x6, waiting for transfers between devices, shifted(): lax.ppermute(value, 'view', [(i, (i + by) % view_count) for i in range(vi...  6.2 us
    unnamed x22, local copies, waits for them, and re-layouts  5.95 us
  transfers between devices with their start and end apart: 7, of which 4 were waited for; matrix products, arithmetic and copies ran while one was open for 0% of the time, Pallas kernels for 1%

profile of v3, /device:TPU:0, one launch (start us, length us, event | category | flops | bytes accessed | tf_op | source)
XLA Modules:
  0.0 142.7 jit_solution(12081149034288289941)
XLA Ops:
  0.6 0.0 copy-start.3
  0.6 0.9 copy-done.3
  1.5 0.0 copy-start.9
  1.5 0.7 copy-done.9
  2.3 2.0 %project.1 = (f32[288,128]{1,0:T(8,128)}, s32[32,128]{1,0:T(8,128)S(1)}, bf16[256,4096]{1,0:T(8,128)(2,1)S(1)}) custom-call(f32[14,2048]{1,0:T(8,128)S(1)} %copy-done.3, s32[32,96]{1,0:T(8,128)S(1)} %bitcast.31), custom_call_target="tpu_custom_call" | custom-call | tf_op jit(solution)/shard_map/project/pallas_call | solution.py:722
  4.3 0.0 copy-start
  4.3 1.3 copy-done
  5.6 7.3 %all-to-all-start = ((f32[32,1,1152]{2,1,0:T(1,128)}), f32[32,1,1152]{2,1,0:T(1,128)S(1)}, u32[]{:S(2)}, u32[]{:S(2)}) async-start(f32[32,1,1152]{2,1,0:T(1,128)} %bitcast.1), calls=%async_computation | async-start | bytes 294912 | tf_op jit(solution)/shard_map/all_to_all | solution.py:760
  12.9 0.0 copy-start.6
  12.9 0.7 copy-done.6
  13.7 0.0 copy-start.10
  13.7 0.7 copy-done.10
  14.3 0.9 tables.1
  15.3 6.2 %all-to-all-done = f32[32,1,1152]{2,1,0:T(1,128)S(1)} async-done(((f32[32,1,1152]{2,1,0:T(1,128)}), f32[32,1,1152]{2,1,0:T(1,128)S(1)}, u32[]{:S(2)}, u32[]{:S(2)}) %all-to-all-start) | async-done | bytes 147488 | tf_op jit(solution)/shard_map/all_to_all | solution.py:760
  21.5 0.0 copy-start.5
  21.5 0.9 copy-done.5
  22.5 0.0 copy-start.7
  22.5 0.7 copy-done.7
  23.1 5.6 %forward.1 = (f32[384,128]{1,0:T(8,128)S(1)}, f32[24,256,128]{2,1,0:T(8,128)S(1)}, bf16[24,256,256]{2,1,0:T(8,128)(2,1)S(1)}, f32[24,256,128]{2,1,0:T(8,128)S(1)...) custom-call(f32[288,128]{1,0:T(8,128)S(1)} %bitcast.14, ...), custom_call_target="tpu_custom_call" | custom-call | tf_op jit(solution)/shard_map/forward/pallas_call | solution.py:722
  28.7 0.1 collective-permute-start.1
  28.8 3.8 %collective-permute-start = (f32[48,256]{1,0:T(8,128)S(1)}, f32[48,256]{1,0:T(8,128)S(1)}, u32[]{:S(2)}, u32[]{:S(2)}) collective-permute-start(f32[48,256]{1,0:T(8,128)S(1)} %get-tuple-element.46.d_ref), channel_id=1, source_target_pairs={{0,3},{1,0},{2,1},{3,2},{4,7},{5,4},{6,5},{7,6},{8,11},{9,8},{10,9... | collective-permute-start | bytes 147464 | tf_op jit(solution)/shard_map/ppermute | solution.py:764
  32.6 2.1 %collective-permute-done.1.past_ref = f32[48,256]{1,0:T(8,128)S(1)} collective-permute-done((f32[48,256]{1,0:T(8,128)S(1)}, f32[48,256]{1,0:T(8,128)S(1)}, u32[]{:S(2)}, u32[]{:S(2)}) %collective-permute-start.1) | collective-permute-done | bytes 49184 | tf_op jit(solution)/shard_map/ppermute | solution.py:764
  34.7 0.0 collective-permute-done.next_ref
  34.7 0.0 copy-start.1
  34.7 0.0 copy-start.2
  34.7 0.0 copy-start.4
  34.7 6.1 %pull.3 = f32[288,128]{1,0:T(8,128)S(1)} custom-call(f32[384,256]{1,0:T(8,128)S(1)} %get-tuple-element.45.j_ref, f32[48,256]{1,0:T(8,128)S(1)} %get-tuple-element.46.d_ref, f32[48,256]{1,0:T(8,128)S(1)} %collective-permute-done.next_ref, f32[48,256]{1,0:T(8,128)S(1)} %collective-permute-done.1.past_ref, s32[1,48]{1,0:T(1,128)S(1)} %bitcast.26, ...), custom_call_target="tpu_custom_call" | custom-call | tf_op jit(solution)/shard_map/pull/pallas_call | solution.py:722
  40.8 12.8 %all_to_all.30 = f32[32,1,1152]{2,1,0:T(1,128)S(1)} all-to-all(f32[32,1,1152]{2,1,0:T(1,128)S(1)} %bitcast.20), channel_id=1, replica_groups=mesh['cell'=8,'view'=4] {'cell','view'}, dimensions={0} | all-to-all | bytes 294912 | tf_op jit(solution)/shard_map/all_to_all | solution.py:760
  53.6 0.0 copy-done.1
  53.6 0.0 copy-done.2
  53.6 0.0 copy-done.4
  53.6 3.0 %gradient.1 = (f32[288,128]{1,0:T(8,128)S(1)}, f32[14,2048]{1,0:T(8,128)S(1)}, f32[14,2048]{1,0:T(8,128)S(1)}) custom-call(f32[288,128]{1,0:T(8,128)S(1)} %bitcast.16, f32[14,2048]{1,0:T(8,128)S(1)} %copy-done.4, f32[14,14,2048]{2,1,0:T(8,128)S(1)} %copy-done.2, s32[32,128]{1,0:T(8,128)S(1)} %get-tuple-element.55.sa_ref, bf16[256,4096]{1,0:T(8,128)(2,1)S(1)} %copy-done.1), custom_call_target="tpu_custom_call" | custom-call | tf_op jit(solution)/shard_map/gradient/pallas_call | solution.py:722
  56.6 10.3 %all_to_all.31 = f32[32,1,1152]{2,1,0:T(1,128)S(1)} all-to-all(f32[32,1,1152]{2,1,0:T(1,128)S(1)} %bitcast.24), channel_id=1, replica_groups=mesh['cell'=8,'view'=4] {'cell','view'}, dimensions={0} | all-to-all | bytes 294912 | tf_op jit(solution)/shard_map/all_to_all | solution.py:760
  66.9 5.1 %tangent.1 = (f32[384,256]{1,0:T(8,128)S(1)}, f32[48,256]{1,0:T(8,128)S(1)}, f32[48,256]{1,0:T(8,128)S(1)}, f32[16,128]{1,0:T(8,128)S(1)}) custom-call(f32[288,128]{1,0:T(8,128)S(1)} %bitcast.19, s32[24,128]{1,0:T(8,128)S(1)} %get-tuple-element.39.ta_ref, bf16[256,3072]{1,0:T(8,128)(2,1)S(1)} %get-tuple-element.40.to_ref, ...), custom_call_target="tpu_custom_call" | custom-call | tf_op jit(solution)/shard_map/tangent/pallas_call | solution.py:722
  72.1 0.1 collective-permute-start.3
  72.1 3.8 %collective-permute-start.2 = (f32[48,256]{1,0:T(8,128)S(1)}, f32[48,256]{1,0:T(8,128)S(1)}, u32[]{:S(2)}, u32[]{:S(2)}) collective-permute-start(f32[48,256]{1,0:T(8,128)S(1)} %get-tuple-element.59.d_ref), channel_id=1, source_target_pairs={{0,3},{1,0},{2,1},{3,2},{4,7},{5,4},{6,5},{7,6},{8,11},{9,8},{10,9... | collective-permute-start | bytes 147464 | tf_op jit(solution)/shard_map/ppermute | solution.py:764
  75.9 2.1 %collective-permute-done.3.past_ref = f32[48,256]{1,0:T(8,128)S(1)} collective-permute-done((f32[48,256]{1,0:T(8,128)S(1)}, f32[48,256]{1,0:T(8,128)S(1)}, u32[]{:S(2)}, u32[]{:S(2)}) %collective-permute-start.3) | collective-permute-done | bytes 49184 | tf_op jit(solution)/shard_map/ppermute | solution.py:764
  78.0 0.0 collective-permute-done.2.next_ref
  78.0 6.1 %pull.4 = f32[288,128]{1,0:T(8,128)S(1)} custom-call(f32[384,256]{1,0:T(8,128)S(1)} %get-tuple-element.58.j_ref.rest_0_, f32[48,256]{1,0:T(8,128)S(1)} %get-tuple-element.59.d_ref, f32[48,256]{1,0:T(8,128)S(1)} %collective-permute-done.2.next_ref, f32[48,256]{1,0:T(8,128)S(1)} %collective-permute-done.3.past_ref, s32[1,48]{1,0:T(1,128)S(1)} %bitcast.28, ...), custom_call_target="tpu_custom_call" | custom-call | tf_op jit(solution)/shard_map/pull/pallas_call | solution.py:722
  84.1 0.0 copy-start.8
  84.1 12.9 %all_to_all.32 = f32[32,1,1152]{2,1,0:T(1,128)S(1)} all-to-all(f32[32,1,1152]{2,1,0:T(1,128)S(1)} %bitcast.21), channel_id=1, replica_groups=mesh['cell'=8,'view'=4] {'cell','view'}, dimensions={0} | all-to-all | bytes 294912 | tf_op jit(solution)/shard_map/all_to_all | solution.py:760
  97.0 3.0 %step.1 = (f32[288,128]{1,0:T(8,128)S(1)}, f32[14,2048]{1,0:T(8,128)S(1)}, f32[14,2048]{1,0:T(8,128)S(1)}, f32[14,2048]{1,0:T(8,128)S(1)}) custom-call(f32[288,128]{1,0:T(8,128)S(1)} %bitcast.15, f32[14,2048]{1,0:T(8,128)S(1)} %copy-done.4, f32[14,14,2048]{2,1,0:T(8,128)S(1)} %copy-done.2, s32[32,128]{1,0:T(8,128)S(1)} %get-tuple-element.55.sa_ref, ...), custom_call_target="tpu_custom_call" | custom-call | tf_op jit(solution)/shard_map/step/pallas_call | solution.py:722
  100.0 10.3 %all_to_all.33 = f32[32,1,1152]{2,1,0:T(1,128)S(1)} all-to-all(f32[32,1,1152]{2,1,0:T(1,128)S(1)} %bitcast.23), channel_id=1, replica_groups=mesh['cell'=8,'view'=4] {'cell','view'}, dimensions={0} | all-to-all | bytes 294912 | tf_op jit(solution)/shard_map/all_to_all | solution.py:760
  110.3 0.0 copy-done.8
  110.3 5.1 %tangent_next.1 = (f32[384,256]{1,0:T(8,128)S(1)}, f32[48,256]{1,0:T(8,128)S(1)}, f32[48,256]{1,0:T(8,128)S(1)}, f32[16,128]{1,0:T(8,128)S(1)}) custom-call(f32[288,128]{1,0:T(8,128)S(1)} %bitcast.18, s32[24,128]{1,0:T(8,128)S(1)} %get-tuple-element.39.ta_ref, bf16[256,3072]{1,0:T(8,128)(2,1)S(1)} %get-tuple-element.40.to_ref, ...), custom_call_target="tpu_custom_call" | custom-call | tf_op jit(solution)/shard_map/tangent_next/pallas_call | solution.py:722
  115.5 0.1 collective-permute-start.5
  115.5 3.8 %collective-permute-start.4 = (f32[48,256]{1,0:T(8,128)S(1)}, f32[48,256]{1,0:T(8,128)S(1)}, u32[]{:S(2)}, u32[]{:S(2)}) collective-permute-start(f32[48,256]{1,0:T(8,128)S(1)} %get-tuple-element.66.d_ref), channel_id=1, source_target_pairs={{0,3},{1,0},{2,1},{3,2},{4,7},{5,4},{6,5},{7,6},{8,11},{9,8},{10,9... | collective-permute-start | bytes 147464 | tf_op jit(solution)/shard_map/ppermute | solution.py:764
  119.3 2.1 %collective-permute-done.5.past_ref = f32[48,256]{1,0:T(8,128)S(1)} collective-permute-done((f32[48,256]{1,0:T(8,128)S(1)}, f32[48,256]{1,0:T(8,128)S(1)}, u32[]{:S(2)}, u32[]{:S(2)}) %collective-permute-start.5) | collective-permute-done | bytes 49184 | tf_op jit(solution)/shard_map/ppermute | solution.py:764
  121.4 0.0 collective-permute-done.4.next_ref
  121.4 6.1 %pull.5 = (f32[288,128]{1,0:T(8,128)S(1)}, f32[14,2048]{1,0:T(8,128)S(1)}) custom-call(f32[384,256]{1,0:T(8,128)S(1)} %get-tuple-element.65.j_ref, f32[48,256]{1,0:T(8,128)S(1)} %get-tuple-element.66.d_ref, f32[48,256]{1,0:T(8,128)S(1)} %collective-permute-done.4.next_ref, f32[48,256]{1,0:T(8,128)S(1)} %collective-permute-done.5.past_ref, ...), custom_call_target="tpu_custom_call" | custom-call | tf_op jit(solution)/shard_map/pull/pallas_call | solution.py:722
  127.5 12.8 %all_to_all.34 = f32[32,1,1152]{2,1,0:T(1,128)S(1)} all-to-all(f32[32,1,1152]{2,1,0:T(1,128)S(1)} %bitcast.22), channel_id=1, replica_groups=mesh['cell'=8,'view'=4] {'cell','view'}, dimensions={0} | all-to-all | bytes 294912 | tf_op jit(solution)/shard_map/all_to_all | solution.py:760
  140.4 2.3 %finish.1 = (f32[14,2048]{1,0:T(8,128)}, f32[14,2048]{1,0:T(8,128)}) custom-call(f32[288,128]{1,0:T(8,128)S(1)} %bitcast.17, f32[14,2048]{1,0:T(8,128)S(1)} %copy-done.4, s32[32,128]{1,0:T(8,128)S(1)} %get-tuple-element.55.sa_ref, bf16[256,4096]{1,0:T(8,128)(2,1)S(1)} %copy-done.1, f32[14,2048]{1,0:T(8,128)S(1)} %get-tuple-element.71.res_in, ...), custom_call_target="tpu_custom_call" | custom-call | tf_op jit(solution)/shard_map/finish/pallas_call | solution.py:722
Async XLA Ops:
  0.6 0.9 copy-start.3
  1.5 0.7 copy-start.9
  4.3 1.3 copy-start
  5.6 15.9 %all-to-all-start = ((f32[32,1,1152]{2,1,0:T(1,128)}), f32[32,1,1152]{2,1,0:T(1,128)S(1)}, u32[]{:S(2)}, u32[]{:S(2)}) async-start(f32[32,1,1152]{2,1,0:T(1,128)} %bitcast.1), calls=%async_computation | async-start | bytes 294912 | tf_op jit(solution)/shard_map/all_to_all | solution.py:760
  12.9 0.7 copy-start.6
  13.7 0.7 copy-start.10
  21.5 0.9 copy-start.5
  22.5 0.7 copy-start.7
  28.7 5.9 %collective-permute-start.1 = (f32[48,256]{1,0:T(8,128)S(1)}, f32[48,256]{1,0:T(8,128)S(1)}, u32[]{:S(2)}, u32[]{:S(2)}) collective-permute-start(f32[48,256]{1,0:T(8,128)S(1)} %get-tuple-element.47), channel_id=1, source_target_pairs={{0,1},{1,2},{2,3},{3,0},{4,5},{5,6},{6,7},{7,4},{8,9},{9,10},{10,1... | collective-permute-start | bytes 147464 | tf_op jit(solution)/shard_map/ppermute | solution.py:764
  28.8 5.9 %collective-permute-start = (f32[48,256]{1,0:T(8,128)S(1)}, f32[48,256]{1,0:T(8,128)S(1)}, u32[]{:S(2)}, u32[]{:S(2)}) collective-permute-start(f32[48,256]{1,0:T(8,128)S(1)} %get-tuple-element.46.d_ref), channel_id=1, source_target_pairs={{0,3},{1,0},{2,1},{3,2},{4,7},{5,4},{6,5},{7,6},{8,11},{9,8},{10,9... | collective-permute-start | bytes 147464 | tf_op jit(solution)/shard_map/ppermute | solution.py:764
  34.7 18.9 %copy-start.1 = (bf16[256,4096]{1,0:T(8,128)(2,1)S(1)}, bf16[256,4096]{1,0:T(8,128)(2,1)}, u32[]{:S(2)}) copy-start(bf16[256,4096]{1,0:T(8,128)(2,1)} %copy-done) | copy-start | bytes 6291460
  34.7 18.9 %copy-start.2 = (f32[14,14,2048]{2,1,0:T(8,128)S(1)}, f32[14,14,2048]{2,1,0:T(8,128)}, u32[]{:S(2)}) copy-start(f32[14,14,2048]{2,1,0:T(8,128)} %pre_ref.3) | copy-start | bytes 4816900
  34.7 18.9 %copy-start.4 = (f32[14,2048]{1,0:T(8,128)S(1)}, f32[14,2048]{1,0:T(8,128)}, u32[]{:S(2)}) copy-start(f32[14,2048]{1,0:T(8,128)} %attr_ref.7) | copy-start | bytes 344068
  72.1 5.9 %collective-permute-start.3 = (f32[48,256]{1,0:T(8,128)S(1)}, f32[48,256]{1,0:T(8,128)S(1)}, u32[]{:S(2)}, u32[]{:S(2)}) collective-permute-start(f32[48,256]{1,0:T(8,128)S(1)} %get-tuple-element.60), channel_id=1, source_target_pairs={{0,1},{1,2},{2,3},{3,0},{4,5},{5,6},{6,7},{7,4},{8,9},{9,10},{10,1... | collective-permute-start | bytes 147464 | tf_op jit(solution)/shard_map/ppermute | solution.py:764
  72.1 5.9 %collective-permute-start.2 = (f32[48,256]{1,0:T(8,128)S(1)}, f32[48,256]{1,0:T(8,128)S(1)}, u32[]{:S(2)}, u32[]{:S(2)}) collective-permute-start(f32[48,256]{1,0:T(8,128)S(1)} %get-tuple-element.59.d_ref), channel_id=1, source_target_pairs={{0,3},{1,0},{2,1},{3,2},{4,7},{5,4},{6,5},{7,6},{8,11},{9,8},{10,9... | collective-permute-start | bytes 147464 | tf_op jit(solution)/shard_map/ppermute | solution.py:764
  84.1 26.2 %copy-start.8 = (s32[48]{0:T(128)S(1)}, s32[48]{0:T(128)}, u32[]{:S(2)}) copy-start(s32[48]{0:T(128)} %param.13) | copy-start | bytes 580
  115.5 5.9 %collective-permute-start.5 = (f32[48,256]{1,0:T(8,128)S(1)}, f32[48,256]{1,0:T(8,128)S(1)}, u32[]{:S(2)}, u32[]{:S(2)}) collective-permute-start(f32[48,256]{1,0:T(8,128)S(1)} %get-tuple-element.67), channel_id=1, source_target_pairs={{0,1},{1,2},{2,3},{3,0},{4,5},{5,6},{6,7},{7,4},{8,9},{9,10},{10,1... | collective-permute-start | bytes 147464 | tf_op jit(solution)/shard_map/ppermute | solution.py:764
  115.5 5.9 %collective-permute-start.4 = (f32[48,256]{1,0:T(8,128)S(1)}, f32[48,256]{1,0:T(8,128)S(1)}, u32[]{:S(2)}, u32[]{:S(2)}) collective-permute-start(f32[48,256]{1,0:T(8,128)S(1)} %get-tuple-element.66.d_ref), channel_id=1, source_target_pairs={{0,3},{1,0},{2,1},{3,2},{4,7},{5,4},{6,5},{7,6},{8,11},{9,8},{10,9... | collective-permute-start | bytes 147464 | tf_op jit(solution)/shard_map/ppermute | solution.py:764

commit v4 on v3

--- a/solution.py
+++ b/solution.py
@@ -306,11 +306,11 @@
 
 
 def first_owner(
-    meta, attr_ref, send_ref, out_ref, sa_ref, so_ref, chunk_ref, source_ref, lhs_ref, sent_ref, ids_ref, sb_ref
+    meta, attr_ref, send_ref, out_ref, sa_ref, sb_ref, chunk_ref, source_ref, lhs_ref, sent_ref, so_ref, ids_ref
 ):
     chunks, devices, slots = meta
     ids_ref[...] = jnp.full(ids_ref.shape, -1, jnp.int32)
-    ids_ref[:, :slots] = send_ref[...]
+    ids_ref[:, :slots] = send_ref[0]
     ids = ids_ref[...]
     put_halves(ids >> 7, ids & (LANES - 1), chunks, ids >= 0, sa_ref, sb_ref)
     put_onehot(sb_ref, devices, so_ref)
@@ -422,10 +422,16 @@
 
 
 def tables(
-    meta, list_ref, anchor_ref, ta_ref, ax_ref, ay_ref, onehot_ref, basis_ref, moment_ref, early_ref, late_ref,
+    meta, list_ref, anchor_ref, pair_ref, sb_ref,
+    ta_ref, ax_ref, ay_ref, onehot_ref, so_ref, to_past_ref, of_next_ref, basis_ref, moment_ref, early_ref, late_ref,
     wide_ref, tb_ref,
 ):
     blocks, devices, slots = meta
+    put_onehot(sb_ref, devices, so_ref)
+    tiles = 2 * blocks
+    partner = jnp.where(iota((tiles, tiles), 0) == pair_ref[...], 1.0, 0.0)
+    to_past_ref[...] = partner.astype(BF16)
+    of_next_ref[...] = partner.T.astype(BF16)
     wide_ref[:, :KSLOTS] = list_ref[...]
     even, odd = (wide_ref[pl.ds(side, blocks, stride=2), :] for side in range(2))
     lane = iota((blocks, LANES), 1)
@@ -475,9 +481,7 @@
 
 
 def send_order(pr_ref, depth, ds_ref):
-    tiles = depth.shape[0]
-    onehot = jnp.where(iota((tiles, tiles), 0) == pr_ref[...], 1.0, 0.0).astype(BF16)
-    ds_ref[...] = sum(dot(onehot, piece) for piece in split(depth, 3))
+    ds_ref[...] = sum(dot(pr_ref[...], piece) for piece in split(depth, 3))
 
 
 def receive_rows(meta, recv_ref, ta_ref, to_ref, source_ref, lhs_ref, out_ref, parts):
@@ -554,7 +558,7 @@
             d_ref[pl.ds(2 * (first + i) + 1, 1), :] = image[12:13]
         return carry
 
-    lax.fori_loop(0, blocks // GROUP, body, 0)
+    lax.fori_loop(0, blocks // GROUP, body, 0, unroll=min(blocks // GROUP, 4))
     send_order(pr_ref, d_ref[...], ds_ref)
 
 
@@ -613,7 +617,7 @@
             d_ref[pl.ds(2 * (first + i) + 1, 1), :] = image[12:13]
         return carry
 
-    lax.fori_loop(0, blocks // GROUP, body, 0)
+    lax.fori_loop(0, blocks // GROUP, body, 0, unroll=min(blocks // GROUP, 4))
     send_order(pr_ref, d_ref[...], ds_ref)
 
 
@@ -630,8 +634,7 @@
     blocks, devices, slots = meta
     tiles = 2 * blocks
     depth = d_ref[...]
-    onehot = jnp.where(iota((tiles, tiles), 0) == pr_ref[...], 1.0, 0.0).T.astype(BF16)
-    partner = sum(dot(onehot, piece) for piece in split(next_ref[...], 3))
+    partner = sum(dot(pr_ref[...], piece) for piece in split(next_ref[...], 3))
     prior = PRIOR_WEIGHT * (depth - partner)
     depth_bar = PRIOR_WEIGHT * prior - PRIOR_WEIGHT * (PRIOR_WEIGHT * (past_ref[...] - depth))
     image = j_ref[...]
@@ -688,7 +691,7 @@
             term_ref[pl.ds(start, 8), :] = column(moments, i)[0:8]
         return carry
 
-    lax.fori_loop(0, blocks // TOGETHER, body, 0, unroll=3)
+    lax.fori_loop(0, blocks // TOGETHER, body, 0, unroll=whole(blocks))
     theta, bars = reader(theta_ref, blocks), reader(term_ref, blocks)
     dx, dy = local_place(theta, ax_ref, ay_ref)
     qxx, qxy, qyy = theta(2), theta(3), theta(4)
@@ -782,26 +785,32 @@
                 ((2, devices // 2 * ROWS, LANES), F32),
             ],
             "pull",
-            image, here, shifted(here, -1), shifted(ordered, 1), pair_row, ta, onehot, moments, late, ax, ay,
+            image, here, shifted(here, -1), shifted(ordered, 1), of_next, ta, onehot, moments, late, ax, ay,
             theta, weight, pieces, rho, left, *extra,
         )
 
     indices = ((devices, LANES), jnp.int32)
-    sent, sa, sends = call(
+    indices = ((devices, LANES), jnp.int32)
+    wide = ((WIDE, devices * LANES), BF16)
+    sent, sa, sb = call(
         functools.partial(first_owner, owner_meta),
-        [payload, indices, ((WIDE, devices * LANES), BF16)],
-        owner_scratch(3) + [indices, indices],
+        [payload, indices, indices],
+        owner_scratch(3) + [wide, indices],
         "project",
-        attributes, send_index[0],
+        attributes, send_index,
     )
     listing = ((blocks, LANES), jnp.int32)
-    ta, ax, ay, onehot, basis, moments, early, late = call(
+    pairing = ((tiles, tiles), BF16)
+    ta, ax, ay, onehot, sends, to_past, of_next, basis, moments, early, late = call(
         functools.partial(tables, tile_meta),
         [
             listing,
             ((blocks, LANES), F32),
             ((blocks, LANES), F32),
             ((WIDE, blocks * LANES), BF16),
+            wide,
+            pairing,
+            pairing,
             ((PIXELS, 32), BF16),
             ((ROWS, 2 * PIXELS), BF16),
             ((3 * LANES, LANES), BF16),
@@ -809,14 +818,14 @@
         ],
         [((tiles, LANES), jnp.int32), listing],
         "tables",
-        tile_list, tile_anchor,
+        tile_list, tile_anchor, pair_row, sb,
     )
     theta, weight, pieces, rho, left, image, here, ordered = call(
         functools.partial(tile_forward, tile_meta),
         [listed, field, ((blocks, PIXELS, WIDE), BF16), field, ((blocks * 32, WIDE), BF16), images, maps, maps],
         tile_scratch(3),
         "forward",
-        exchange(sent), ta, onehot, basis, early, ax, ay, target, pair_row,
+        exchange(sent), ta, onehot, basis, early, ax, ay, target, to_past,
     )
     (sent,) = pull(0, image, (here, ordered), (), [])
     sent, residual, direction = call(
@@ -831,7 +840,7 @@
         [images, maps, maps, scalars],
         tile_scratch(2) + [listed],
         "tangent",
-        exchange(sent), ta, onehot, basis, early, ax, ay, pair_row, theta, weight, pieces, rho, left,
+        exchange(sent), ta, onehot, basis, early, ax, ay, to_past, theta, weight, pieces, rho, left,
     )
     (sent,) = pull(1, image, (here, ordered), (direction,), [])
     sent, residual, update, scaled = call(
@@ -846,7 +855,7 @@
         [images, maps, maps, scalars],
         tile_scratch(2) + [listed],
         "tangent_next",
-        exchange(sent), ta, onehot, basis, early, ax, ay, pair_row, theta, weight, pieces, rho, left, image, first_sums,
+        exchange(sent), ta, onehot, basis, early, ax, ay, to_past, theta, weight, pieces, rho, left, image, first_sums,
     )
     sent, direction = pull(2, image, (here, ordered), (scaled, direction, sums), [owned])
     update, residual = call(

time: 143 us -> 137 us (0.958)
  Pallas kernels: 45.5 us -> 42.6 us
  waiting for transfers between devices: 12.4 us -> 9.51 us
    pallas_call x11, Pallas kernels: 45.5 us -> 42.6 us  [call(): pl.pallas_call(body, out_shape=[jax.ShapeDtypeStruct(shape, dtype) for sh...]
    all_to_all x1, waiting for transfers between devices: 6.24 us -> 3.31 us  [exchange(): lax.all_to_all(value, ('cell', 'view'), split_axis=0, concat_axis=0, tile...]
    unnamed x22 -> x20, local copies, waits for them, and re-layouts: 5.95 us -> 5.95 us
where the time goes in v4:
time: 137 us
  blocking collectives  59.2 us (43%)
  Pallas kernels  42.6 us (31%)
  starting transfers between devices  18.9 us (14%)
  waiting for transfers between devices  9.51 us (7%)
  local copies, waits for them, and re-layouts  5.95 us (4%)
    all_to_all x5, blocking collectives, exchange(): lax.all_to_all(value, ('cell', 'view'), split_axis=0, concat_axis=0, tile...  59.2 us
    pallas_call x11, Pallas kernels, call(): pl.pallas_call(body, out_shape=[jax.ShapeDtypeStruct(shape, dtype) for sh...  42.6 us
    ppermute x6, starting transfers between devices, shifted(): lax.ppermute(value, 'view', [(i, (i + by) % view_count) for i in range(vi...  11.5 us
    all_to_all x1, starting transfers between devices, exchange(): lax.all_to_all(value, ('cell', 'view'), split_axis=0, concat_axis=0, tile...  7.33 us
    ppermute x6, waiting for transfers between devices, shifted(): lax.ppermute(value, 'view', [(i, (i + by) % view_count) for i in range(vi...  6.2 us
    unnamed x20, local copies, waits for them, and re-layouts  5.95 us
    all_to_all x1, waiting for transfers between devices, exchange(): lax.all_to_all(value, ('cell', 'view'), split_axis=0, concat_axis=0, tile...  3.31 us
  transfers between devices with their start and end apart: 7, of which 4 were waited for; matrix products, arithmetic and copies ran while one was open for 0% of the time, Pallas kernels for 1%

profile of v4, /device:TPU:0, one launch (start us, length us, event | category | flops | bytes accessed | tf_op | source)
XLA Modules:
  0.0 136.8 jit_solution(1497162100776899631)
XLA Ops:
  0.6 0.0 copy-start.3
  0.6 0.9 copy-done.3
  1.5 0.0 copy-start.7
  1.5 0.7 copy-done.7
  2.3 2.0 %project.1 = (f32[288,128]{1,0:T(8,128)}, s32[32,128]{1,0:T(8,128)S(1)}, s32[32,128]{1,0:T(8,128)S(1)}) custom-call(f32[14,2048]{1,0:T(8,128)S(1)} %copy-done.3, s32[1,32,96]{2,1,0:T(8,128)S(1)} %copy-done.7), custom_call_target="tpu_custom_call" | custom-call | tf_op jit(solution)/shard_map/project/pallas_call | solution.py:725
  4.3 7.3 %all-to-all-start = ((f32[32,1,1152]{2,1,0:T(1,128)}), f32[32,1,1152]{2,1,0:T(1,128)S(1)}, u32[]{:S(2)}, u32[]{:S(2)}) async-start(f32[32,1,1152]{2,1,0:T(1,128)} %bitcast), calls=%async_computation | async-start | bytes 294912 | tf_op jit(solution)/shard_map/all_to_all | solution.py:763
  11.6 0.0 copy-start.6
  11.6 0.7 copy-done.6
  12.3 0.0 copy-start.8
  12.3 0.7 copy-done.8
  13.0 0.0 copy-start.9
  13.0 0.7 copy-done.9
  13.7 1.9 %tables.1 = (s32[24,128]{1,0:T(8,128)S(1)}, f32[24,128]{1,0:T(8,128)S(1)}, f32[24,128]{1,0:T(8,128)S(1)}, bf16[256,3072]{1,0:T(8,128)(2,1)S(1)}, bf16[256,4096]{...) custom-call(s32[48,64]{1,0:T(8,128)S(1)} %copy-done.6, ...), custom_call_target="tpu_custom_call" | custom-call | tf_op jit(solution)/shard_map/tables/pallas_call | solution.py:725
  15.6 0.0 copy-start
  15.6 1.3 copy-done
  16.9 3.3 %all-to-all-done = f32[32,1,1152]{2,1,0:T(1,128)S(1)} async-done(((f32[32,1,1152]{2,1,0:T(1,128)}), f32[32,1,1152]{2,1,0:T(1,128)S(1)}, u32[]{:S(2)}, u32[]{:S(2)}) %all-to-all-start) | async-done | bytes 147488 | tf_op jit(solution)/shard_map/all_to_all | solution.py:763
  20.2 0.0 copy-start.5
  20.2 0.9 copy-done.5
  21.1 4.9 %forward.1 = (f32[384,128]{1,0:T(8,128)S(1)}, f32[24,256,128]{2,1,0:T(8,128)S(1)}, bf16[24,256,256]{2,1,0:T(8,128)(2,1)S(1)}, f32[24,256,128]{2,1,0:T(8,128)S(1)...) custom-call(f32[288,128]{1,0:T(8,128)S(1)} %bitcast.13, ...), custom_call_target="tpu_custom_call" | custom-call | tf_op jit(solution)/shard_map/forward/pallas_call | solution.py:725
  26.0 0.0 collective-permute-start.1
  26.1 3.8 %collective-permute-start = (f32[48,256]{1,0:T(8,128)S(1)}, f32[48,256]{1,0:T(8,128)S(1)}, u32[]{:S(2)}, u32[]{:S(2)}) collective-permute-start(f32[48,256]{1,0:T(8,128)S(1)} %get-tuple-element.51.d_ref), channel_id=1, source_target_pairs={{0,3},{1,0},{2,1},{3,2},{4,7},{5,4},{6,5},{7,6},{8,11},{9,8},{10,9... | collective-permute-start | bytes 147464 | tf_op jit(solution)/shard_map/ppermute | solution.py:767
  29.9 2.1 %collective-permute-done.1.past_ref = f32[48,256]{1,0:T(8,128)S(1)} collective-permute-done((f32[48,256]{1,0:T(8,128)S(1)}, f32[48,256]{1,0:T(8,128)S(1)}, u32[]{:S(2)}, u32[]{:S(2)}) %collective-permute-start.1) | collective-permute-done | bytes 49184 | tf_op jit(solution)/shard_map/ppermute | solution.py:767
  31.9 0.0 collective-permute-done.next_ref
  31.9 0.0 copy-start.1
  31.9 0.0 copy-start.2
  31.9 0.0 copy-start.4
  32.0 5.6 %pull.3 = f32[288,128]{1,0:T(8,128)S(1)} custom-call(f32[384,256]{1,0:T(8,128)S(1)} %get-tuple-element.50.j_ref, f32[48,256]{1,0:T(8,128)S(1)} %get-tuple-element.51.d_ref, f32[48,256]{1,0:T(8,128)S(1)} %collective-permute-done.next_ref, f32[48,256]{1,0:T(8,128)S(1)} %collective-permute-done.1.past_ref, bf16[48,48]{1,0:T(8,128)(2,1)S(1)} %get-tuple-element.53.pr_ref, ...), custom_call_target="tpu_custom_call" | custom-call | tf_op jit(solution)/shard_map/pull/pallas_call | solution.py:725
  37.6 12.9 %all_to_all.30 = f32[32,1,1152]{2,1,0:T(1,128)S(1)} all-to-all(f32[32,1,1152]{2,1,0:T(1,128)S(1)} %bitcast.19), channel_id=1, replica_groups=mesh['cell'=8,'view'=4] {'cell','view'}, dimensions={0} | all-to-all | bytes 294912 | tf_op jit(solution)/shard_map/all_to_all | solution.py:763
  50.5 0.0 copy-done.1
  50.5 0.0 copy-done.2
  50.5 0.0 copy-done.4
  50.5 3.0 %gradient.1 = (f32[288,128]{1,0:T(8,128)S(1)}, f32[14,2048]{1,0:T(8,128)S(1)}, f32[14,2048]{1,0:T(8,128)S(1)}) custom-call(f32[288,128]{1,0:T(8,128)S(1)} %bitcast.15, f32[14,2048]{1,0:T(8,128)S(1)} %copy-done.4, f32[14,14,2048]{2,1,0:T(8,128)S(1)} %copy-done.2, s32[32,128]{1,0:T(8,128)S(1)} %get-tuple-element.61.sa_ref, bf16[256,4096]{1,0:T(8,128)(2,1)S(1)} %copy-done.1), custom_call_target="tpu_custom_call" | custom-call | tf_op jit(solution)/shard_map/gradient/pallas_call | solution.py:725
  53.5 10.3 %all_to_all.31 = f32[32,1,1152]{2,1,0:T(1,128)S(1)} all-to-all(f32[32,1,1152]{2,1,0:T(1,128)S(1)} %bitcast.23), channel_id=1, replica_groups=mesh['cell'=8,'view'=4] {'cell','view'}, dimensions={0} | all-to-all | bytes 294912 | tf_op jit(solution)/shard_map/all_to_all | solution.py:763
  63.8 4.2 %tangent.1 = (f32[384,256]{1,0:T(8,128)S(1)}, f32[48,256]{1,0:T(8,128)S(1)}, f32[48,256]{1,0:T(8,128)S(1)}, f32[16,128]{1,0:T(8,128)S(1)}) custom-call(f32[288,128]{1,0:T(8,128)S(1)} %bitcast.18, s32[24,128]{1,0:T(8,128)S(1)} %get-tuple-element.43.ta_ref, bf16[256,3072]{1,0:T(8,128)(2,1)S(1)} %get-tuple-element.44.to_ref, ...), custom_call_target="tpu_custom_call" | custom-call | tf_op jit(solution)/shard_map/tangent/pallas_call | solution.py:725
  68.0 0.0 collective-permute-start.3
  68.0 3.8 %collective-permute-start.2 = (f32[48,256]{1,0:T(8,128)S(1)}, f32[48,256]{1,0:T(8,128)S(1)}, u32[]{:S(2)}, u32[]{:S(2)}) collective-permute-start(f32[48,256]{1,0:T(8,128)S(1)} %get-tuple-element.65.d_ref), channel_id=1, source_target_pairs={{0,3},{1,0},{2,1},{3,2},{4,7},{5,4},{6,5},{7,6},{8,11},{9,8},{10,9... | collective-permute-start | bytes 147464 | tf_op jit(solution)/shard_map/ppermute | solution.py:767
  71.8 2.1 %collective-permute-done.3.past_ref = f32[48,256]{1,0:T(8,128)S(1)} collective-permute-done((f32[48,256]{1,0:T(8,128)S(1)}, f32[48,256]{1,0:T(8,128)S(1)}, u32[]{:S(2)}, u32[]{:S(2)}) %collective-permute-start.3) | collective-permute-done | bytes 49184 | tf_op jit(solution)/shard_map/ppermute | solution.py:767
  73.9 0.0 collective-permute-done.2.next_ref
  73.9 5.7 %pull.4 = f32[288,128]{1,0:T(8,128)S(1)} custom-call(f32[384,256]{1,0:T(8,128)S(1)} %get-tuple-element.64.j_ref.rest_0_, f32[48,256]{1,0:T(8,128)S(1)} %get-tuple-element.65.d_ref, f32[48,256]{1,0:T(8,128)S(1)} %collective-permute-done.2.next_ref, f32[48,256]{1,0:T(8,128)S(1)} %collective-permute-done.3.past_ref, ...), custom_call_target="tpu_custom_call" | custom-call | tf_op jit(solution)/shard_map/pull/pallas_call | solution.py:725
  79.6 12.9 %all_to_all.32 = f32[32,1,1152]{2,1,0:T(1,128)S(1)} all-to-all(f32[32,1,1152]{2,1,0:T(1,128)S(1)} %bitcast.20), channel_id=1, replica_groups=mesh['cell'=8,'view'=4] {'cell','view'}, dimensions={0} | all-to-all | bytes 294912 | tf_op jit(solution)/shard_map/all_to_all | solution.py:763
  92.4 3.0 %step.1 = (f32[288,128]{1,0:T(8,128)S(1)}, f32[14,2048]{1,0:T(8,128)S(1)}, f32[14,2048]{1,0:T(8,128)S(1)}, f32[14,2048]{1,0:T(8,128)S(1)}) custom-call(f32[288,128]{1,0:T(8,128)S(1)} %bitcast.14, f32[14,2048]{1,0:T(8,128)S(1)} %copy-done.4, f32[14,14,2048]{2,1,0:T(8,128)S(1)} %copy-done.2, s32[32,128]{1,0:T(8,128)S(1)} %get-tuple-element.61.sa_ref, ...), custom_call_target="tpu_custom_call" | custom-call | tf_op jit(solution)/shard_map/step/pallas_call | solution.py:725
  95.4 10.3 %all_to_all.33 = f32[32,1,1152]{2,1,0:T(1,128)S(1)} all-to-all(f32[32,1,1152]{2,1,0:T(1,128)S(1)} %bitcast.22), channel_id=1, replica_groups=mesh['cell'=8,'view'=4] {'cell','view'}, dimensions={0} | all-to-all | bytes 294912 | tf_op jit(solution)/shard_map/all_to_all | solution.py:763
  105.8 4.2 %tangent_next.1 = (f32[384,256]{1,0:T(8,128)S(1)}, f32[48,256]{1,0:T(8,128)S(1)}, f32[48,256]{1,0:T(8,128)S(1)}, f32[16,128]{1,0:T(8,128)S(1)}) custom-call(f32[288,128]{1,0:T(8,128)S(1)} %bitcast.17, s32[24,128]{1,0:T(8,128)S(1)} %get-tuple-element.43.ta_ref, bf16[256,3072]{1,0:T(8,128)(2,1)S(1)} %get-tuple-element.44.to_ref, ...), custom_call_target="tpu_custom_call" | custom-call | tf_op jit(solution)/shard_map/tangent_next/pallas_call | solution.py:725
  110.0 0.0 collective-permute-start.5
  110.0 3.8 %collective-permute-start.4 = (f32[48,256]{1,0:T(8,128)S(1)}, f32[48,256]{1,0:T(8,128)S(1)}, u32[]{:S(2)}, u32[]{:S(2)}) collective-permute-start(f32[48,256]{1,0:T(8,128)S(1)} %get-tuple-element.72.d_ref), channel_id=1, source_target_pairs={{0,3},{1,0},{2,1},{3,2},{4,7},{5,4},{6,5},{7,6},{8,11},{9,8},{10,9... | collective-permute-start | bytes 147464 | tf_op jit(solution)/shard_map/ppermute | solution.py:767
  113.9 2.1 %collective-permute-done.5.past_ref = f32[48,256]{1,0:T(8,128)S(1)} collective-permute-done((f32[48,256]{1,0:T(8,128)S(1)}, f32[48,256]{1,0:T(8,128)S(1)}, u32[]{:S(2)}, u32[]{:S(2)}) %collective-permute-start.5) | collective-permute-done | bytes 49184 | tf_op jit(solution)/shard_map/ppermute | solution.py:767
  115.9 0.0 collective-permute-done.4.next_ref
  115.9 5.7 %pull.5 = (f32[288,128]{1,0:T(8,128)S(1)}, f32[14,2048]{1,0:T(8,128)S(1)}) custom-call(f32[384,256]{1,0:T(8,128)S(1)} %get-tuple-element.71.j_ref, f32[48,256]{1,0:T(8,128)S(1)} %get-tuple-element.72.d_ref, f32[48,256]{1,0:T(8,128)S(1)} %collective-permute-done.4.next_ref, f32[48,256]{1,0:T(8,128)S(1)} %collective-permute-done.5.past_ref, ...), custom_call_target="tpu_custom_call" | custom-call | tf_op jit(solution)/shard_map/pull/pallas_call | solution.py:725
  121.6 12.8 %all_to_all.34 = f32[32,1,1152]{2,1,0:T(1,128)S(1)} all-to-all(f32[32,1,1152]{2,1,0:T(1,128)S(1)} %bitcast.21), channel_id=1, replica_groups=mesh['cell'=8,'view'=4] {'cell','view'}, dimensions={0} | all-to-all | bytes 294912 | tf_op jit(solution)/shard_map/all_to_all | solution.py:763
  134.4 2.3 %finish.1 = (f32[14,2048]{1,0:T(8,128)}, f32[14,2048]{1,0:T(8,128)}) custom-call(f32[288,128]{1,0:T(8,128)S(1)} %bitcast.16, f32[14,2048]{1,0:T(8,128)S(1)} %copy-done.4, s32[32,128]{1,0:T(8,128)S(1)} %get-tuple-element.61.sa_ref, bf16[256,4096]{1,0:T(8,128)(2,1)S(1)} %copy-done.1, f32[14,2048]{1,0:T(8,128)S(1)} %get-tuple-element.77.res_in, ...), custom_call_target="tpu_custom_call" | custom-call | tf_op jit(solution)/shard_map/finish/pallas_call | solution.py:725
Async XLA Ops:
  0.6 0.9 copy-start.3
  1.5 0.7 copy-start.7
  4.3 15.9 %all-to-all-start = ((f32[32,1,1152]{2,1,0:T(1,128)}), f32[32,1,1152]{2,1,0:T(1,128)S(1)}, u32[]{:S(2)}, u32[]{:S(2)}) async-start(f32[32,1,1152]{2,1,0:T(1,128)} %bitcast), calls=%async_computation | async-start | bytes 294912 | tf_op jit(solution)/shard_map/all_to_all | solution.py:763
  11.6 0.7 copy-start.6
  12.3 0.7 copy-start.8
  13.0 0.7 copy-start.9
  15.6 1.3 copy-start
  20.2 0.9 copy-start.5
  26.0 5.9 %collective-permute-start.1 = (f32[48,256]{1,0:T(8,128)S(1)}, f32[48,256]{1,0:T(8,128)S(1)}, u32[]{:S(2)}, u32[]{:S(2)}) collective-permute-start(f32[48,256]{1,0:T(8,128)S(1)} %get-tuple-element.52), channel_id=1, source_target_pairs={{0,1},{1,2},{2,3},{3,0},{4,5},{5,6},{6,7},{7,4},{8,9},{9,10},{10,1... | collective-permute-start | bytes 147464 | tf_op jit(solution)/shard_map/ppermute | solution.py:767
  26.1 5.9 %collective-permute-start = (f32[48,256]{1,0:T(8,128)S(1)}, f32[48,256]{1,0:T(8,128)S(1)}, u32[]{:S(2)}, u32[]{:S(2)}) collective-permute-start(f32[48,256]{1,0:T(8,128)S(1)} %get-tuple-element.51.d_ref), channel_id=1, source_target_pairs={{0,3},{1,0},{2,1},{3,2},{4,7},{5,4},{6,5},{7,6},{8,11},{9,8},{10,9... | collective-permute-start | bytes 147464 | tf_op jit(solution)/shard_map/ppermute | solution.py:767
  31.9 18.5 %copy-start.1 = (bf16[256,4096]{1,0:T(8,128)(2,1)S(1)}, bf16[256,4096]{1,0:T(8,128)(2,1)}, u32[]{:S(2)}) copy-start(bf16[256,4096]{1,0:T(8,128)(2,1)} %copy-done) | copy-start | bytes 6291460
  31.9 18.5 %copy-start.2 = (f32[14,14,2048]{2,1,0:T(8,128)S(1)}, f32[14,14,2048]{2,1,0:T(8,128)}, u32[]{:S(2)}) copy-start(f32[14,14,2048]{2,1,0:T(8,128)} %pre_ref.3) | copy-start | bytes 4816900
  31.9 18.5 %copy-start.4 = (f32[14,2048]{1,0:T(8,128)S(1)}, f32[14,2048]{1,0:T(8,128)}, u32[]{:S(2)}) copy-start(f32[14,2048]{1,0:T(8,128)} %attr_ref.7) | copy-start | bytes 344068
  68.0 5.9 %collective-permute-start.3 = (f32[48,256]{1,0:T(8,128)S(1)}, f32[48,256]{1,0:T(8,128)S(1)}, u32[]{:S(2)}, u32[]{:S(2)}) collective-permute-start(f32[48,256]{1,0:T(8,128)S(1)} %get-tuple-element.66), channel_id=1, source_target_pairs={{0,1},{1,2},{2,3},{3,0},{4,5},{5,6},{6,7},{7,4},{8,9},{9,10},{10,1... | collective-permute-start | bytes 147464 | tf_op jit(solution)/shard_map/ppermute | solution.py:767
  68.0 5.9 %collective-permute-start.2 = (f32[48,256]{1,0:T(8,128)S(1)}, f32[48,256]{1,0:T(8,128)S(1)}, u32[]{:S(2)}, u32[]{:S(2)}) collective-permute-start(f32[48,256]{1,0:T(8,128)S(1)} %get-tuple-element.65.d_ref), channel_id=1, source_target_pairs={{0,3},{1,0},{2,1},{3,2},{4,7},{5,4},{6,5},{7,6},{8,11},{9,8},{10,9... | collective-permute-start | bytes 147464 | tf_op jit(solution)/shard_map/ppermute | solution.py:767
  110.0 5.9 %collective-permute-start.5 = (f32[48,256]{1,0:T(8,128)S(1)}, f32[48,256]{1,0:T(8,128)S(1)}, u32[]{:S(2)}, u32[]{:S(2)}) collective-permute-start(f32[48,256]{1,0:T(8,128)S(1)} %get-tuple-element.73), channel_id=1, source_target_pairs={{0,1},{1,2},{2,3},{3,0},{4,5},{5,6},{6,7},{7,4},{8,9},{9,10},{10,1... | collective-permute-start | bytes 147464 | tf_op jit(solution)/shard_map/ppermute | solution.py:767
  110.0 5.9 %collective-permute-start.4 = (f32[48,256]{1,0:T(8,128)S(1)}, f32[48,256]{1,0:T(8,128)S(1)}, u32[]{:S(2)}, u32[]{:S(2)}) collective-permute-start(f32[48,256]{1,0:T(8,128)S(1)} %get-tuple-element.72.d_ref), channel_id=1, source_target_pairs={{0,3},{1,0},{2,1},{3,2},{4,7},{5,4},{6,5},{7,6},{8,11},{9,8},{10,9... | collective-permute-start | bytes 147464 | tf_op jit(solution)/shard_map/ppermute | solution.py:767
